TPU v7x, 32 devices: a whole 2x2x4 slice. The times are simulated.
32 devices in a mesh: groups: 2 (over x), ctx: 16 (over z, y, core).
Axes of the slice: x: 2, y: 2, z: 4, core: 2. Of those that a mesh axis runs over, the one named last changes fastest.
Arguments:
- features: bfloat16 [4096, 3, 8192], P(('groups', 'ctx')), parts along dimension 0, may hold values from -6 to 6
- short_filter: bfloat16 [3, 3, 8192], P(None, None, 'ctx'), may hold values from -3.5 to 3.5
- residues: float32 [8192, 16], P('ctx'), may hold values from -1.5 to 1.5
- rates: float32 [8192, 16], P('ctx'), may hold values from 0.02 to 64
Outputs:
- gated: bfloat16 [4096, 8192], P(('groups', 'ctx')), parts along dimension 0
There are 2 independent parts, one for each index of `groups`. A program takes and returns all parts, laid end to end along the dimension named above; an argument that names none is the same for every part. Nothing has to cross between parts.
All inputs are finite; a program needn't handle non-finite values.
Results may differ from a plain program's by a relative error of at most 0.001.
Values may be sent and summed in bfloat16 or wider, within the bound.
No kernel may reach another device: no remote copies, remote signals or barrier semaphores. Data moves between devices by JAX's collectives and lax.ppermute only.
A program may use at most 256 MiB of HBM per device.

v0:
```python
import jax
import jax.numpy as jnp
from jax import lax
from jax.sharding import PartitionSpec as P

BLOCK = 16


def from_behind(value, axis, by):
    size = lax.axis_size(axis)
    pairs = [(i, i + by) for i in range(size) if 0 <= i + by < size]
    return lax.ppermute(value, axis, pairs)


def carried_in(value, axis, combine, identity):
    size, mine = (lax.axis_size(axis), lax.axis_index(axis))
    everything = jax.tree.map(lambda part: lax.all_gather(part, axis), value)
    start = jax.tree.map(
        lambda part, zero: jnp.broadcast_to(jnp.asarray(zero, part.dtype), part.shape),
        value,
        identity,
    )

    def step(k, before):
        reached = k < mine
        new = combine(before, jax.tree.map(lambda part: part[k], everything))
        return jax.tree.map(lambda a, b: jnp.where(reached, a, b), new, before)

    return lax.fori_loop(0, size, step, start)


def featurize(tail, feats, taps):
    full = jnp.concatenate([tail, feats], 0).astype(jnp.float32)
    rows = feats.shape[0]
    return taps[0] * full[2:] + taps[1] * full[1 : rows + 1] + taps[2] * full[:rows]


def prepare(rates_t, coef_t, scale):
    lags = jnp.arange(BLOCK, dtype=jnp.float32)[:, None, None]
    powers = jnp.exp(-rates_t[None] * lags * scale)
    kernel = jnp.sum(coef_t[None] * powers, axis=1)
    reach = coef_t[None] * powers * jnp.exp(-rates_t * scale)[None]
    block_decay = jnp.exp(-rates_t * (BLOCK * scale))
    return (powers, kernel, reach, block_decay)


def modal_local(drive, powers, kernel, block_decay):
    rows, width = drive.shape
    count = rows // BLOCK
    blocks = drive.reshape(count, BLOCK, width)
    intra = blocks * kernel[0]
    for lag in range(1, BLOCK):
        moved = jnp.pad(blocks[:, : BLOCK - lag], ((0, 0), (lag, 0), (0, 0)))
        intra = intra + kernel[lag] * moved
    ends = blocks[:, 0][:, None, :] * powers[BLOCK - 1][None]
    for place in range(1, BLOCK):
        ends = ends + blocks[:, place][:, None, :] * powers[BLOCK - 1 - place][None]

    def advance(carry, end):
        return (block_decay * carry + end, carry)

    local_end, starts = lax.scan(advance, jnp.zeros_like(block_decay), ends)
    return (intra, starts, local_end)


def modal_finish(intra, starts, reach, incoming, rates_t, scale):
    count = starts.shape[0]
    index = jnp.arange(count, dtype=jnp.float32)[:, None, None]
    starts = starts + jnp.exp(-rates_t[None] * (index * (BLOCK * scale))) * incoming[None]
    mixed = intra
    for mode in range(starts.shape[1]):
        mixed = mixed + starts[:, mode][:, None, :] * reach[:, mode][None]
    return mixed.reshape(-1, intra.shape[2])


def per_device(features, short_filter, residues, rates):
    rows = features.shape[0]
    scale = 1.0 / (rows * lax.axis_size("ctx"))
    tail = from_behind(features[-2:], "ctx", 1)
    taps_all, residue_all, rate_all = (
        lax.all_gather(short_filter.astype(jnp.float32), "ctx", axis=2, tiled=True),
        lax.all_gather(residues, "ctx", axis=0, tiled=True),
        lax.all_gather(rates, "ctx", axis=0, tiled=True),
    )
    rates_t = rate_all.T
    coef_t = (residue_all * jnp.sqrt(-jnp.expm1(-2.0 * rate_all * scale))).T
    powers, kernel, reach, block_decay = prepare(rates_t, coef_t, scale)
    filtered = featurize(tail, features, taps_all)
    drive = filtered[:, 1] * filtered[:, 2]
    intra, starts, local_end = modal_local(drive, powers, kernel, block_decay)

    def carry_join(earlier, later):
        return (
            earlier[0] + later[0],
            jnp.exp(-rates_t * (rows * scale) * later[0]) * earlier[1] + later[1],
        )

    shard_count = jnp.ones((1,), jnp.float32)
    identity = (jnp.zeros((1,), jnp.float32), jnp.zeros_like(local_end))
    incoming = carried_in((shard_count, local_end), "ctx", carry_join, identity)[1]
    mixed = modal_finish(intra, starts, reach, incoming, rates_t, scale)
    return (filtered[:, 0] * mixed).astype(jnp.bfloat16)


def solution(mesh):
    in_specs = (
        P(("groups", "ctx"), None, None),
        P(None, None, "ctx"),
        P("ctx", None),
        P("ctx", None),
    )
    out_specs = P(("groups", "ctx"), None)
    return jax.shard_map(
        per_device, mesh=mesh, in_specs=in_specs, out_specs=out_specs, check_vma=False
    )
```

profile of v0, /device:TPU:1, one launch (start us, length us, event | category | flops | bytes accessed | tf_op | source)
XLA Modules:
  0.0 367.1 jit_solution(7102333934976114112)
XLA Ops:
  7.6 4.5 %collective-permute-start = (bf16[2,3,8192]{2,0,1:T(2,128)(2,1)S(1)}, bf16[2,3,8192]{2,0,1:T(2,128)(2,1)S(1)}, u32[]{:S(2)}, u32[]{:S(2)}) collective-permute-start(bf16[2,3,8192]{2,0,1:T(2,128)(2,1)S(1)} %slice.314), channel_id=1, source_target_pairs={{0,1},{1,2},{2,3},{3,4},{4,5},{5,6},{6,7},{7,8},{8,9},{9,10},{10,1... | collective-permute-start | bytes 294920 | tf_op jit(solution)/shard_map/ppermute | solution.py:12
  12.9 21.4 %all_gather.18 = f32[3,3,8192]{2,1,0:T(4,128)S(1)} all-gather(f32[3,3,512]{2,1,0:T(4,128)S(1)} %convert_element_type.39), channel_id=1, replica_groups=mesh['groups'=2,'ctx'=16] {'ctx'}, dimensions={2}, use_global_device_ids=true | all-gather | bytes 313344 | tf_op jit(solution)/shard_map/all_gather | solution.py:81
  35.1 19.1 %all_gather.20 = f32[8192,16]{0,1:T(8,128)S(1)} all-gather(f32[512,16]{0,1:T(8,128)} %param.11), channel_id=1, replica_groups=mesh['groups'=2,'ctx'=16] {'ctx'}, dimensions={0}, use_global_device_ids=true | all-gather | bytes 557056 | tf_op jit(solution)/shard_map/all_gather | solution.py:83
  54.2 20.5 %all_gather.19 = f32[8192,16]{0,1:T(8,128)S(1)} all-gather(f32[512,16]{0,1:T(8,128)} %param.10), channel_id=1, replica_groups=mesh['groups'=2,'ctx'=16] {'ctx'}, dimensions={0}, use_global_device_ids=true | all-gather | bytes 557056 | tf_op jit(solution)/shard_map/all_gather | solution.py:82
  75.3 5.2 %multiply_reduce_fusion = (f32[16,8192]{1,0:T(8,128)}, f32[16,16,8192]{2,1,0:T(8,128)}, f32[16,16,8192]{2,1,0:T(8,128)S(1)}) fusion(f32[16,8192]{1,0:T(8,128)S(1)} %get-tuple-element.461, f32[16,8192]{1,0:T(8,128)S(1)} %get-tuple-element.331, f32[16,8192]{1,0:T(8,128)S(1)} %get-tuple-element.330), kind=kLoop, calls=%fused_computation.12 | loop fusion | flops 10354688 | bytes 18874368 | tf_op jit(solution)/shard_map/reduce_sum | solution.py:41
  80.4 3.1 slice_bitcast_fusion.16
  85.0 29.2 %all-reduce.15 = f32[16]{0:T(128)S(1)} all-reduce(f32[16]{0:T(128)S(1)} %dynamic-update-slice), channel_id=1, replica_groups=mesh['groups'=2,'ctx'=16] {'ctx'}, use_global_device_ids=true, to_apply=%add.15 | all-reduce | flops 16 | bytes 128
  114.1 27.4 %fusion.6 = (f32[16,1,8192]{2,1,0:T(1,128)}, f32[16,1,8192]{2,1,0:T(1,128)}, f32[16,1,8192]{2,1,0:T(1,128)}, f32[16,1,8192]{2,1,0:T(1,128)}, f32[16,1,8192]{2,1,...) fusion(f32[16,16,8192]{2,1,0:T(8,128)} %get-tuple-element.311), kind=kLoop, calls=%fused_computation.94 | loop fusion | bytes 16777216 | tf_op jit(solution)/shard_map/slice | solution.py:72
  141.6 4.8 %maximum_convert_fusion = f32[130,3,8192]{2,0,1:T(8,128)S(1)} fusion(bf16[128,3,8192]{2,0,1:T(8,128)(2,1)} %param.8, bf16[2,3,8192]{2,0,1:T(2,128)(2,1)S(1)} %collective-permute-done), kind=kLoop, calls=%fused_computation.13 | loop fusion | flops 12779520 | bytes 19169280 | tf_op jit(solution)/shard_map/convert_element_type | solution.py:33
  146.4 7.5 %fusion.1 = f32[128,3,8192]{2,0,1:T(8,128)} fusion(f32[130,3,8192]{2,0,1:T(8,128)S(1)} %maximum_convert_fusion, f32[3,8192]{1,0:T(4,128)} %get-tuple-element.334, f32[3,8192]{1,0:T(4,128)} %get-tuple-element.335, f32[3,8192]{1,0:T(4,128)S(1)} %get-tuple-element.333), kind=kLoop, calls=%fused_computation.6 | loop fusion | flops 15728640 | bytes 50626560 | tf_op jit(solution)/shard_map/add | solution.py:35
  153.8 3.9 %slice_multiply_fusion.3 = f32[128,1,8192]{2,0,1:T(8,128)S(1)} fusion(f32[128,3,8192]{2,0,1:T(8,128)} %fusion.1), kind=kLoop, calls=%fused_computation.14 | loop fusion | flops 1048576 | bytes 12582912 | tf_op jit(solution)/shard_map/mul | solution.py:89
  157.8 3.9 %fusion.8 = (f32[8,1,8192]{2,1,0:T(1,128)S(1)}, f32[8,1,8192]{2,1,0:T(1,128)S(1)}, f32[8,1,8192]{2,1,0:T(1,128)S(1)}, f32[8,1,8192]{2,1,0:T(1,128)S(1)}, f32[8,1...) fusion(f32[8,16,8192]{2,1,0:T(8,128)S(1)} %bitcast.210), kind=kLoop, calls=%fused_computation.96 | loop fusion | bytes 8388608 | tf_op jit(solution)/shard_map/slice | solution.py:57
  163.1 2.1 copy_bitcast_fusion.38
  168.4 5.8 %multiply_add_fusion.2 = f32[8,16,8192]{2,1,0:T(8,128)} fusion(f32[16,8192]{1,0:T(8,128)S(1)} %copy-done.19, f32[8,8192]{1,0:T(8,128)S(1)} %get-tuple-element.336, f32[16,8192]{1,0:T(8,128)S(1)} %copy-done.5, f32[8,8192]{1,0:T(8,128)S(1)} %get-tuple-element.337, f32[16,8192]{1,0:T(8,128)S(1)} %copy-done.6, f32[8,8192]{1,0:T(8,128)S(1)} %get-tuple-element.338, ...), kind=kLoop, calls=%fused_computation.20 | loop fusion | flops 32505856 | bytes 16777216 | tf_op jit(solution)/shard_map/add | solution.py:57
  174.2 18.1 %while.29 = (s32[]{:T(128)}, f32[16,8192]{1,0:T(8,128)S(1)}, f32[8,16,8192]{2,1,0:T(8,128)}, f32[16,8192]{1,0:T(8,128)S(1)}, f32[8,16,8192]{2,1,0:T(8,128)}, /*index=5*/s32[]{:T(128)}, s32[]{:T(128)}) while((s32[]{:T(128)}, f32[16,8192]{1,0:T(8,128)S(1)}, f32[8,16,8192]{2,1,0:T(8,128)}, f32[16,8192]{1,0:T(8,128)S(1)}, ...), condition=%wide.region_2.3_spmd.clone, body=%wide.region_1.2_spmd.clone.sunk | while | flops 524291 | bytes 3146332 | solution.py:62
  194.2 2.9 copy_bitcast_fusion
  197.1 2.9 copy_bitcast_fusion.2
  217.7 48.5 %all-gather.3.cloned.1.call-done = f32[256,8192]{1,0:T(8,128)} async-done(((f32[16,8192]{1,0:T(8,128)}), f32[256,8192]{1,0:T(8,128)}) %all-gather.3.cloned.1.call-update) | async-done | bytes 8388624 | tf_op jit(solution)/shard_map/all_gather | solution.py:17
  266.2 41.4 %while.30 = (s32[]{:T(128)}, f32[16,8192]{1,0:T(8,128)S(1)}, s32[]{:T(128)}, f32[16,1]{0,1:T(1,128)S(1)}, f32[16,8192]{1,0:T(8,128)S(1)}, /*index=5*/f32[16,16,8192]{2,1,0:T(8,128)}, s32[]{:T(128)}, s32[]{:T(128)}) while((s32[]{:T(128)}, f32[16,8192]{1,0:T(8,128)S(1)}, s32[]{:T(128)}, f32[16,1]{0,1:T(1,128)S(1)}, ...), condition=%wide.region_4.5_spmd.clone, body=%wide.region_3.4_spmd.clone.sunk | while | flops 655365 | bytes 2097277 | solution.py:29
  269.4 2.0 fusion.13
  307.6 2.9 multiply_add_fusion.1
  310.5 4.3 %fusion.7 = (f32[8,1,8192]{2,1,0:T(1,128)S(1)}, f32[8,1,8192]{2,1,0:T(1,128)S(1)}, f32[8,1,8192]{2,1,0:T(1,128)S(1)}, f32[8,1,8192]{2,1,0:T(1,128)S(1)}, f32[8,1...) fusion(f32[8,16,8192]{2,1,0:T(8,128)S(1)} %multiply_add_fusion.1), kind=kLoop, calls=%fused_computation.95 | loop fusion | bytes 8388608 | tf_op jit(solution)/shard_map/slice | solution.py:72
  328.7 26.4 %multiply_add_fusion = f32[8,16,8192]{2,1,0:T(8,128)} fusion(f32[8,1,8192]{2,1,0:T(1,128)} %copy-done.4, f32[8,2,8192]{2,1,0:T(2,128)} %slice.454, f32[8,3,8192]{2,1,0:T(4,128)} %slice.452, f32[8,4,8192]{2,1,0:T(4,128)S(1)} %slice.450, f32[8,5,8192]{2,1,0:T(8,128)} %slice.448, f32[8,6,8192]{2,1,0:T(8,128)} %slice.446, f32[8,7,8192]{2,1,0:T(8,128)} %slice.444, ...), kind=kLoop, calls=%fused_computation.18 | loop fusion | flops 66060288 | bytes 52953088 | tf_op jit(solution)/shard_map/add | solution.py:72
  355.1 5.2 %fusion.4 = bf16[128,8192]{1,0:T(8,128)(2,1)} fusion(f32[128,3,8192]{2,0,1:T(8,128)} %fusion.1, f32[8,16,8192]{2,1,0:T(8,128)} %multiply_add_fusion), kind=kLoop, calls=%fused_computation.17 | loop fusion | flops 2097152 | bytes 10485760 | tf_op jit(solution)/shard_map/convert_element_type | solution.py:102
  (179 shorter events, 99.0 us)
Async XLA Ops:
  6.5 259.7 %all-gather.3.cloned.1.call-start = ((), (), s32[]{:S(2)}) async-start(), calls=%async_computation | async-start | bytes 8912896 | tf_op jit(solution)/shard_map/all_gather | solution.py:17
  7.6 133.9 %collective-permute-start = (bf16[2,3,8192]{2,0,1:T(2,128)(2,1)S(1)}, bf16[2,3,8192]{2,0,1:T(2,128)(2,1)S(1)}, u32[]{:S(2)}, u32[]{:S(2)}) collective-permute-start(bf16[2,3,8192]{2,0,1:T(2,128)(2,1)S(1)} %slice.314), channel_id=1, source_target_pairs={{0,1},{1,2},{2,3},{3,4},{4,5},{5,6},{6,7},{7,8},{8,9},{9,10},{10,1... | collective-permute-start | bytes 294920 | tf_op jit(solution)/shard_map/ppermute | solution.py:12
  161.7 6.6 %copy-start.4 = (f32[8,1,8192]{2,1,0:T(1,128)}, f32[8,1,8192]{2,1,0:T(1,128)S(1)}, u32[]{:S(2)}) copy-start(f32[8,1,8192]{2,1,0:T(1,128)S(1)} %get-tuple-element.309) | copy-start | bytes 786436
  161.7 6.5 %copy-start.5 = (f32[16,8192]{1,0:T(8,128)S(1)}, f32[16,8192]{1,0:T(8,128)}, u32[]{:S(2)}) copy-start(f32[16,8192]{1,0:T(8,128)} %get-tuple-element.263) | copy-start | bytes 1572868
  161.7 6.5 %copy-start.6 = (f32[16,8192]{1,0:T(8,128)S(1)}, f32[16,8192]{1,0:T(8,128)}, u32[]{:S(2)}) copy-start(f32[16,8192]{1,0:T(8,128)} %get-tuple-element.264) | copy-start | bytes 1572868
  161.7 6.5 %copy-start.7 = (f32[16,8192]{1,0:T(8,128)S(1)}, f32[16,8192]{1,0:T(8,128)}, u32[]{:S(2)}) copy-start(f32[16,8192]{1,0:T(8,128)} %get-tuple-element.265) | copy-start | bytes 1572868
  161.7 6.5 %copy-start.8 = (f32[16,8192]{1,0:T(8,128)S(1)}, f32[16,8192]{1,0:T(8,128)}, u32[]{:S(2)}) copy-start(f32[16,8192]{1,0:T(8,128)} %get-tuple-element.266) | copy-start | bytes 1572868
  161.8 6.5 %copy-start.9 = (f32[16,8192]{1,0:T(8,128)S(1)}, f32[16,8192]{1,0:T(8,128)}, u32[]{:S(2)}) copy-start(f32[16,8192]{1,0:T(8,128)} %get-tuple-element.267) | copy-start | bytes 1572868
  161.8 6.5 %copy-start.10 = (f32[16,8192]{1,0:T(8,128)S(1)}, f32[16,8192]{1,0:T(8,128)}, u32[]{:S(2)}) copy-start(f32[16,8192]{1,0:T(8,128)} %get-tuple-element.268) | copy-start | bytes 1572868
  161.8 6.5 %copy-start.11 = (f32[16,8192]{1,0:T(8,128)S(1)}, f32[16,8192]{1,0:T(8,128)}, u32[]{:S(2)}) copy-start(f32[16,8192]{1,0:T(8,128)} %get-tuple-element.269) | copy-start | bytes 1572868
  174.2 18.9 %copy-start.20 = (f32[16,8192]{1,0:T(8,128)S(1)}, f32[16,8192]{1,0:T(8,128)}, u32[]{:S(2)}) copy-start(f32[16,8192]{1,0:T(8,128)} %get-tuple-element.310) | copy-start | bytes 1572868
  192.3 9.3 %copy-start.29 = (f32[16,1,8192]{2,1,0:T(1,128)S(1)}, f32[16,1,8192]{2,1,0:T(1,128)}, u32[]{:S(2)}) copy-start(f32[16,1,8192]{2,1,0:T(1,128)} %get-tuple-element.253) | copy-start | bytes 1572868
  192.4 9.3 %copy-start.30 = (f32[16,1,8192]{2,1,0:T(1,128)S(1)}, f32[16,1,8192]{2,1,0:T(1,128)}, u32[]{:S(2)}) copy-start(f32[16,1,8192]{2,1,0:T(1,128)} %get-tuple-element.254) | copy-start | bytes 1572868
  193.2 6.9 %copy-start.31 = (f32[16,1,8192]{2,1,0:T(1,128)S(1)}, f32[16,1,8192]{2,1,0:T(1,128)}, u32[]{:S(2)}) copy-start(f32[16,1,8192]{2,1,0:T(1,128)} %get-tuple-element.251) | copy-start | bytes 1572868
  193.2 6.8 %copy-start.32 = (f32[16,1,8192]{2,1,0:T(1,128)S(1)}, f32[16,1,8192]{2,1,0:T(1,128)}, u32[]{:S(2)}) copy-start(f32[16,1,8192]{2,1,0:T(1,128)} %get-tuple-element.252) | copy-start | bytes 1572868
  194.2 9.0 %copy-start.27 = (f32[16,1,8192]{2,1,0:T(1,128)S(1)}, f32[16,1,8192]{2,1,0:T(1,128)}, u32[]{:S(2)}) copy-start(f32[16,1,8192]{2,1,0:T(1,128)} %get-tuple-element.255) | copy-start | bytes 1572868
  194.2 9.0 %copy-start.28 = (f32[16,1,8192]{2,1,0:T(1,128)S(1)}, f32[16,1,8192]{2,1,0:T(1,128)}, u32[]{:S(2)}) copy-start(f32[16,1,8192]{2,1,0:T(1,128)} %get-tuple-element.256) | copy-start | bytes 1572868
  197.1 7.7 %copy-start.25 = (f32[16,1,8192]{2,1,0:T(1,128)S(1)}, f32[16,1,8192]{2,1,0:T(1,128)}, u32[]{:S(2)}) copy-start(f32[16,1,8192]{2,1,0:T(1,128)} %get-tuple-element.257) | copy-start | bytes 1572868
  197.1 7.7 %copy-start.26 = (f32[16,1,8192]{2,1,0:T(1,128)S(1)}, f32[16,1,8192]{2,1,0:T(1,128)}, u32[]{:S(2)}) copy-start(f32[16,1,8192]{2,1,0:T(1,128)} %get-tuple-element.258) | copy-start | bytes 1572868
  314.8 13.9 %copy-start.3 = (f32[8,8,8192]{2,1,0:T(8,128)S(1)}, f32[8,8,8192]{2,1,0:T(8,128)}, u32[]{:S(2)}) copy-start(f32[8,8,8192]{2,1,0:T(8,128)} %slice.442) | copy-start | bytes 6291460
  314.8 13.9 %copy-start.35 = (f32[1,8192]{1,0:T(1,128)S(1)}, f32[1,8192]{1,0:T(1,128)}, u32[]{:S(2)}) copy-start(f32[1,8192]{1,0:T(1,128)} %get-tuple-element.319) | copy-start | bytes 98308
  314.9 13.8 %copy-start.36 = (f32[1,8192]{1,0:T(1,128)S(1)}, f32[1,8192]{1,0:T(1,128)}, u32[]{:S(2)}) copy-start(f32[1,8192]{1,0:T(1,128)} %get-tuple-element.320) | copy-start | bytes 98308
  314.9 13.8 %copy-start.37 = (f32[1,8192]{1,0:T(1,128)S(1)}, f32[1,8192]{1,0:T(1,128)}, u32[]{:S(2)}) copy-start(f32[1,8192]{1,0:T(1,128)} %get-tuple-element.321) | copy-start | bytes 98308
  314.9 13.8 %copy-start.38 = (f32[1,8192]{1,0:T(1,128)S(1)}, f32[1,8192]{1,0:T(1,128)}, u32[]{:S(2)}) copy-start(f32[1,8192]{1,0:T(1,128)} %get-tuple-element.322) | copy-start | bytes 98308
  (18 other events, 104.8 us)
Sparse Core Ops, SparseCore 0:
  193.3 72.8 all-gather.2
where the time goes:
time: 369 us; the launch traced here: 367 us
  other arithmetic  122 us (33%)
  blocking collectives  90.2 us (24%)
  local copies, waits for them, and re-layouts  87.5 us (24%)
  waiting for transfers between devices  48.6 us (13%)
  between operations  14 us (4%)
  starting transfers between devices  4.54 us (1%)
    all_gather x1, waiting for transfers between devices, carried_in(): everything = jax.tree.map(lambda part: lax.all_gather(part, axis), value)  48.5 us
    unnamed x115, local copies, waits for them, and re-layouts  37.8 us
    slice x2, local copies, waits for them, and re-layouts, modal_finish(): mixed = mixed + starts[:, mode][:, None, :] * reach[:, mode][None]  31.7 us
    select_n x16, other arithmetic, step(): return jax.tree.map(lambda a, b: jnp.where(reached, a, b), new, before)  31.7 us
    unnamed x1, blocking collectives  29.2 us
    add x1, other arithmetic, modal_finish(): mixed = mixed + starts[:, mode][:, None, :] * reach[:, mode][None]  26.4 us
    all_gather x1, blocking collectives, per_device(): lax.all_gather(short_filter.astype(jnp.float32), 'ctx', axis=2, tiled=True)  21.4 us
    all_gather x1, blocking collectives, per_device(): lax.all_gather(residues, 'ctx', axis=0, tiled=True)  20.5 us
  transfers between devices with their start and end apart: 2, of which 1 were waited for; matrix products, arithmetic and copies ran while one was open for 17% of the time, Pallas kernels for 0%

commit v1 on v0

v1 whole, which is shorter than its diff:
```python
import functools
import jax
import jax.numpy as jnp
from jax import lax
from jax.experimental import pallas as pl
from jax.experimental.pallas import tpu as pltpu
from jax.sharding import PartitionSpec as P

WIDTH = 512
LANES = 128
CHUNKS = WIDTH // LANES
HALF = 8
SUB = 8
TAPS = 9


def rows_out(scratch, natural, first, stride):
    for k in range(CHUNKS):
        scratch[pl.ds(first + k, natural.shape[0], stride=stride), :] = natural[
            :, k * LANES : (k + 1) * LANES
        ]


def modes_out(scratch, natural):
    for h in range(2):
        rows_out(scratch, natural[h * HALF : (h + 1) * HALF], h * CHUNKS, SUB)


def registers(scratch, count):
    return [scratch[j * SUB : (j + 1) * SUB, :] for j in range(count)]


def local_kernel(
    scale, unroll, ids, feats, tail, params, coef, ends, packed, fkv, fq, taps_s, a_s, c_s, s_s
):
    rows = feats.shape[1]
    rows_out(a_s, jnp.exp(params[0, 0:HALF] * (-scale)), 0, SUB)
    rows_out(a_s, jnp.exp(params[0, HALF : 2 * HALF] * (-scale)), CHUNKS, SUB)
    modes_out(c_s, coef[0])
    rows_out(taps_s, params[0, 2 * HALF : 2 * HALF + TAPS], CHUNKS, CHUNKS)
    for branch, dest, first in ((1, fkv, 0), (2, fkv, CHUNKS), (0, fq, CHUNKS)):
        rows_out(dest, tail[branch].astype(jnp.float32), first, SUB)
        rows_out(dest, feats[branch].astype(jnp.float32), 2 * SUB + first, SUB)
    a = registers(a_s, HALF)
    c = registers(c_s, HALF)
    tap = [taps_s[pl.ds(CHUNKS + (3 * j + 1) * CHUNKS, SUB), :] for j in range(3)]
    tap_q = [taps_s[pl.ds((3 * j) * CHUNKS, SUB), :] for j in range(3)]
    upper = lax.broadcasted_iota(jnp.int32, (SUB, LANES), 0) >= CHUNKS

    def step(t0, carry):
        state, f1, f2, q1, q2 = carry
        state = list(state)
        for u in range(unroll):
            at = pl.multiple_of((t0 * unroll + u + 2) * SUB, SUB)
            f0 = fkv[pl.ds(at, SUB), :]
            q0 = fq[pl.ds(at, SUB), :]
            filtered = tap[0] * f0 + tap[1] * f1 + tap[2] * f2
            query = tap_q[0] * q0 + tap_q[1] * q1 + tap_q[2] * q2
            drive = filtered * pltpu.roll(filtered, CHUNKS, 0)
            terms = []
            for j in range(HALF):
                state[j] = a[j] * state[j] + drive
                terms.append(c[j] * state[j])
            while len(terms) > 1:
                terms = [x + y for x, y in zip(terms[::2], terms[1::2])]
            y = terms[0] + pltpu.roll(terms[0], CHUNKS, 0)
            packed[0, pl.ds(pl.multiple_of((t0 * unroll + u) * SUB, SUB), SUB), :] = jnp.where(
                upper, query, y
            )
            f1, f2, q1, q2 = f0, f1, q0, q1
        return tuple(state), f1, f2, q1, q2

    zero = jnp.zeros((SUB, LANES), jnp.float32)
    start = (
        (zero,) * HALF,
        fkv[SUB : 2 * SUB, :],
        fkv[0:SUB, :],
        fq[SUB : 2 * SUB, :],
        fq[0:SUB, :],
    )
    state = lax.fori_loop(0, rows // unroll, step, start)[0]
    for j in range(HALF):
        s_s[j * SUB : (j + 1) * SUB, :] = state[j]
    for h in range(2):
        for k in range(CHUNKS):
            ends[0, h * HALF : (h + 1) * HALF, k * LANES : (k + 1) * LANES] = s_s[
                pl.ds(h * CHUNKS + k, HALF, stride=SUB), :
            ]


def finish_kernel(scale, unroll, ids, packed, params, coef, incoming, out, a_s, p_s, y_s):
    rows = out.shape[0]
    decay = jnp.exp(params[0, 0 : 2 * HALF] * (-scale))
    modes_out(a_s, decay)
    modes_out(p_s, coef[0] * decay * incoming[0])
    a = registers(a_s, HALF)

    def step(t0, p):
        p = list(p)
        for u in range(unroll):
            at = pl.multiple_of((t0 * unroll + u) * SUB, SUB)
            z = packed[0, pl.ds(at, SUB), :]
            terms = p
            while len(terms) > 1:
                terms = [x + y for x, y in zip(terms[::2], terms[1::2])]
            y = terms[0] + pltpu.roll(terms[0], CHUNKS, 0)
            y_s[pl.ds(at, SUB), :] = (z + y) * pltpu.roll(z, CHUNKS, 0)
            p = [x * d for x, d in zip(p, a)]
        return tuple(p)

    lax.fori_loop(0, rows // unroll, step, tuple(registers(p_s, HALF)))
    for k in range(CHUNKS):
        out[:, k * LANES : (k + 1) * LANES] = y_s[pl.ds(k, rows, stride=SUB), :].astype(out.dtype)


def by_piece(*shape):
    return pl.BlockSpec((1,) + shape, lambda i, ids: (i, 0, 0))


def local_part(ids, feats, tail, params, coef, scale):
    pieces, rows = params.shape[0], feats.shape[1]
    f32 = jnp.float32
    column = lambda i, ids: (0, 0, ids[i])
    return pl.pallas_call(
        functools.partial(local_kernel, scale, 8),
        out_shape=(
            jax.ShapeDtypeStruct((pieces, 2 * HALF, WIDTH), f32),
            jax.ShapeDtypeStruct((pieces, rows * SUB, LANES), f32),
        ),
        grid_spec=pltpu.PrefetchScalarGridSpec(
            num_scalar_prefetch=1,
            grid=(pieces,),
            in_specs=[
                pl.BlockSpec((3, rows, WIDTH), column),
                pl.BlockSpec((3, 2, WIDTH), column),
                by_piece(*params.shape[1:]),
                by_piece(*coef.shape[1:]),
            ],
            out_specs=[by_piece(2 * HALF, WIDTH), by_piece(rows * SUB, LANES)],
            scratch_shapes=[
                pltpu.VMEM(((rows + 2) * SUB, LANES), f32),
                pltpu.VMEM(((rows + 2) * SUB, LANES), f32),
                pltpu.VMEM(((TAPS + 1) * CHUNKS, LANES), f32),
                pltpu.VMEM((HALF * SUB, LANES), f32),
                pltpu.VMEM((HALF * SUB, LANES), f32),
                pltpu.VMEM((HALF * SUB, LANES), f32),
            ],
        ),
        name="local_part",
    )(ids, feats, tail, params, coef)


def finish_part(ids, packed, params, coef, incoming, scale):
    pieces, rows = packed.shape[0], packed.shape[1] // SUB
    f32 = jnp.float32
    return pl.pallas_call(
        functools.partial(finish_kernel, scale, 8),
        out_shape=jax.ShapeDtypeStruct((rows, pieces * WIDTH), jnp.bfloat16),
        grid_spec=pltpu.PrefetchScalarGridSpec(
            num_scalar_prefetch=1,
            grid=(pieces,),
            in_specs=[
                by_piece(rows * SUB, LANES),
                by_piece(*params.shape[1:]),
                by_piece(*coef.shape[1:]),
                by_piece(2 * HALF, WIDTH),
            ],
            out_specs=pl.BlockSpec((rows, WIDTH), lambda i, ids: (0, ids[i])),
            scratch_shapes=[
                pltpu.VMEM((HALF * SUB, LANES), f32),
                pltpu.VMEM((HALF * SUB, LANES), f32),
                pltpu.VMEM((rows * SUB, LANES), f32),
            ],
        ),
        name="finish_part",
    )(ids, packed, params, coef, incoming)


def swap(value, bit):
    size = lax.axis_size("ctx")
    return lax.ppermute(value, "ctx", [(i, i ^ bit) for i in range(size)])


def gather_pieces(value, bits):
    value = value[None]
    for bit in bits:
        value = jnp.concatenate([value, swap(value, bit)], 0)
    return value


def exchange_by_swaps(ends, rates, me, span, bits):
    split = bits[-2:]
    whole = bits[:-2]
    mine, kept, count = ends, [], 1
    decay = jnp.exp(rates * (-span))
    for bit in reversed(split):
        half = mine.shape[0] // 2
        theirs = swap(mine[half:], bit)
        mine, decay = mine[:half], decay[:half]
        later = (me & bit) != 0
        low = jnp.where(later, theirs, mine)
        high = jnp.where(later, mine, theirs)
        kept.append((bit, later, low, decay))
        mine = decay * low + high
        decay = decay * decay
    before = jnp.zeros_like(mine)
    total = mine
    reach = jnp.ones_like(decay)
    for bit in sorted(whole):
        place = whole.index(bit)
        flat = swap(total, bit)
        other = flat.reshape((2,) * len(whole) + flat.shape[1:])
        other = jnp.flip(other, len(whole) - 1 - place).reshape(flat.shape)
        later = (me & bit) != 0
        low = jnp.where(later, other, total)
        high = jnp.where(later, total, other)
        before = before + jnp.where(later, reach * low, 0.0)
        total = decay * low + high
        reach = reach * jnp.where(later, decay, 1.0)
        decay = decay * decay
    for bit, later, low, decay in reversed(kept):
        after = decay * before + low
        theirs = swap(jnp.where(later, before, after), bit)
        before = jnp.concatenate([jnp.where(later, after, before), theirs], 0)
    return before


def to_pieces(value):
    rows = value.shape[0]
    return value.reshape(rows, -1, WIDTH).transpose(1, 0, 2)


def exchange_by_owner(ends, rates_t, me, span):
    size = lax.axis_size("ctx")
    modes = ends.shape[1]
    blocks = ends.transpose(1, 0, 2).reshape(modes, size, -1).transpose(1, 0, 2)
    blocks = lax.all_to_all(blocks, "ctx", 0, 0, tiled=True)
    decay = jnp.exp(rates_t * (-span))

    def advance(carry, end):
        return decay * carry + end, carry

    before = lax.scan(advance, jnp.zeros_like(blocks[0]), blocks)[1]
    before = lax.all_to_all(before, "ctx", 0, 0, tiled=True)
    return to_pieces(before.transpose(1, 0, 2).reshape(modes, -1))


def per_device(features, short_filter, residues, rates):
    rows = features.shape[0]
    size = lax.axis_size("ctx")
    me = lax.axis_index("ctx")
    scale = 1.0 / (rows * size)
    feats = features.transpose(1, 0, 2)
    tail = lax.ppermute(feats[:, -2:], "ctx", [(i, i + 1) for i in range(size - 1)])
    rates_t = rates.T
    coef_t = (residues * jnp.sqrt(-jnp.expm1(-2.0 * rates * scale))).T
    taps = short_filter.astype(jnp.float32).reshape(TAPS, -1)
    params = jnp.concatenate([rates_t, taps], 0)
    by_swaps = rates.shape[0] == WIDTH and size == 16
    if by_swaps:
        bits = (8, 4, 2, 1)
        params_all = gather_pieces(params, bits)
        coef_all = gather_pieces(coef_t, bits)
        order = [0]
        for bit in bits:
            order += [x ^ bit for x in order]
        ids = jnp.bitwise_xor(jnp.array(order, jnp.int32), me.astype(jnp.int32))
    else:
        params_all = to_pieces(lax.all_gather(params, "ctx", axis=1, tiled=True))
        coef_all = to_pieces(lax.all_gather(coef_t, "ctx", axis=1, tiled=True))
        ids = jnp.arange(params_all.shape[0], dtype=jnp.int32)
    ends, packed = local_part(ids, feats, tail, params_all, coef_all, scale)
    if by_swaps:
        incoming = exchange_by_swaps(ends, params_all[:, : 2 * HALF], me, rows * scale, bits)
    else:
        incoming = exchange_by_owner(ends, rates_t, me, rows * scale)
    return finish_part(ids, packed, params_all, coef_all, incoming, scale)


def solution(mesh):
    in_specs = (
        P(("groups", "ctx"), None, None),
        P(None, None, "ctx"),
        P("ctx", None),
        P("ctx", None),
    )
    out_specs = P(("groups", "ctx"), None)
    return jax.shard_map(
        per_device, mesh=mesh, in_specs=in_specs, out_specs=out_specs, check_vma=False
    )
```

time: 369 us -> 100 us (0.27)
  other arithmetic: 122 us -> 5.83 us
  blocking collectives: 90.2 us -> 0 us
  local copies, waits for them, and re-layouts: 87.5 us -> 5.75 us
  Pallas kernels: 0 us -> 35.9 us
  waiting for transfers between devices: 48.6 us -> 27.2 us
  starting transfers between devices: 4.54 us -> 23.9 us
  between operations: 14 us -> 0.19 us
    all_gather x3 -> x0, blocking collectives: 61.1 us -> none  [the longest x1 21.4 us: per_device(): lax.all_gather(short_filter.astype(jnp.float32), 'ctx', axis=2, tiled=True)]
    add x12 -> x2, other arithmetic: 53.6 us -> 0.06 us  [the longest x1 0.04 us: exchange_by_swaps(): total = decay * low + high]
    all_gather x1 -> x0, waiting for transfers between devices: 48.5 us -> none  [carried_in(): everything = jax.tree.map(lambda part: lax.all_gather(part, axis), value)]
    slice x12 -> x4, local copies, waits for them, and re-layouts: 45.8 us -> 3.23 us  [the longest x1 1.1 us: per_device(): feats[:, -2:]]
    unnamed x115 -> x14, local copies, waits for them, and re-layouts: 37.8 us -> 1.73 us
    pallas_call x0 -> x2, Pallas kernels: none -> 35.9 us  [the longest x1 20.7 us: local_part(): pl.pallas_call(functools.partial(local_kernel, scale, 8), out_shape=(jax....]
    select_n x16 -> x3, other arithmetic: 31.7 us -> 0.25 us  [the longest x2 0.21 us: exchange_by_swaps(): before = jnp.concatenate([jnp.where(later, after, before), theirs], 0)]
    unnamed x1 -> x0, blocking collectives: 29.2 us -> none
  transfers between devices with their start and end apart: 2 -> 15, of which waited for: 1 -> 12; matrix products, arithmetic and copies ran while one was open for 17% -> 5% of each run, Pallas kernels for 0% -> 0%
where the time goes in v1:
time: 100 us; the launch traced here: 98.8 us
  Pallas kernels  35.9 us (36%)
  waiting for transfers between devices  27.2 us (27%)
  starting transfers between devices  23.9 us (24%)
  other arithmetic  5.83 us (6%)
  local copies, waits for them, and re-layouts  5.75 us (6%)
    ppermute x14, waiting for transfers between devices, swap(): return lax.ppermute(value, 'ctx', [(i, i ^ bit) for i in range(size)])  27.2 us
    pallas_call x1, Pallas kernels, local_part(): pl.pallas_call(functools.partial(local_kernel, scale, 8), out_shape=(jax....  20.7 us
    ppermute x14, starting transfers between devices, swap(): return lax.ppermute(value, 'ctx', [(i, i ^ bit) for i in range(size)])  19.9 us
    pallas_call x1, Pallas kernels, finish_part(): pl.pallas_call(functools.partial(finish_kernel, scale, 8), out_shape=jax....  15.2 us
    ppermute x1, starting transfers between devices, per_device(): lax.ppermute(feats[:, -2:], 'ctx', [(i, i + 1) for i in range(size - 1)])  3.99 us
  transfers between devices with their start and end apart: 15, of which 12 were waited for; matrix products, arithmetic and copies ran while one was open for 5% of the time, Pallas kernels for 0%

profile of v1, /device:TPU:1, one launch (start us, length us, event | category | flops | bytes accessed | tf_op | source)
XLA Modules:
  0.0 98.8 jit_solution(11439545067295660954)
XLA Ops:
  1.5 3.1 %collective-permute-start.1 = (f32[1,25,512]{2,1,0:T(8,128)S(1)}, f32[1,25,512]{2,1,0:T(8,128)S(1)}, u32[]{:S(2)}, u32[]{:S(2)}) collective-permute-start(f32[1,25,512]{2,1,0:T(8,128)S(1)} %maximum_bitcast_fusion), channel_id=1, source_target_pairs={{0,8},{1,9},{2,10},{3,11},{4,12},{5,13},{6,14},{7,15},{8,0},{9,1},... | collective-permute-start | bytes 153608 | tf_op jit(solution)/shard_map/ppermute | solution.py:181
  5.7 4.0 %collective-permute-start = (bf16[3,2,8192]{2,1,0:T(2,128)(2,1)S(1)}, bf16[3,2,8192]{2,1,0:T(2,128)(2,1)S(1)}, u32[]{:S(2)}, u32[]{:S(2)}) collective-permute-start(bf16[3,2,8192]{2,1,0:T(2,128)(2,1)S(1)} %slice.32), channel_id=1, source_target_pairs={{0,1},{1,2},{2,3},{3,4},{4,5},{5,6},{6,7},{7,8},{8,9},{9,10},{10,1... | collective-permute-start | bytes 294920 | tf_op jit(solution)/shard_map/ppermute | solution.py:254
  10.7 1.2 %broadcast_xor_fusion.ids = s32[16]{0:T(128)} fusion(s32[16]{0:T(128)} %constant.26.clone, s32[]{:T(128)S(6)} %axis_index.12), kind=kLoop, calls=%fused_computation.40 | loop fusion | flops 16 | bytes 132 | tf_op jit(solution)/shard_map/xor | solution.py:267
  12.6 1.7 %collective-permute-done.5 = f32[1,16,512]{2,1,0:T(8,128)S(1)} collective-permute-done((f32[1,16,512]{2,1,0:T(8,128)S(1)}, f32[1,16,512]{2,1,0:T(8,128)S(1)}, u32[]{:S(2)}, u32[]{:S(2)}) %collective-permute-start.5) | collective-permute-done | bytes 32800 | tf_op jit(solution)/shard_map/ppermute | solution.py:181
  14.3 1.3 %collective-permute-start.6 = (f32[2,16,512]{2,1,0:T(8,128)S(1)}, f32[2,16,512]{2,1,0:T(8,128)S(1)}, u32[]{:S(2)}, u32[]{:S(2)}) collective-permute-start(f32[2,16,512]{2,1,0:T(8,128)S(1)} %pad_maximum_fusion.7), channel_id=1, source_target_pairs={{0,4},{1,5},{2,6},{3,7},{4,0},{5,1},{6,2},{7,3},{8,12},{9,13},{10,... | collective-permute-start | bytes 196616 | tf_op jit(solution)/shard_map/ppermute | solution.py:181
  15.8 2.5 %collective-permute-done.6 = f32[2,16,512]{2,1,0:T(8,128)S(1)} collective-permute-done((f32[2,16,512]{2,1,0:T(8,128)S(1)}, f32[2,16,512]{2,1,0:T(8,128)S(1)}, u32[]{:S(2)}, u32[]{:S(2)}) %collective-permute-start.6) | collective-permute-done | bytes 65568 | tf_op jit(solution)/shard_map/ppermute | solution.py:181
  19.3 1.2 %collective-permute-done.2 = f32[2,25,512]{2,1,0:T(8,128)S(1)} collective-permute-done((f32[2,25,512]{2,1,0:T(8,128)S(1)}, f32[2,25,512]{2,1,0:T(8,128)S(1)}, u32[]{:S(2)}, u32[]{:S(2)}) %collective-permute-start.2) | collective-permute-done | bytes 102432 | tf_op jit(solution)/shard_map/ppermute | solution.py:181
  20.5 1.2 %collective-permute-start.3 = (f32[4,25,512]{2,1,0:T(8,128)S(1)}, f32[4,25,512]{2,1,0:T(8,128)S(1)}, u32[]{:S(2)}, u32[]{:S(2)}) collective-permute-start(f32[4,25,512]{2,1,0:T(8,128)S(1)} %pad_maximum_fusion.2), channel_id=1, source_target_pairs={{0,2},{1,3},{2,0},{3,1},{4,6},{5,7},{6,4},{7,5},{8,10},{9,11},{10,... | collective-permute-start | bytes 614408 | tf_op jit(solution)/shard_map/ppermute | solution.py:181
  21.7 1.3 %collective-permute-done.7 = f32[4,16,512]{2,1,0:T(8,128)S(1)} collective-permute-done((f32[4,16,512]{2,1,0:T(8,128)S(1)}, f32[4,16,512]{2,1,0:T(8,128)S(1)}, u32[]{:S(2)}, u32[]{:S(2)}) %collective-permute-start.7) | collective-permute-done | bytes 131104 | tf_op jit(solution)/shard_map/ppermute | solution.py:181
  23.1 2.0 %collective-permute-start.8 = (f32[8,16,512]{2,1,0:T(8,128)S(1)}, f32[8,16,512]{2,1,0:T(8,128)S(1)}, u32[]{:S(2)}, u32[]{:S(2)}) collective-permute-start(f32[8,16,512]{2,1,0:T(8,128)S(1)} %pad_maximum_fusion.3), channel_id=1, source_target_pairs={{0,1},{1,0},{2,3},{3,2},{4,5},{5,4},{6,7},{7,6},{8,9},{9,8},{10,11... | collective-permute-start | bytes 786440 | tf_op jit(solution)/shard_map/ppermute | solution.py:181
  25.0 3.5 %collective-permute-done.3 = f32[4,25,512]{2,1,0:T(8,128)S(1)} collective-permute-done((f32[4,25,512]{2,1,0:T(8,128)S(1)}, f32[4,25,512]{2,1,0:T(8,128)S(1)}, u32[]{:S(2)}, u32[]{:S(2)}) %collective-permute-start.3) | collective-permute-done | bytes 204832 | tf_op jit(solution)/shard_map/ppermute | solution.py:181
  28.6 1.4 %collective-permute-start.4 = (f32[8,25,512]{2,1,0:T(8,128)S(1)}, f32[8,25,512]{2,1,0:T(8,128)S(1)}, u32[]{:S(2)}, u32[]{:S(2)}) collective-permute-start(f32[8,25,512]{2,1,0:T(8,128)S(1)} %pad_maximum_fusion), channel_id=1, source_target_pairs={{0,1},{1,0},{2,3},{3,2},{4,5},{5,4},{6,7},{7,6},{8,9},{9,8},{10,11... | collective-permute-start | bytes 1228808 | tf_op jit(solution)/shard_map/ppermute | solution.py:181
  30.2 1.4 %collective-permute-done.4 = f32[8,25,512]{2,1,0:T(8,128)S(1)} collective-permute-done((f32[8,25,512]{2,1,0:T(8,128)S(1)}, f32[8,25,512]{2,1,0:T(8,128)S(1)}, u32[]{:S(2)}, u32[]{:S(2)}) %collective-permute-start.4) | collective-permute-done | bytes 409632 | tf_op jit(solution)/shard_map/ppermute | solution.py:181
  33.3 20.7 %local_part.1 = (f32[16,16,512]{2,1,0:T(8,128)}, f32[16,1024,128]{2,1,0:T(8,128)}) custom-call(s32[16]{0:T(128)} %broadcast_xor_fusion.ids, bf16[3,128,8192]{2,1,0:T(8,128)(2,1)} %bitcast.35, bf16[3,2,8192]{2,1,0:T(2,128)(2,1)} %copy-done.3, f32[16,25,512]{2,1,0:T(8,128)} %copy-done, f32[16,16,512]{2,1,0:T(8,128)} %copy-done.1), custom_call_target="tpu_custom_call" | custom-call | tf_op jit(solution)/shard_map/local_part/pallas_call | solution.py:124
  57.7 1.2 %collective-permute-start.10 = (f32[4,16,512]{2,1,0:T(8,128)S(1)}, f32[4,16,512]{2,1,0:T(8,128)S(1)}, u32[]{:S(2)}, u32[]{:S(2)}) collective-permute-start(f32[4,16,512]{2,1,0:T(8,128)S(1)} %slice.36), channel_id=1, source_target_pairs={{0,2},{1,3},{2,0},{3,1},{4,6},{5,7},{6,4},{7,5},{8,10},{9,11},{10,... | collective-permute-start | bytes 393224 | tf_op jit(solution)/shard_map/ppermute | solution.py:181
  58.9 3.5 %collective-permute-done.10 = f32[4,16,512]{2,1,0:T(8,128)S(1)} collective-permute-done((f32[4,16,512]{2,1,0:T(8,128)S(1)}, f32[4,16,512]{2,1,0:T(8,128)S(1)}, u32[]{:S(2)}, u32[]{:S(2)}) %collective-permute-start.10) | collective-permute-done | bytes 131104 | tf_op jit(solution)/shard_map/ppermute | solution.py:181
  62.5 1.3 %collective-permute-start.11 = (f32[4,16,512]{2,1,0:T(8,128)S(1)}, f32[4,16,512]{2,1,0:T(8,128)S(1)}, u32[]{:S(2)}, u32[]{:S(2)}) collective-permute-start(f32[4,16,512]{2,1,0:T(8,128)S(1)} %select_add_fusion.1), channel_id=1, source_target_pairs={{0,4},{1,5},{2,6},{3,7},{4,0},{5,1},{6,2},{7,3},{8,12},{9,13},{10,... | collective-permute-start | bytes 393224 | tf_op jit(solution)/shard_map/ppermute | solution.py:181
  63.8 2.6 %collective-permute-done.11 = f32[4,16,512]{2,1,0:T(8,128)S(1)} collective-permute-done((f32[4,16,512]{2,1,0:T(8,128)S(1)}, f32[4,16,512]{2,1,0:T(8,128)S(1)}, u32[]{:S(2)}, u32[]{:S(2)}) %collective-permute-start.11) | collective-permute-done | bytes 131104 | tf_op jit(solution)/shard_map/ppermute | solution.py:181
  67.1 5.5 %collective-permute-done.12 = f32[4,16,512]{2,1,0:T(8,128)S(1)} collective-permute-done((f32[4,16,512]{2,1,0:T(8,128)S(1)}, f32[4,16,512]{2,1,0:T(8,128)S(1)}, u32[]{:S(2)}, u32[]{:S(2)}) %collective-permute-start.12) | collective-permute-done | bytes 131104 | tf_op jit(solution)/shard_map/ppermute | solution.py:181
  72.8 1.2 %collective-permute-start.13 = (f32[4,16,512]{2,1,0:T(8,128)S(1)}, f32[4,16,512]{2,1,0:T(8,128)S(1)}, u32[]{:S(2)}, u32[]{:S(2)}) collective-permute-start(f32[4,16,512]{2,1,0:T(8,128)S(1)} %broadcast_select_fusion), channel_id=1, source_target_pairs={{0,2},{1,3},{2,0},{3,1},{4,6},{5,7},{6,4},{7,5},{8,10},{9,11},{10,... | collective-permute-start | bytes 393224 | tf_op jit(solution)/shard_map/ppermute | solution.py:181
  74.0 2.7 %collective-permute-done.13 = f32[4,16,512]{2,1,0:T(8,128)S(1)} collective-permute-done((f32[4,16,512]{2,1,0:T(8,128)S(1)}, f32[4,16,512]{2,1,0:T(8,128)S(1)}, u32[]{:S(2)}, u32[]{:S(2)}) %collective-permute-start.13) | collective-permute-done | bytes 131104 | tf_op jit(solution)/shard_map/ppermute | solution.py:181
  76.8 4.7 %collective-permute-start.14 = (f32[8,16,512]{2,1,0:T(8,128)S(1)}, f32[8,16,512]{2,1,0:T(8,128)S(1)}, u32[]{:S(2)}, u32[]{:S(2)}) collective-permute-start(f32[8,16,512]{2,1,0:T(8,128)S(1)} %get-tuple-element.14), channel_id=1, source_target_pairs={{0,1},{1,0},{2,3},{3,2},{4,5},{5,4},{6,7},{7,6},{8,9},{9,8},{10,11... | collective-permute-start | bytes 786440 | tf_op jit(solution)/shard_map/ppermute | solution.py:181
  81.5 1.2 %collective-permute-done.14 = f32[8,16,512]{2,1,0:T(8,128)S(1)} collective-permute-done((f32[8,16,512]{2,1,0:T(8,128)S(1)}, f32[8,16,512]{2,1,0:T(8,128)S(1)}, u32[]{:S(2)}, u32[]{:S(2)}) %collective-permute-start.14) | collective-permute-done | bytes 262176 | tf_op jit(solution)/shard_map/ppermute | solution.py:181
  83.6 15.2 %finish_part.1 = bf16[128,8192]{1,0:T(8,128)(2,1)} custom-call(s32[16]{0:T(128)} %broadcast_xor_fusion.ids, f32[16,1024,128]{2,1,0:T(8,128)} %get-tuple-element.7.packed, f32[16,25,512]{2,1,0:T(8,128)} %copy-done, f32[16,16,512]{2,1,0:T(8,128)} %copy-done.1, f32[16,16,512]{2,1,0:T(8,128)} %pad_maximum_fusion.1.incoming), custom_call_target="tpu_custom_call" | custom-call | tf_op jit(solution)/shard_map/finish_part/pallas_call | solution.py:156
  (48 shorter events, 12.9 us)
Async XLA Ops:
  1.5 14.1 %collective-permute-start.1 = (f32[1,25,512]{2,1,0:T(8,128)S(1)}, f32[1,25,512]{2,1,0:T(8,128)S(1)}, u32[]{:S(2)}, u32[]{:S(2)}) collective-permute-start(f32[1,25,512]{2,1,0:T(8,128)S(1)} %maximum_bitcast_fusion), channel_id=1, source_target_pairs={{0,8},{1,9},{2,10},{3,11},{4,12},{5,13},{6,14},{7,15},{8,0},{9,1},... | collective-permute-start | bytes 153608 | tf_op jit(solution)/shard_map/ppermute | solution.py:181
  5.7 25.9 %collective-permute-start = (bf16[3,2,8192]{2,1,0:T(2,128)(2,1)S(1)}, bf16[3,2,8192]{2,1,0:T(2,128)(2,1)S(1)}, u32[]{:S(2)}, u32[]{:S(2)}) collective-permute-start(bf16[3,2,8192]{2,1,0:T(2,128)(2,1)S(1)} %slice.32), channel_id=1, source_target_pairs={{0,1},{1,2},{2,3},{3,4},{4,5},{5,6},{6,7},{7,8},{8,9},{9,10},{10,1... | collective-permute-start | bytes 294920 | tf_op jit(solution)/shard_map/ppermute | solution.py:254
  10.5 3.7 %collective-permute-start.5 = (f32[1,16,512]{2,1,0:T(8,128)S(1)}, f32[1,16,512]{2,1,0:T(8,128)S(1)}, u32[]{:S(2)}, u32[]{:S(2)}) collective-permute-start(f32[1,16,512]{2,1,0:T(8,128)S(1)} %get-tuple-element.12), channel_id=1, source_target_pairs={{0,8},{1,9},{2,10},{3,11},{4,12},{5,13},{6,14},{7,15},{8,0},{9,1},... | collective-permute-start | bytes 98312 | tf_op jit(solution)/shard_map/ppermute | solution.py:181
  14.3 4.1 %collective-permute-start.6 = (f32[2,16,512]{2,1,0:T(8,128)S(1)}, f32[2,16,512]{2,1,0:T(8,128)S(1)}, u32[]{:S(2)}, u32[]{:S(2)}) collective-permute-start(f32[2,16,512]{2,1,0:T(8,128)S(1)} %pad_maximum_fusion.7), channel_id=1, source_target_pairs={{0,4},{1,5},{2,6},{3,7},{4,0},{5,1},{6,2},{7,3},{8,12},{9,13},{10,... | collective-permute-start | bytes 196616 | tf_op jit(solution)/shard_map/ppermute | solution.py:181
  15.6 4.9 %collective-permute-start.2 = (f32[2,25,512]{2,1,0:T(8,128)S(1)}, f32[2,25,512]{2,1,0:T(8,128)S(1)}, u32[]{:S(2)}, u32[]{:S(2)}) collective-permute-start(f32[2,25,512]{2,1,0:T(8,128)S(1)} %pad_maximum_fusion.5), channel_id=1, source_target_pairs={{0,4},{1,5},{2,6},{3,7},{4,0},{5,1},{6,2},{7,3},{8,12},{9,13},{10,... | collective-permute-start | bytes 307208 | tf_op jit(solution)/shard_map/ppermute | solution.py:181
  18.3 4.7 %collective-permute-start.7 = (f32[4,16,512]{2,1,0:T(8,128)S(1)}, f32[4,16,512]{2,1,0:T(8,128)S(1)}, u32[]{:S(2)}, u32[]{:S(2)}) collective-permute-start(f32[4,16,512]{2,1,0:T(8,128)S(1)} %pad_maximum_fusion.6), channel_id=1, source_target_pairs={{0,2},{1,3},{2,0},{3,1},{4,6},{5,7},{6,4},{7,5},{8,10},{9,11},{10,... | collective-permute-start | bytes 393224 | tf_op jit(solution)/shard_map/ppermute | solution.py:181
  20.5 8.1 %collective-permute-start.3 = (f32[4,25,512]{2,1,0:T(8,128)S(1)}, f32[4,25,512]{2,1,0:T(8,128)S(1)}, u32[]{:S(2)}, u32[]{:S(2)}) collective-permute-start(f32[4,25,512]{2,1,0:T(8,128)S(1)} %pad_maximum_fusion.2), channel_id=1, source_target_pairs={{0,2},{1,3},{2,0},{3,1},{4,6},{5,7},{6,4},{7,5},{8,10},{9,11},{10,... | collective-permute-start | bytes 614408 | tf_op jit(solution)/shard_map/ppermute | solution.py:181
  23.1 7.1 %collective-permute-start.8 = (f32[8,16,512]{2,1,0:T(8,128)S(1)}, f32[8,16,512]{2,1,0:T(8,128)S(1)}, u32[]{:S(2)}, u32[]{:S(2)}) collective-permute-start(f32[8,16,512]{2,1,0:T(8,128)S(1)} %pad_maximum_fusion.3), channel_id=1, source_target_pairs={{0,1},{1,0},{2,3},{3,2},{4,5},{5,4},{6,7},{7,6},{8,9},{9,8},{10,11... | collective-permute-start | bytes 786440 | tf_op jit(solution)/shard_map/ppermute | solution.py:181
  28.6 3.0 %collective-permute-start.4 = (f32[8,25,512]{2,1,0:T(8,128)S(1)}, f32[8,25,512]{2,1,0:T(8,128)S(1)}, u32[]{:S(2)}, u32[]{:S(2)}) collective-permute-start(f32[8,25,512]{2,1,0:T(8,128)S(1)} %pad_maximum_fusion), channel_id=1, source_target_pairs={{0,1},{1,0},{2,3},{3,2},{4,5},{5,4},{6,7},{7,6},{8,9},{9,8},{10,11... | collective-permute-start | bytes 1228808 | tf_op jit(solution)/shard_map/ppermute | solution.py:181
  30.1 1.5 %copy-start.1 = (f32[16,16,512]{2,1,0:T(8,128)}, f32[16,16,512]{2,1,0:T(8,128)S(1)}, u32[]{:S(2)}) copy-start(f32[16,16,512]{2,1,0:T(8,128)S(1)} %constant_dynamic-update-slice_fusion.5.coef) | copy-start | bytes 1572868
  31.6 1.1 %copy-start = (f32[16,25,512]{2,1,0:T(8,128)}, f32[16,25,512]{2,1,0:T(8,128)S(1)}, u32[]{:S(2)}) copy-start(f32[16,25,512]{2,1,0:T(8,128)S(1)} %constant_dynamic-update-slice_fusion.params) | copy-start | bytes 2457604
  32.7 0.6 copy-start.3
  54.0 22.7 %copy-start.2 = (f32[16,16,512]{2,1,0:T(8,128)S(1)}, f32[16,16,512]{2,1,0:T(8,128)}, u32[]{:S(2)}) copy-start(f32[16,16,512]{2,1,0:T(8,128)} %get-tuple-element.8) | copy-start | bytes 1572868
  55.0 1.6 %collective-permute-start.9 = (f32[8,16,512]{2,1,0:T(8,128)S(1)}, f32[8,16,512]{2,1,0:T(8,128)S(1)}, u32[]{:S(2)}, u32[]{:S(2)}) collective-permute-start(f32[8,16,512]{2,1,0:T(8,128)S(1)} %slice.28), channel_id=1, source_target_pairs={{0,1},{1,0},{2,3},{3,2},{4,5},{5,4},{6,7},{7,6},{8,9},{9,8},{10,11... | collective-permute-start | bytes 786440 | tf_op jit(solution)/shard_map/ppermute | solution.py:181
  57.7 4.8 %collective-permute-start.10 = (f32[4,16,512]{2,1,0:T(8,128)S(1)}, f32[4,16,512]{2,1,0:T(8,128)S(1)}, u32[]{:S(2)}, u32[]{:S(2)}) collective-permute-start(f32[4,16,512]{2,1,0:T(8,128)S(1)} %slice.36), channel_id=1, source_target_pairs={{0,2},{1,3},{2,0},{3,1},{4,6},{5,7},{6,4},{7,5},{8,10},{9,11},{10,... | collective-permute-start | bytes 393224 | tf_op jit(solution)/shard_map/ppermute | solution.py:181
  62.5 3.9 %collective-permute-start.11 = (f32[4,16,512]{2,1,0:T(8,128)S(1)}, f32[4,16,512]{2,1,0:T(8,128)S(1)}, u32[]{:S(2)}, u32[]{:S(2)}) collective-permute-start(f32[4,16,512]{2,1,0:T(8,128)S(1)} %select_add_fusion.1), channel_id=1, source_target_pairs={{0,4},{1,5},{2,6},{3,7},{4,0},{5,1},{6,2},{7,3},{8,12},{9,13},{10,... | collective-permute-start | bytes 393224 | tf_op jit(solution)/shard_map/ppermute | solution.py:181
  66.5 6.2 %collective-permute-start.12 = (f32[4,16,512]{2,1,0:T(8,128)S(1)}, f32[4,16,512]{2,1,0:T(8,128)S(1)}, u32[]{:S(2)}, u32[]{:S(2)}) collective-permute-start(f32[4,16,512]{2,1,0:T(8,128)S(1)} %fusion.6), channel_id=1, source_target_pairs={{0,8},{1,9},{2,10},{3,11},{4,12},{5,13},{6,14},{7,15},{8,0},{9,1},... | collective-permute-start | bytes 393224 | tf_op jit(solution)/shard_map/ppermute | solution.py:181
  72.8 3.9 %collective-permute-start.13 = (f32[4,16,512]{2,1,0:T(8,128)S(1)}, f32[4,16,512]{2,1,0:T(8,128)S(1)}, u32[]{:S(2)}, u32[]{:S(2)}) collective-permute-start(f32[4,16,512]{2,1,0:T(8,128)S(1)} %broadcast_select_fusion), channel_id=1, source_target_pairs={{0,2},{1,3},{2,0},{3,1},{4,6},{5,7},{6,4},{7,5},{8,10},{9,11},{10,... | collective-permute-start | bytes 393224 | tf_op jit(solution)/shard_map/ppermute | solution.py:181
  76.8 5.9 %collective-permute-start.14 = (f32[8,16,512]{2,1,0:T(8,128)S(1)}, f32[8,16,512]{2,1,0:T(8,128)S(1)}, u32[]{:S(2)}, u32[]{:S(2)}) collective-permute-start(f32[8,16,512]{2,1,0:T(8,128)S(1)} %get-tuple-element.14), channel_id=1, source_target_pairs={{0,1},{1,0},{2,3},{3,2},{4,5},{5,4},{6,7},{7,6},{8,9},{9,8},{10,11... | collective-permute-start | bytes 786440 | tf_op jit(solution)/shard_map/ppermute | solution.py:181

commit v2 on v0

v2 whole, which is shorter than its diff:
```python
import functools
import jax
import jax.numpy as jnp
from jax import lax
from jax.experimental import pallas as pl
from jax.experimental.pallas import tpu as pltpu
from jax.sharding import PartitionSpec as P

WIDTH = 512
LANES = 128
CHUNKS = WIDTH // LANES
HALF = 8
MODES = 2 * HALF
SUB = 8
TAPS = 9
RATE_COLS = 2 * WIDTH
TAP_COLS = RATE_COLS + WIDTH
PARAM_COLS = TAP_COLS + LANES
GROUP = 4
GROUPS = 4
UNROLL = 16
F32 = jnp.float32
VMEM = pl.BlockSpec(memory_space=pltpu.VMEM)


def rows_out(scratch, natural, first, stride):
    for k in range(CHUNKS):
        scratch[pl.ds(first + k, natural.shape[0], stride=stride), :] = natural[
            :, k * LANES : (k + 1) * LANES
        ]


def modes_out(scratch, natural):
    for h in range(2):
        rows_out(scratch, natural[h * HALF : (h + 1) * HALF], h * CHUNKS, SUB)


def rates_of(params, i):
    return jnp.concatenate([params[i, :, 0:WIDTH], params[i, :, WIDTH:RATE_COLS]], 0)


def taps_out(scratch, params, i, first, stride):
    rows_out(scratch, params[i, :, RATE_COLS:TAP_COLS], first, stride)
    at = first + stride * SUB
    scratch[at : at + CHUNKS, :] = params[i, 0:CHUNKS, TAP_COLS:PARAM_COLS]


def registers(scratch, count):
    return [scratch[j * SUB : (j + 1) * SUB, :] for j in range(count)]


def total(terms):
    while len(terms) > 1:
        terms = [x + y for x, y in zip(terms[::2], terms[1::2])]
    return terms[0]


def aligned(index):
    return pl.ds(pl.multiple_of(index, SUB), SUB)


def stage_body(branches, stride, feats, *refs):
    staged, done, held, sems = refs[-4:]
    rows, blocks = feats.shape[1], staged.shape[0]

    def fetch(i, b):
        column = pl.ds(i * WIDTH, WIDTH)
        return pltpu.make_async_copy(feats.at[branches[b], :, column], held.at[i, b], sems.at[i, b])

    for i in range(blocks):
        for b in range(len(branches)):
            fetch(i, b).start()
    for i in range(blocks):
        for b in range(len(branches)):
            fetch(i, b).wait()
            rows_out(staged.at[i], held[i, b].astype(F32), b * CHUNKS, stride)
    done[...] = jnp.zeros_like(done)


def pack_kernel(scale, filters, residues, rates, wide):
    for h in range(2):
        part = slice(h * HALF, (h + 1) * HALF)
        decayed = rates[part] * (2.0 * scale)
        power = jnp.tanh(0.5 * decayed) * (1.0 + jnp.exp(-decayed))
        wide[:, h * WIDTH : (h + 1) * WIDTH] = rates[part]
        at = PARAM_COLS + h * WIDTH
        wide[:, at : at + WIDTH] = residues[part] * jnp.sqrt(power)
    for r in range(TAPS):
        row = filters[r // 3, r % 3 : r % 3 + 1, :].astype(F32)
        if r < SUB:
            wide[r : r + 1, RATE_COLS:TAP_COLS] = row
        else:
            wide[:, TAP_COLS:PARAM_COLS] = jnp.zeros((SUB, LANES), F32)
            for k in range(CHUNKS):
                wide[k : k + 1, TAP_COLS:PARAM_COLS] = row[:, k * LANES : (k + 1) * LANES]


def stack_kernel(*refs):
    params, coef = refs[-2:]
    for i in range(GROUP):
        params[i] = refs[i][:, 0:PARAM_COLS]
        for h in range(2):
            at = PARAM_COLS + h * WIDTH
            coef[i, h * HALF : (h + 1) * HALF, :] = refs[i][:, at : at + WIDTH]


def ends_kernel(
    scale, group, i, me, keyed, tail, params, ends, drive, last_s, taps_s, a_s, s_s
):
    rows = drive.shape[1] // SUB
    block = me[0] ^ (GROUP * i + group)
    column = pl.ds(pl.multiple_of(block * WIDTH, WIDTH), WIDTH)
    modes_out(a_s, jnp.exp(rates_of(params, i) * (-scale)))
    taps_out(taps_s, params, i, 0, CHUNKS)
    for branch, first in ((1, 0), (2, CHUNKS)):
        rows_out(last_s, tail[branch, :, column].astype(F32), first, SUB)
    a = registers(a_s, HALF)
    tap = [taps_s[pl.ds((3 * j + 1) * CHUNKS, SUB), :] for j in range(3)]

    def step(t0, carry):
        state, f1, f2 = carry
        state = list(state)
        for u in range(UNROLL):
            at = aligned((t0 * UNROLL + u) * SUB)
            f0 = keyed[block, at, :]
            filtered = tap[0] * f0 + tap[1] * f1 + tap[2] * f2
            now = filtered * pltpu.roll(filtered, CHUNKS, 0)
            drive[i, at, :] = now
            for j in range(HALF):
                state[j] = a[j] * state[j] + now
            f1, f2 = f0, f1
        return tuple(state), f1, f2

    start = ((jnp.zeros((SUB, LANES), F32),) * HALF, last_s[SUB : 2 * SUB, :], last_s[0:SUB, :])
    state = lax.fori_loop(0, rows // UNROLL, step, start)[0]
    for j in range(HALF):
        s_s[j * SUB : (j + 1) * SUB, :] = state[j]
    for h in range(2):
        for k in range(CHUNKS):
            ends[i, h * HALF : (h + 1) * HALF, k * LANES : (k + 1) * LANES] = s_s[
                pl.ds(h * CHUNKS + k, HALF, stride=SUB), :
            ]


def inner_kernel(
    scale, group, i, me, query, tail, params, coef, drive, packed, last_s, taps_s, a_s, c_s
):
    rows = drive.shape[1] // SUB
    block = me[0] ^ (GROUP * i + group)
    column = pl.ds(pl.multiple_of(block * WIDTH, WIDTH), WIDTH)
    modes_out(a_s, jnp.exp(rates_of(params, i) * (-scale)))
    modes_out(c_s, coef[i])
    for twice in range(2):
        taps_out(taps_s, params, i, twice * CHUNKS, SUB)
    rows_out(last_s, tail[0, :, column].astype(F32), 0, CHUNKS)
    a = registers(a_s, HALF)
    c = registers(c_s, HALF)
    tap = [taps_s[3 * j * SUB : (3 * j + 1) * SUB, :] for j in range(3)]
    upper = lax.broadcasted_iota(jnp.int32, (SUB, LANES), 0) >= CHUNKS

    def step(t0, carry):
        state, before = carry
        state = list(state)
        for u in range(0, UNROLL, 2):
            latest = query[block, aligned((t0 * UNROLL + u) * CHUNKS), :]
            middle = pltpu.roll(jnp.where(upper, before, latest), CHUNKS, 0)
            filtered = tap[0] * latest + tap[1] * middle + tap[2] * before
            before = latest
            for v, q in ((0, pltpu.roll(filtered, CHUNKS, 0)), (1, filtered)):
                at = aligned((t0 * UNROLL + u + v) * SUB)
                now = drive[i, at, :]
                for j in range(HALF):
                    state[j] = a[j] * state[j] + now
                y = total([x * s for x, s in zip(c, state)])
                packed[i, at, :] = jnp.where(upper, q, y + pltpu.roll(y, CHUNKS, 0))
        return tuple(state), before

    start = ((jnp.zeros((SUB, LANES), F32),) * HALF, last_s[0:SUB, :])
    lax.fori_loop(0, rows // UNROLL, step, start)


def finish_kernel(scale, group, i, me, packed, params, coef, incoming, *refs):
    out, a_s, p_s, y_s, held, sems = refs[-6:]
    rows = out.shape[0]
    decay = jnp.exp(rates_of(params, i) * (-scale))
    modes_out(a_s, decay)
    modes_out(p_s, coef[i] * decay * incoming[i])
    a = registers(a_s, HALF)

    def step(t0, p):
        p = list(p)
        for u in range(UNROLL):
            at = aligned((t0 * UNROLL + u) * SUB)
            z = packed[i, at, :]
            y = total(p)
            y = y + pltpu.roll(y, CHUNKS, 0)
            y_s[at, :] = (z + y) * pltpu.roll(z, CHUNKS, 0)
            p = [x * d for x, d in zip(p, a)]
        return tuple(p)

    lax.fori_loop(0, rows // UNROLL, step, tuple(registers(p_s, HALF)))
    for k in range(CHUNKS):
        held[i, :, k * LANES : (k + 1) * LANES] = y_s[pl.ds(k, rows, stride=SUB), :].astype(
            out.dtype
        )
    columns_home(group, i, me, out, held, sems).start()


def columns_home(group, i, me, out, held, sems):
    column = pl.ds(pl.multiple_of((me[0] ^ (GROUP * i + group)) * WIDTH, WIDTH), WIDTH)
    return pltpu.make_async_copy(held.at[i], out.at[:, column], sems.at[i])


def pieces(kernel, last, skip, *refs):
    refs = refs[:1] + refs[1 + skip :]

    def one(i, carry):
        kernel(i, *refs)
        return carry

    lax.fori_loop(0, GROUP, one, 0)
    if last is not None:
        for i in range(GROUP):
            last(i, refs[0], refs[-6], refs[-2], refs[-1]).wait()


def whole(inputs, outputs, scratch, more=(), smem=1, room=4):
    return dict(
        compiler_params=pltpu.CompilerParams(vmem_limit_bytes=room << 20),
        in_specs=[pl.BlockSpec(memory_space=pltpu.SMEM)] * smem + inputs,
        out_specs=outputs,
        scratch_shapes=[pltpu.VMEM((n, LANES), F32) for n in scratch] + list(more),
    )


def cost(rows, ops):
    work = GROUP * rows * SUB * LANES * ops
    return pl.CostEstimate(flops=work, bytes_accessed=work // 4, transcendentals=0)


ANYWHERE = pl.BlockSpec(memory_space=pl.ANY)


def stage_part(branches, feats, *earlier):
    rows, blocks = feats.shape[1], feats.shape[2] // WIDTH
    stride = CHUNKS * len(branches)
    return pl.pallas_call(
        functools.partial(stage_body, branches, stride),
        out_shape=(
            pltpu.VMEM((blocks, rows * stride, LANES), F32),
            pltpu.VMEM((SUB, LANES), F32),
        ),
        cost_estimate=cost(rows, 20 * len(branches)),
        name="stage_part",
        **whole(
            [pl.BlockSpec(memory_space=pltpu.HBM)] + [ANYWHERE] * len(earlier),
            [VMEM] * 2,
            (),
            (
                pltpu.VMEM((blocks, len(branches), rows, WIDTH), feats.dtype),
                pltpu.SemaphoreType.DMA((blocks, len(branches))),
            ),
            smem=0,
            room=8,
        ),
    )(feats, *earlier)


def pack_part(filters, residues, rates, scale):
    return pl.pallas_call(
        functools.partial(pack_kernel, scale),
        out_shape=pltpu.VMEM((SUB, PARAM_COLS + 2 * WIDTH), F32),
        grid=(1,),
        name="pack_part",
        compiler_params=pltpu.CompilerParams(vmem_limit_bytes=4 << 20),
    )(filters, residues, rates)


def stack_part(parts, *earlier):
    return pl.pallas_call(
        stack_kernel,
        out_shape=(
            pltpu.VMEM((GROUP, SUB, PARAM_COLS), F32),
            pltpu.VMEM((GROUP, MODES, WIDTH), F32),
        ),
        cost_estimate=pl.CostEstimate(flops=1 << 18, bytes_accessed=1 << 18, transcendentals=0),
        name="stack_part",
        **whole([VMEM] * GROUP + [ANYWHERE] * len(earlier), [VMEM] * 2, (), smem=0),
    )(*parts, *earlier)


def ends_part(group, me, keyed, tail, params, scale, *earlier):
    rows = keyed.shape[1] // SUB
    return pl.pallas_call(
        functools.partial(
            pieces, functools.partial(ends_kernel, scale, group), None, len(earlier)
        ),
        out_shape=(
            pltpu.VMEM((GROUP, MODES, WIDTH), F32),
            pltpu.VMEM((GROUP, rows * SUB, LANES), F32),
        ),
        cost_estimate=cost(rows, 24),
        name="ends_part",
        **whole(
            [ANYWHERE] * len(earlier) + [VMEM] * 3,
            [VMEM] * 2,
            (2 * SUB, TAPS * CHUNKS, HALF * SUB, HALF * SUB),
        ),
    )(me, *earlier, keyed, tail, params)


def inner_part(group, me, query, tail, params, coef, drive, scale):
    rows = drive.shape[1] // SUB
    return pl.pallas_call(
        functools.partial(pieces, functools.partial(inner_kernel, scale, group), None, 0),
        out_shape=pltpu.VMEM((GROUP, rows * SUB, LANES), F32),
        cost_estimate=cost(rows, 36),
        name="inner_part",
        **whole([VMEM] * 5, VMEM, (2 * CHUNKS, TAPS * SUB, HALF * SUB, HALF * SUB)),
    )(me, query, tail, params, coef, drive)


def finish_part(group, me, packed, params, coef, incoming, out, scale):
    rows = packed.shape[1] // SUB
    given = [] if out is None else [out]
    return pl.pallas_call(
        functools.partial(
            pieces,
            functools.partial(finish_kernel, scale, group),
            functools.partial(columns_home, group),
            0,
        ),
        out_shape=jax.ShapeDtypeStruct((rows, GROUPS * GROUP * WIDTH), jnp.bfloat16),
        cost_estimate=cost(rows, 20),
        name="finish_part",
        input_output_aliases={5: 0} if given else {},
        **whole(
            [VMEM] * 4 + [pl.BlockSpec(memory_space=pl.ANY)] * len(given),
            pl.BlockSpec(memory_space=pl.ANY),
            (HALF * SUB, HALF * SUB, rows * SUB),
            (
                pltpu.VMEM((GROUP, rows, WIDTH), jnp.bfloat16),
                pltpu.SemaphoreType.DMA((GROUP,)),
            ),
        ),
    )(me, packed, params, coef, incoming, *given)


CORE, Y, Z = 1, 2, 4


def swap(value, bit):
    size = lax.axis_size("ctx")
    return lax.ppermute(value, "ctx", [(i, i ^ bit) for i in range(size)])


def small(kernel, count, name, me, *args):
    return pl.pallas_call(
        kernel,
        out_shape=tuple(pltpu.VMEM((GROUP, MODES, WIDTH), F32) for _ in range(count)),
        cost_estimate=pl.CostEstimate(flops=1 << 18, bytes_accessed=1 << 18, transcendentals=0),
        name=name,
        **whole([VMEM] * len(args), [VMEM] * count, ()),
    )(me, *args)


def join_kernel(bit, span, flip, me, mine, theirs, params, low, both):
    later = (me[0] & bit) != 0
    for i in range(GROUP):
        m, t = mine[i], theirs[i ^ flip]
        decay = jnp.exp(rates_of(params, i) * (-span))
        first = jnp.where(later, t, m)
        low[i] = first
        both[i] = decay * first + jnp.where(later, m, t)


def turn_kernel(span, me, first, far, plane_low, core_low, params, row_out, mine, core_out):
    core, row = (me[0] & CORE) != 0, (me[0] & Y) != 0
    odd, high = (me[0] & Z) != 0, (me[0] & (2 * Z)) != 0
    for i in range(GROUP):
        rates = rates_of(params, i)
        reach = jnp.where(odd, jnp.exp(rates * (-4 * span)), 1.0)
        before = jnp.where(odd, first[i], 0.0) + jnp.where(high, reach * far[i ^ 2], 0.0)
        after = jnp.exp(rates * (-2 * span)) * before + plane_low[i]
        row_out[i] = jnp.where(row, before, after)
        before = jnp.where(row, after, before)
        after = jnp.exp(rates * (-span)) * before + core_low[i]
        core_out[i] = jnp.where(core, before, after)
        mine[i] = jnp.where(core, after, before)


def core_kernel(span, me, given, core_low, params, mine, core_out):
    core = (me[0] & CORE) != 0
    for i in range(GROUP):
        before = given[i]
        after = jnp.exp(rates_of(params, i) * (-span)) * before + core_low[i]
        core_out[i] = jnp.where(core, before, after)
        mine[i] = jnp.where(core, after, before)


def join(bit, span, flip, *args):
    return small(functools.partial(join_kernel, bit, span, flip), 2, "join", *args)


def after(value, *others):
    return lax.optimization_barrier((value,) + others)


def to_groups(value):
    pieces = value.reshape(value.shape[0], -1, WIDTH).transpose(1, 0, 2)
    return [pieces[g::GROUPS] for g in range(GROUPS)]


def by_owner(ends, rates_t, span):
    size = lax.axis_size("ctx")
    pieces = jnp.stack(ends, 1).reshape((-1,) + ends[0].shape[1:])
    blocks = pieces.transpose(1, 0, 2).reshape(MODES, size, -1).transpose(1, 0, 2)
    blocks = lax.all_to_all(blocks, "ctx", 0, 0, tiled=True)
    decay = jnp.exp(rates_t * (-span))

    def advance(carry, end):
        return decay * carry + end, carry

    before = lax.scan(advance, jnp.zeros_like(blocks[0]), blocks)[1]
    before = lax.all_to_all(before, "ctx", 0, 0, tiled=True)
    return to_groups(before.transpose(1, 0, 2).reshape(MODES, -1))


def by_gathers(feats, tail, short_filter, residues, rates, scale, span):
    rates_t = rates.T
    taps = short_filter.astype(F32).reshape(TAPS, -1)
    coef_t = (residues * jnp.sqrt(-jnp.expm1(-2.0 * rates * scale))).T
    named = jnp.concatenate([rates_t, taps, coef_t], 0)
    named = lax.all_gather(named, "ctx", axis=1, tiled=True)
    last = named[MODES + SUB].reshape(-1, CHUNKS, LANES)
    last = jnp.pad(last, ((0, 0), (0, SUB - CHUNKS), (0, 0)))
    named = named.reshape(named.shape[0], -1, WIDTH).transpose(1, 0, 2)
    parts = [named[:, k * SUB : (k + 1) * SUB] for k in range(3)]
    params = jnp.concatenate(parts + [last], 2)
    params = [params[g::GROUPS] for g in range(GROUPS)]
    coef = [named[g::GROUPS, MODES + TAPS :] for g in range(GROUPS)]
    base = jnp.zeros((1,), jnp.int32)
    keyed, query = stage_part((1, 2), feats)[0], stage_part((0,), feats)[0]
    groups = range(GROUPS)
    ends, drive = zip(*[ends_part(g, base, keyed, tail, params[g], scale) for g in groups])
    packed = [inner_part(g, base, query, tail, params[g], coef[g], drive[g], scale) for g in groups]
    incoming = by_owner(ends, rates_t, span)
    out = None
    for g in groups:
        out = finish_part(g, base, packed[g], params[g], coef[g], incoming[g], out, scale)
    return out


def per_device(features, short_filter, residues, rates):
    rows = features.shape[0]
    size = lax.axis_size("ctx")
    me = lax.axis_index("ctx").astype(jnp.int32)
    scale = 1.0 / (rows * size)
    feats = features.transpose(1, 0, 2)
    tail_rows = feats[:, -2:]
    tail = lax.ppermute(tail_rows, "ctx", [(i, i + 1) for i in range(size - 1)])
    rates_t = rates.T
    span = rows * scale
    swaps = rates.shape[0] == WIDTH and size == GROUP * GROUPS
    if not swaps:
        return by_gathers(feats, tail, short_filter, residues, rates, scale, span)

    base = me.reshape(1)
    wide = pack_part(short_filter, residues.T, rates_t, scale)
    near = [swap(wide, Z * k) for k in range(1, GROUP)]
    keyed, staged = stage_part((1, 2), feats, tail_rows, base)
    params, coef = ([x] for x in stack_part([wide] + near, staged, tail))
    params.append(swap(params[0], CORE))
    params.append(swap(params[0], Y))
    coef.append(swap(coef[0], CORE))
    query, staged = stage_part((0,), feats, params[0])
    ends, drive, packed = [None] * GROUPS, [None] * GROUPS, [None] * GROUPS

    def run_ends(g, *earlier):
        ends[g], drive[g] = ends_part(g, base, keyed, tail, params[g], scale, *earlier)

    def run_inner(g):
        packed[g] = inner_part(g, base, query, tail, params[g], coef[g], drive[g], scale)

    run_ends(1)
    from_1 = swap(ends[1], CORE)
    run_ends(0)
    params[2], ends[0], from_1, _ = after(params[2], ends[0], from_1, staged)
    params.append(swap(params[2], CORE))
    run_ends(2)
    low_z, chip_z = join(CORE, span, 0, base, ends[0], from_1, params[0])
    params[3], ends[2], chip_z = after(params[3], ends[2], chip_z)
    run_ends(3)
    from_3 = swap(ends[3], CORE)
    low_y, chip_y = join(CORE, span, 0, base, ends[2], from_3, params[2])
    from_y = swap(chip_y, Y)
    run_inner(0)
    from_y, packed[0], drive[1] = after(from_y, packed[0], drive[1])
    low, plane = join(Y, 2 * span, 0, base, chip_z, from_y, params[0])
    from_near = swap(plane, Z)
    coef.append(swap(coef[0], Y))
    run_inner(1)
    from_near, packed[1], coef[2] = after(from_near, packed[1], coef[2])
    first, pair = join(Z, 4 * span, 1, base, plane, from_near, params[0])
    from_far = swap(pair, 2 * Z)
    coef.append(swap(coef[2], CORE))
    run_inner(2)
    run_inner(3)
    from_far, packed[2], packed[3] = after(from_far, packed[2], packed[3])
    to_row, mine_z, to_core = small(
        functools.partial(turn_kernel, span),
        3,
        "turn",
        base,
        first,
        from_far,
        low,
        low_z,
        params[0],
    )
    from_row = swap(to_row, Y)
    core_z = swap(to_core, CORE)
    out = finish_part(0, base, packed[0], params[0], coef[0], mine_z, None, scale)
    out = finish_part(1, base, packed[1], params[1], coef[1], core_z, out, scale)
    from_row, out = after(from_row, out)
    mine_y, to_core = small(
        functools.partial(core_kernel, span), 2, "turn_core", base, from_row, low_y, params[2]
    )
    core_y = swap(to_core, CORE)
    out = finish_part(2, base, packed[2], params[2], coef[2], mine_y, out, scale)
    return finish_part(3, base, packed[3], params[3], coef[3], core_y, out, scale)


def solution(mesh):
    in_specs = (
        P(("groups", "ctx"), None, None),
        P(None, None, "ctx"),
        P("ctx", None),
        P("ctx", None),
    )
    out_specs = P(("groups", "ctx"), None)
    return jax.shard_map(
        per_device, mesh=mesh, in_specs=in_specs, out_specs=out_specs, check_vma=False
    )
```

time: 369 us -> 66.5 us (0.18)
  other arithmetic: 122 us -> 0.01 us
  blocking collectives: 90.2 us -> 0 us
  local copies, waits for them, and re-layouts: 87.5 us -> 6.12 us
  waiting for transfers between devices: 48.6 us -> 4.38 us
  Pallas kernels: 0 us -> 33.7 us
  starting transfers between devices: 4.54 us -> 21.6 us
  between operations: 14 us -> 0.24 us
    all_gather x3 -> x0, blocking collectives: 61.1 us -> none  [the longest x1 21.4 us: per_device(): lax.all_gather(short_filter.astype(jnp.float32), 'ctx', axis=2, tiled=True)]
    add x12 -> x0, other arithmetic: 53.6 us -> none  [the longest x1 26.4 us: modal_finish(): mixed = mixed + starts[:, mode][:, None, :] * reach[:, mode][None]]
    all_gather x1 -> x0, waiting for transfers between devices: 48.5 us -> none  [carried_in(): everything = jax.tree.map(lambda part: lax.all_gather(part, axis), value)]
    slice x12 -> x1, local copies, waits for them, and re-layouts: 45.8 us -> 1.1 us  [per_device(): tail_rows = feats[:, -2:]]
    pallas_call x0 -> x22, Pallas kernels: none -> 33.7 us  [the longest x4 11.6 us: inner_part(): pl.pallas_call(functools.partial(pieces, functools.partial(inner_kernel,...]
    unnamed x115 -> x12, local copies, waits for them, and re-layouts: 37.8 us -> 5.02 us
    select_n x16 -> x0, other arithmetic: 31.7 us -> none  [step(): return jax.tree.map(lambda a, b: jnp.where(reached, a, b), new, before)]
    unnamed x1 -> x0, blocking collectives: 29.2 us -> none
  transfers between devices with their start and end apart: 2 -> 18, of which waited for: 1 -> 6; matrix products, arithmetic and copies ran while one was open for 17% -> 0% of each run, Pallas kernels for 0% -> 44%
where the time goes in v2:
time: 66.5 us; the launch traced here: 66 us
  Pallas kernels  33.7 us (51%)
  starting transfers between devices  21.6 us (32%)
  local copies, waits for them, and re-layouts  6.12 us (9%)
  waiting for transfers between devices  4.38 us (7%)
    ppermute x17, starting transfers between devices, swap(): return lax.ppermute(value, 'ctx', [(i, i ^ bit) for i in range(size)])  17 us
    pallas_call x4, Pallas kernels, inner_part(): pl.pallas_call(functools.partial(pieces, functools.partial(inner_kernel,...  11.6 us
    pallas_call x4, Pallas kernels, finish_part(): pl.pallas_call(functools.partial(pieces, functools.partial(finish_kernel,...  10 us
    pallas_call x4, Pallas kernels, ends_part(): pl.pallas_call(functools.partial(pieces, functools.partial(ends_kernel, s...  7.39 us
    unnamed x12, local copies, waits for them, and re-layouts  5.02 us
    ppermute x1, starting transfers between devices, per_device(): tail = lax.ppermute(tail_rows, 'ctx', [(i, i + 1) for i in range(size - 1)])  4.54 us
    ppermute x17, waiting for transfers between devices, swap(): return lax.ppermute(value, 'ctx', [(i, i ^ bit) for i in range(size)])  4.38 us
    pallas_call x2, Pallas kernels, stage_part(): pl.pallas_call(functools.partial(stage_body, branches, stride), out_shape...  4.32 us
  transfers between devices with their start and end apart: 18, of which 6 were waited for; matrix products, arithmetic and copies ran while one was open for 0% of the time, Pallas kernels for 44%

profile of v2, /device:TPU:1, one launch (start us, length us, event | category | flops | bytes accessed | tf_op | source)
XLA Modules:
  0.0 66.0 jit_solution(16182331760249855658)
XLA Ops:
  1.1 4.5 %collective-permute-start.3 = (bf16[3,2,8192]{2,1,0:T(2,128)(2,1)S(1)}, bf16[3,2,8192]{2,1,0:T(2,128)(2,1)S(1)}, u32[]{:S(2)}, u32[]{:S(2)}) collective-permute-start(bf16[3,2,8192]{2,1,0:T(2,128)(2,1)S(1)} %slice.4.refs_0_), channel_id=1, source_target_pairs={{0,1},{1,2},{2,3},{3,4},{4,5},{5,6},{6,7},{7,8},{8,9},{9,10},{10,1... | collective-permute-start | bytes 294920 | tf_op jit(solution)/shard_map/ppermute | solution.py:461
  7.9 1.4 %collective-permute-start = (f32[8,2688]{1,0:T(8,128)S(1)}, f32[8,2688]{1,0:T(8,128)S(1)}, u32[]{:S(2)}, u32[]{:S(2)}) collective-permute-start(f32[8,2688]{1,0:T(8,128)S(1)} %pack_part.1.refs_0_), channel_id=1, source_target_pairs={{0,4},{1,5},{2,6},{3,7},{4,0},{5,1},{6,2},{7,3},{8,12},{9,13},{10,... | collective-permute-start | bytes 258056 | tf_op jit(solution)/shard_map/ppermute | solution.py:354
  9.3 2.3 %collective-permute-start.1 = (f32[8,2688]{1,0:T(8,128)S(1)}, f32[8,2688]{1,0:T(8,128)S(1)}, u32[]{:S(2)}, u32[]{:S(2)}) collective-permute-start(f32[8,2688]{1,0:T(8,128)S(1)} %pack_part.1.refs_0_), channel_id=1, source_target_pairs={{0,8},{1,9},{2,10},{3,11},{4,12},{5,13},{6,14},{7,15},{8,0},{9,1},... | collective-permute-start | bytes 258056 | tf_op jit(solution)/shard_map/ppermute | solution.py:354
  11.6 2.8 %copy-done = bf16[128,3,8192]{2,0,1:T(8,128)(2,1)S(1)} copy-done((bf16[128,3,8192]{2,0,1:T(8,128)(2,1)S(1)}, bf16[128,3,8192]{2,0,1:T(8,128)(2,1)}, u32[]{:S(2)}) %copy-start) | copy-done | bytes 6291480
  14.4 2.9 %stage_part.2 = (f32[16,1024,128]{2,1,0:T(8,128)S(1)}, f32[8,128]{1,0:T(8,128)S(1)}) custom-call(bf16[3,128,8192]{2,1,0:T(8,128)(2,1)S(1)} %bitcast.5, bf16[3,2,8192]{2,1,0:T(2,128)(2,1)S(1)} %slice.4.refs_0_, s32[1]{0:T(128)} %bitcast.refs_1_.refs_0_.me), custom_call_target="tpu_custom_call" | custom-call | flops 20971520 | bytes 5242880 | tf_op jit(solution)/shard_map/stage_part/pallas_call | solution.py:247
  18.2 1.2 %collective-permute-start.4 = (f32[4,8,1664]{2,1,0:T(8,128)S(1)}, f32[4,8,1664]{2,1,0:T(8,128)S(1)}, u32[]{:S(2)}, u32[]{:S(2)}) collective-permute-start(f32[4,8,1664]{2,1,0:T(8,128)S(1)} %get-tuple-element.49.refs_3_.params.refs_0_.refs_2_), channel_id=1, source_target_pairs={{0,2},{1,3},{2,0},{3,1},{4,6},{5,7},{6,4},{7,5},{8,10},{9,11},{10,... | collective-permute-start | bytes 638984 | tf_op jit(solution)/shard_map/ppermute | solution.py:354
  19.6 1.8 %ends_part.5 = (f32[4,16,512]{2,1,0:T(8,128)S(1)}, f32[4,1024,128]{2,1,0:T(8,128)S(1)}) custom-call(s32[1]{0:T(128)} %bitcast.refs_1_.refs_0_.me, f32[16,1024,128]{2,1,0:T(8,128)S(1)} %get-tuple-element.50.refs_1_, bf16[3,2,8192]{2,1,0:T(2,128)(2,1)S(1)} %collective-permute-done.3.refs_5_.refs_2_, f32[4,8,1664]{2,1,0:T(8,128)S(1)} %collective-permute-done.5.refs_3_.refs_2_), custom_call_target="tpu_custom_call" | custom-call | flops 12582912 | bytes 3145728 | tf_op jit(solution)/shard_map/ends_part/pallas_call | solution.py:294
  22.1 1.8 %ends_part.4 = (f32[4,16,512]{2,1,0:T(8,128)S(1)}, f32[4,1024,128]{2,1,0:T(8,128)S(1)}) custom-call(s32[1]{0:T(128)} %bitcast.refs_1_.refs_0_.me, f32[16,1024,128]{2,1,0:T(8,128)S(1)} %get-tuple-element.50.refs_1_, bf16[3,2,8192]{2,1,0:T(2,128)(2,1)S(1)} %collective-permute-done.3.refs_5_.refs_2_, ...), custom_call_target="tpu_custom_call" | custom-call | flops 12582912 | bytes 3145728 | tf_op jit(solution)/shard_map/ends_part/pallas_call | solution.py:294
  24.7 1.2 %collective-permute-start.7 = (f32[4,8,1664]{2,1,0:T(8,128)S(1)}, f32[4,8,1664]{2,1,0:T(8,128)S(1)}, u32[]{:S(2)}, u32[]{:S(2)}) collective-permute-start(f32[4,8,1664]{2,1,0:T(8,128)S(1)} %collective-permute-done.4.refs_3_.params.refs_2_), channel_id=1, source_target_pairs={{0,1},{1,0},{2,3},{3,2},{4,5},{5,4},{6,7},{7,6},{8,9},{9,8},{10,11... | collective-permute-start | bytes 638984 | tf_op jit(solution)/shard_map/ppermute | solution.py:354
  26.0 1.8 %ends_part.6 = (f32[4,16,512]{2,1,0:T(8,128)S(1)}, f32[4,1024,128]{2,1,0:T(8,128)S(1)}) custom-call(s32[1]{0:T(128)} %bitcast.refs_1_.refs_0_.me, f32[16,1024,128]{2,1,0:T(8,128)S(1)} %get-tuple-element.50.refs_1_, bf16[3,2,8192]{2,1,0:T(2,128)(2,1)S(1)} %collective-permute-done.3.refs_5_.refs_2_, f32[4,8,1664]{2,1,0:T(8,128)S(1)} %collective-permute-done.4.refs_3_.params.refs_2_), custom_call_target="tpu_custom_call" | custom-call | flops 12582912 | bytes 3145728 | tf_op jit(solution)/shard_map/ends_part/pallas_call | solution.py:294
  27.8 1.8 %ends_part.7 = (f32[4,16,512]{2,1,0:T(8,128)S(1)}, f32[4,1024,128]{2,1,0:T(8,128)S(1)}) custom-call(s32[1]{0:T(128)} %bitcast.refs_1_.refs_0_.me, f32[16,1024,128]{2,1,0:T(8,128)S(1)} %get-tuple-element.50.refs_1_, bf16[3,2,8192]{2,1,0:T(2,128)(2,1)S(1)} %collective-permute-done.3.refs_5_.refs_2_, f32[4,8,1664]{2,1,0:T(8,128)S(1)} %collective-permute-done.7.refs_3_.refs_2_), custom_call_target="tpu_custom_call" | custom-call | flops 12582912 | bytes 3145728 | tf_op jit(solution)/shard_map/ends_part/pallas_call | solution.py:294
  29.8 1.3 %collective-permute-done.8.theirs = f32[4,16,512]{2,1,0:T(8,128)S(1)} collective-permute-done((f32[4,16,512]{2,1,0:T(8,128)S(1)}, f32[4,16,512]{2,1,0:T(8,128)S(1)}, u32[]{:S(2)}, u32[]{:S(2)}) %collective-permute-start.8) | collective-permute-done | bytes 131104 | tf_op jit(solution)/shard_map/ppermute | solution.py:354
  31.2 1.3 %collective-permute-start.9 = (f32[4,16,512]{2,1,0:T(8,128)S(1)}, f32[4,16,512]{2,1,0:T(8,128)S(1)}, u32[]{:S(2)}, u32[]{:S(2)}) collective-permute-start(f32[4,16,512]{2,1,0:T(8,128)S(1)} %get-tuple-element.62), channel_id=1, source_target_pairs={{0,2},{1,3},{2,0},{3,1},{4,6},{5,7},{6,4},{7,5},{8,10},{9,11},{10,... | collective-permute-start | bytes 393224 | tf_op jit(solution)/shard_map/ppermute | solution.py:354
  33.1 1.4 %stage_part.3 = (f32[16,512,128]{2,1,0:T(8,128)S(1)}, f32[8,128]{1,0:T(8,128)}) custom-call(bf16[3,128,8192]{2,1,0:T(8,128)(2,1)S(1)} %bitcast.8, f32[4,8,1664]{2,1,0:T(8,128)S(1)} %get-tuple-element.49.refs_3_.params.refs_0_.refs_2_), custom_call_target="tpu_custom_call" | custom-call | flops 10485760 | bytes 2621440 | tf_op jit(solution)/shard_map/stage_part/pallas_call | solution.py:247
  34.6 2.9 %inner_part.4.refs_1_ = f32[4,1024,128]{2,1,0:T(8,128)S(1)} custom-call(s32[1]{0:T(128)} %bitcast.refs_1_.refs_0_.me, f32[16,512,128]{2,1,0:T(8,128)S(1)} %get-tuple-element.63.refs_1_, bf16[3,2,8192]{2,1,0:T(2,128)(2,1)S(1)} %collective-permute-done.3.refs_5_.refs_2_, f32[4,8,1664]{2,1,0:T(8,128)S(1)} %get-tuple-element.49.refs_3_.params.refs_0_.refs_2_, ...), custom_call_target="tpu_custom_call" | custom-call | flops 18874368 | bytes 4718592 | tf_op jit(solution)/shard_map/inner_part/pallas_call | solution.py:314
  37.6 2.2 %collective-permute-start.10 = (f32[4,16,512]{2,1,0:T(8,128)S(1)}, f32[4,16,512]{2,1,0:T(8,128)S(1)}, u32[]{:S(2)}, u32[]{:S(2)}) collective-permute-start(f32[4,16,512]{2,1,0:T(8,128)S(1)} %get-tuple-element.68.mine), channel_id=1, source_target_pairs={{0,4},{1,5},{2,6},{3,7},{4,0},{5,1},{6,2},{7,3},{8,12},{9,13},{10,... | collective-permute-start | bytes 393224 | tf_op jit(solution)/shard_map/ppermute | solution.py:354
  39.8 2.9 %inner_part.5.refs_1_ = f32[4,1024,128]{2,1,0:T(8,128)S(1)} custom-call(s32[1]{0:T(128)} %bitcast.refs_1_.refs_0_.me, f32[16,512,128]{2,1,0:T(8,128)S(1)} %get-tuple-element.63.refs_1_, bf16[3,2,8192]{2,1,0:T(2,128)(2,1)S(1)} %collective-permute-done.3.refs_5_.refs_2_, f32[4,8,1664]{2,1,0:T(8,128)S(1)} %collective-permute-done.5.refs_3_.refs_2_, ...), custom_call_target="tpu_custom_call" | custom-call | flops 18874368 | bytes 4718592 | tf_op jit(solution)/shard_map/inner_part/pallas_call | solution.py:314
  44.2 2.6 %collective-permute-start.13 = (f32[4,16,512]{2,1,0:T(8,128)S(1)}, f32[4,16,512]{2,1,0:T(8,128)S(1)}, u32[]{:S(2)}, u32[]{:S(2)}) collective-permute-start(f32[4,16,512]{2,1,0:T(8,128)S(1)} %get-tuple-element.71), channel_id=1, source_target_pairs={{0,8},{1,9},{2,10},{3,11},{4,12},{5,13},{6,14},{7,15},{8,0},{9,1},... | collective-permute-start | bytes 393224 | tf_op jit(solution)/shard_map/ppermute | solution.py:354
  46.8 2.9 %inner_part.6.refs_1_ = f32[4,1024,128]{2,1,0:T(8,128)S(1)} custom-call(s32[1]{0:T(128)} %bitcast.refs_1_.refs_0_.me, f32[16,512,128]{2,1,0:T(8,128)S(1)} %get-tuple-element.63.refs_1_, bf16[3,2,8192]{2,1,0:T(2,128)(2,1)S(1)} %collective-permute-done.3.refs_5_.refs_2_, f32[4,8,1664]{2,1,0:T(8,128)S(1)} %collective-permute-done.4.refs_3_.params.refs_2_, ...), custom_call_target="tpu_custom_call" | custom-call | flops 18874368 | bytes 4718592 | tf_op jit(solution)/shard_map/inner_part/pallas_call | solution.py:314
  49.8 2.9 %inner_part.7.refs_1_ = f32[4,1024,128]{2,1,0:T(8,128)S(1)} custom-call(s32[1]{0:T(128)} %bitcast.refs_1_.refs_0_.me, f32[16,512,128]{2,1,0:T(8,128)S(1)} %get-tuple-element.63.refs_1_, bf16[3,2,8192]{2,1,0:T(2,128)(2,1)S(1)} %collective-permute-done.3.refs_5_.refs_2_, f32[4,8,1664]{2,1,0:T(8,128)S(1)} %collective-permute-done.7.refs_3_.refs_2_, ...), custom_call_target="tpu_custom_call" | custom-call | flops 18874368 | bytes 4718592 | tf_op jit(solution)/shard_map/inner_part/pallas_call | solution.py:314
  55.5 2.5 %finish_part.4.refs_5_ = bf16[128,8192]{1,0:T(8,128)(2,1)} custom-call(s32[1]{0:T(128)} %bitcast.refs_1_.refs_0_.me, f32[4,1024,128]{2,1,0:T(8,128)S(1)} %inner_part.4.refs_1_, f32[4,8,1664]{2,1,0:T(8,128)S(1)} %get-tuple-element.49.refs_3_.params.refs_0_.refs_2_, f32[4,16,512]{2,1,0:T(8,128)S(1)} %get-tuple-element.64.refs_4_.refs_3_, ...), custom_call_target="tpu_custom_call" | custom-call | flops 10485760 | bytes 2621440 | tf_op jit(solution)/shard_map/finish_part/pallas_call | solution.py:326
  58.0 2.5 %finish_part.5.refs_5_ = bf16[128,8192]{1,0:T(8,128)(2,1)} custom-call(s32[1]{0:T(128)} %bitcast.refs_1_.refs_0_.me, f32[4,1024,128]{2,1,0:T(8,128)S(1)} %inner_part.5.refs_1_, f32[4,8,1664]{2,1,0:T(8,128)S(1)} %collective-permute-done.5.refs_3_.refs_2_, f32[4,16,512]{2,1,0:T(8,128)S(1)} %collective-permute-done.11.refs_4_.refs_3_, ...), custom_call_target="tpu_custom_call", output_to_operand_aliasing={{}: (5, {})} | custom-call | flops 10485760 | bytes 2621440 | tf_op jit(solution)/shard_map/finish_part/pallas_call | solution.py:326
  61.0 2.5 %finish_part.6.refs_5_ = bf16[128,8192]{1,0:T(8,128)(2,1)} custom-call(s32[1]{0:T(128)} %bitcast.refs_1_.refs_0_.me, f32[4,1024,128]{2,1,0:T(8,128)S(1)} %inner_part.6.refs_1_, f32[4,8,1664]{2,1,0:T(8,128)S(1)} %collective-permute-done.4.refs_3_.params.refs_2_, ...), custom_call_target="tpu_custom_call", output_to_operand_aliasing={{}: (5, {})} | custom-call | flops 10485760 | bytes 2621440 | tf_op jit(solution)/shard_map/finish_part/pallas_call | solution.py:326
  63.5 2.5 %finish_part.7 = bf16[128,8192]{1,0:T(8,128)(2,1)} custom-call(s32[1]{0:T(128)} %bitcast.refs_1_.refs_0_.me, f32[4,1024,128]{2,1,0:T(8,128)S(1)} %inner_part.7.refs_1_, f32[4,8,1664]{2,1,0:T(8,128)S(1)} %collective-permute-done.7.refs_3_.refs_2_, f32[4,16,512]{2,1,0:T(8,128)S(1)} %collective-permute-done.14.refs_4_.refs_3_, ...), custom_call_target="tpu_custom_call", output_to_operand_aliasing={{}: (5, {})} | custom-call | flops 10485760 | bytes 2621440 | tf_op jit(solution)/shard_map/finish_part/pallas_call | solution.py:326
  (48 shorter events, 11.5 us)
Async XLA Ops:
  1.1 16.9 %collective-permute-start.3 = (bf16[3,2,8192]{2,1,0:T(2,128)(2,1)S(1)}, bf16[3,2,8192]{2,1,0:T(2,128)(2,1)S(1)}, u32[]{:S(2)}, u32[]{:S(2)}) collective-permute-start(bf16[3,2,8192]{2,1,0:T(2,128)(2,1)S(1)} %slice.4.refs_0_), channel_id=1, source_target_pairs={{0,1},{1,2},{2,3},{3,4},{4,5},{5,6},{6,7},{7,8},{8,9},{9,10},{10,1... | collective-permute-start | bytes 294920 | tf_op jit(solution)/shard_map/ppermute | solution.py:461
  5.6 0.8 %copy-start.1 = (f32[512,16]{0,1:T(8,128)S(1)}, f32[512,16]{0,1:T(8,128)}, u32[]{:S(2)}) copy-start(f32[512,16]{0,1:T(8,128)} %param.6) | copy-start | bytes 98308
  6.4 0.8 %copy-start.2 = (f32[512,16]{0,1:T(8,128)S(1)}, f32[512,16]{0,1:T(8,128)}, u32[]{:S(2)}) copy-start(f32[512,16]{0,1:T(8,128)} %param.7) | copy-start | bytes 98308
  7.2 0.7 %copy-start.3 = (bf16[3,3,512]{2,1,0:T(4,128)(2,1)S(1)}, bf16[3,3,512]{2,1,0:T(4,128)(2,1)}, u32[]{:S(2)}) copy-start(bf16[3,3,512]{2,1,0:T(4,128)(2,1)} %filters.1) | copy-start | bytes 27652
  7.9 9.3 %collective-permute-start = (f32[8,2688]{1,0:T(8,128)S(1)}, f32[8,2688]{1,0:T(8,128)S(1)}, u32[]{:S(2)}, u32[]{:S(2)}) collective-permute-start(f32[8,2688]{1,0:T(8,128)S(1)} %pack_part.1.refs_0_), channel_id=1, source_target_pairs={{0,4},{1,5},{2,6},{3,7},{4,0},{5,1},{6,2},{7,3},{8,12},{9,13},{10,... | collective-permute-start | bytes 258056 | tf_op jit(solution)/shard_map/ppermute | solution.py:354
  9.3 8.8 %collective-permute-start.1 = (f32[8,2688]{1,0:T(8,128)S(1)}, f32[8,2688]{1,0:T(8,128)S(1)}, u32[]{:S(2)}, u32[]{:S(2)}) collective-permute-start(f32[8,2688]{1,0:T(8,128)S(1)} %pack_part.1.refs_0_), channel_id=1, source_target_pairs={{0,8},{1,9},{2,10},{3,11},{4,12},{5,13},{6,14},{7,15},{8,0},{9,1},... | collective-permute-start | bytes 258056 | tf_op jit(solution)/shard_map/ppermute | solution.py:354
  11.6 6.4 %collective-permute-start.2 = (f32[8,2688]{1,0:T(8,128)S(1)}, f32[8,2688]{1,0:T(8,128)S(1)}, u32[]{:S(2)}, u32[]{:S(2)}) collective-permute-start(f32[8,2688]{1,0:T(8,128)S(1)} %pack_part.1.refs_0_), channel_id=1, source_target_pairs={{0,12},{1,13},{2,14},{3,15},{4,8},{5,9},{6,10},{7,11},{8,4},{9,5},... | collective-permute-start | bytes 258056 | tf_op jit(solution)/shard_map/ppermute | solution.py:354
  11.6 2.8 %copy-start = (bf16[128,3,8192]{2,0,1:T(8,128)(2,1)S(1)}, bf16[128,3,8192]{2,0,1:T(8,128)(2,1)}, u32[]{:S(2)}) copy-start(bf16[128,3,8192]{2,0,1:T(8,128)(2,1)} %param.4) | copy-start | bytes 18874372
  18.1 1.5 %collective-permute-start.5 = (f32[4,8,1664]{2,1,0:T(8,128)S(1)}, f32[4,8,1664]{2,1,0:T(8,128)S(1)}, u32[]{:S(2)}, u32[]{:S(2)}) collective-permute-start(f32[4,8,1664]{2,1,0:T(8,128)S(1)} %get-tuple-element.49.refs_3_.params.refs_0_.refs_2_), channel_id=1, source_target_pairs={{0,1},{1,0},{2,3},{3,2},{4,5},{5,4},{6,7},{7,6},{8,9},{9,8},{10,11... | collective-permute-start | bytes 638984 | tf_op jit(solution)/shard_map/ppermute | solution.py:354
  18.2 6.4 %collective-permute-start.4 = (f32[4,8,1664]{2,1,0:T(8,128)S(1)}, f32[4,8,1664]{2,1,0:T(8,128)S(1)}, u32[]{:S(2)}, u32[]{:S(2)}) collective-permute-start(f32[4,8,1664]{2,1,0:T(8,128)S(1)} %get-tuple-element.49.refs_3_.params.refs_0_.refs_2_), channel_id=1, source_target_pairs={{0,2},{1,3},{2,0},{3,1},{4,6},{5,7},{6,4},{7,5},{8,10},{9,11},{10,... | collective-permute-start | bytes 638984 | tf_op jit(solution)/shard_map/ppermute | solution.py:354
  21.4 3.2 %collective-permute-start.6 = (f32[4,16,512]{2,1,0:T(8,128)S(1)}, f32[4,16,512]{2,1,0:T(8,128)S(1)}, u32[]{:S(2)}, u32[]{:S(2)}) collective-permute-start(f32[4,16,512]{2,1,0:T(8,128)S(1)} %get-tuple-element.52), channel_id=1, source_target_pairs={{0,1},{1,0},{2,3},{3,2},{4,5},{5,4},{6,7},{7,6},{8,9},{9,8},{10,11... | collective-permute-start | bytes 393224 | tf_op jit(solution)/shard_map/ppermute | solution.py:354
  24.7 3.1 %collective-permute-start.7 = (f32[4,8,1664]{2,1,0:T(8,128)S(1)}, f32[4,8,1664]{2,1,0:T(8,128)S(1)}, u32[]{:S(2)}, u32[]{:S(2)}) collective-permute-start(f32[4,8,1664]{2,1,0:T(8,128)S(1)} %collective-permute-done.4.refs_3_.params.refs_2_), channel_id=1, source_target_pairs={{0,1},{1,0},{2,3},{3,2},{4,5},{5,4},{6,7},{7,6},{8,9},{9,8},{10,11... | collective-permute-start | bytes 638984 | tf_op jit(solution)/shard_map/ppermute | solution.py:354
  25.9 7.2 %slice-start = ((s8[6291456]{0:T(1024)(128)(4,1)}), s8[4194304]{0:T(1024)(128)(4,1)S(1)}, s32[]{:S(2)}) async-start(s8[6291456]{0:T(1024)(128)(4,1)} %bitcast.6), calls=%async_computation | async-start | bytes 8388608
  27.8 5.3 %slice-start.1 = ((s8[6291456]{0:T(1024)(128)(4,1)}), s8[2097152]{0:T(1024)(128)(4,1)S(1)}, s32[]{:S(2)}) async-start(s8[6291456]{0:T(1024)(128)(4,1)} %bitcast.6), calls=%async_computation.1 | async-start | bytes 4194304
  29.7 1.4 %collective-permute-start.8 = (f32[4,16,512]{2,1,0:T(8,128)S(1)}, f32[4,16,512]{2,1,0:T(8,128)S(1)}, u32[]{:S(2)}, u32[]{:S(2)}) collective-permute-start(f32[4,16,512]{2,1,0:T(8,128)S(1)} %get-tuple-element.61), channel_id=1, source_target_pairs={{0,1},{1,0},{2,3},{3,2},{4,5},{5,4},{6,7},{7,6},{8,9},{9,8},{10,11... | collective-permute-start | bytes 393224 | tf_op jit(solution)/shard_map/ppermute | solution.py:354
  31.2 6.3 %collective-permute-start.9 = (f32[4,16,512]{2,1,0:T(8,128)S(1)}, f32[4,16,512]{2,1,0:T(8,128)S(1)}, u32[]{:S(2)}, u32[]{:S(2)}) collective-permute-start(f32[4,16,512]{2,1,0:T(8,128)S(1)} %get-tuple-element.62), channel_id=1, source_target_pairs={{0,2},{1,3},{2,0},{3,1},{4,6},{5,7},{6,4},{7,5},{8,10},{9,11},{10,... | collective-permute-start | bytes 393224 | tf_op jit(solution)/shard_map/ppermute | solution.py:354
  32.5 7.3 %collective-permute-start.11 = (f32[4,16,512]{2,1,0:T(8,128)S(1)}, f32[4,16,512]{2,1,0:T(8,128)S(1)}, u32[]{:S(2)}, u32[]{:S(2)}) collective-permute-start(f32[4,16,512]{2,1,0:T(8,128)S(1)} %get-tuple-element.64.refs_4_.refs_3_), channel_id=1, source_target_pairs={{0,1},{1,0},{2,3},{3,2},{4,5},{5,4},{6,7},{7,6},{8,9},{9,8},{10,11... | collective-permute-start | bytes 393224 | tf_op jit(solution)/shard_map/ppermute | solution.py:354
  32.9 9.8 %collective-permute-start.12 = (f32[4,16,512]{2,1,0:T(8,128)S(1)}, f32[4,16,512]{2,1,0:T(8,128)S(1)}, u32[]{:S(2)}, u32[]{:S(2)}) collective-permute-start(f32[4,16,512]{2,1,0:T(8,128)S(1)} %get-tuple-element.64.refs_4_.refs_3_), channel_id=1, source_target_pairs={{0,2},{1,3},{2,0},{3,1},{4,6},{5,7},{6,4},{7,5},{8,10},{9,11},{10,... | collective-permute-start | bytes 393224 | tf_op jit(solution)/shard_map/ppermute | solution.py:354
  37.6 5.8 %collective-permute-start.10 = (f32[4,16,512]{2,1,0:T(8,128)S(1)}, f32[4,16,512]{2,1,0:T(8,128)S(1)}, u32[]{:S(2)}, u32[]{:S(2)}) collective-permute-start(f32[4,16,512]{2,1,0:T(8,128)S(1)} %get-tuple-element.68.mine), channel_id=1, source_target_pairs={{0,4},{1,5},{2,6},{3,7},{4,0},{5,1},{6,2},{7,3},{8,12},{9,13},{10,... | collective-permute-start | bytes 393224 | tf_op jit(solution)/shard_map/ppermute | solution.py:354
  43.3 6.4 %collective-permute-start.14 = (f32[4,16,512]{2,1,0:T(8,128)S(1)}, f32[4,16,512]{2,1,0:T(8,128)S(1)}, u32[]{:S(2)}, u32[]{:S(2)}) collective-permute-start(f32[4,16,512]{2,1,0:T(8,128)S(1)} %collective-permute-done.12.refs_4_.refs_3_), channel_id=1, source_target_pairs={{0,1},{1,0},{2,3},{3,2},{4,5},{5,4},{6,7},{7,6},{8,9},{9,8},{10,11... | collective-permute-start | bytes 393224 | tf_op jit(solution)/shard_map/ppermute | solution.py:354
  44.2 9.1 %collective-permute-start.13 = (f32[4,16,512]{2,1,0:T(8,128)S(1)}, f32[4,16,512]{2,1,0:T(8,128)S(1)}, u32[]{:S(2)}, u32[]{:S(2)}) collective-permute-start(f32[4,16,512]{2,1,0:T(8,128)S(1)} %get-tuple-element.71), channel_id=1, source_target_pairs={{0,8},{1,9},{2,10},{3,11},{4,12},{5,13},{6,14},{7,15},{8,0},{9,1},... | collective-permute-start | bytes 393224 | tf_op jit(solution)/shard_map/ppermute | solution.py:354
  53.5 4.5 %collective-permute-start.16 = (f32[4,16,512]{2,1,0:T(8,128)S(1)}, f32[4,16,512]{2,1,0:T(8,128)S(1)}, u32[]{:S(2)}, u32[]{:S(2)}) collective-permute-start(f32[4,16,512]{2,1,0:T(8,128)S(1)} %get-tuple-element.82), channel_id=1, source_target_pairs={{0,1},{1,0},{2,3},{3,2},{4,5},{5,4},{6,7},{7,6},{8,9},{9,8},{10,11... | collective-permute-start | bytes 393224 | tf_op jit(solution)/shard_map/ppermute | solution.py:354
  54.3 6.3 %collective-permute-start.15 = (f32[4,16,512]{2,1,0:T(8,128)S(1)}, f32[4,16,512]{2,1,0:T(8,128)S(1)}, u32[]{:S(2)}, u32[]{:S(2)}) collective-permute-start(f32[4,16,512]{2,1,0:T(8,128)S(1)} %get-tuple-element.80), channel_id=1, source_target_pairs={{0,2},{1,3},{2,0},{3,1},{4,6},{5,7},{6,4},{7,5},{8,10},{9,11},{10,... | collective-permute-start | bytes 393224 | tf_op jit(solution)/shard_map/ppermute | solution.py:354
  60.6 2.9 %collective-permute-start.17 = (f32[4,16,512]{2,1,0:T(8,128)S(1)}, f32[4,16,512]{2,1,0:T(8,128)S(1)}, u32[]{:S(2)}, u32[]{:S(2)}) collective-permute-start(f32[4,16,512]{2,1,0:T(8,128)S(1)} %get-tuple-element.87), channel_id=1, source_target_pairs={{0,1},{1,0},{2,3},{3,2},{4,5},{5,4},{6,7},{7,6},{8,9},{9,8},{10,11... | collective-permute-start | bytes 393224 | tf_op jit(solution)/shard_map/ppermute | solution.py:354

commit v3 on v2

--- a/solution.py
+++ b/solution.py
@@ -18,7 +18,8 @@
 PARAM_COLS = TAP_COLS + LANES
 GROUP = 4
 GROUPS = 4
-UNROLL = 16
+UNROLL = 32
+HBM = pl.BlockSpec(memory_space=pltpu.HBM)
 F32 = jnp.float32
 VMEM = pl.BlockSpec(memory_space=pltpu.VMEM)
 
@@ -77,22 +78,43 @@
     done[...] = jnp.zeros_like(done)
 
 
-def pack_kernel(scale, filters, residues, rates, wide):
+def pack_kernel(scale, filters_in, residues_in, rates_in, wide, filters, residues, rates, sems):
+    copies = [
+        pltpu.make_async_copy(source, dest, sems.at[n])
+        for n, (source, dest) in enumerate(
+            ((rates_in, rates), (residues_in, residues), (filters_in, filters))
+        )
+    ]
+    for copy in copies:
+        copy.start()
+    copies[0].wait()
+    copies[1].wait()
     for h in range(2):
         part = slice(h * HALF, (h + 1) * HALF)
-        decayed = rates[part] * (2.0 * scale)
+        decayed = rates[part, :] * (2.0 * scale)
         power = jnp.tanh(0.5 * decayed) * (1.0 + jnp.exp(-decayed))
-        wide[:, h * WIDTH : (h + 1) * WIDTH] = rates[part]
+        wide[:, h * WIDTH : (h + 1) * WIDTH] = rates[part, :]
         at = PARAM_COLS + h * WIDTH
-        wide[:, at : at + WIDTH] = residues[part] * jnp.sqrt(power)
+        wide[:, at : at + WIDTH] = residues[part, :] * jnp.sqrt(power)
+    copies[2].wait()
+    wide[:, TAP_COLS:PARAM_COLS] = jnp.zeros((SUB, LANES), F32)
     for r in range(TAPS):
         row = filters[r // 3, r % 3 : r % 3 + 1, :].astype(F32)
         if r < SUB:
             wide[r : r + 1, RATE_COLS:TAP_COLS] = row
         else:
-            wide[:, TAP_COLS:PARAM_COLS] = jnp.zeros((SUB, LANES), F32)
             for k in range(CHUNKS):
                 wide[k : k + 1, TAP_COLS:PARAM_COLS] = row[:, k * LANES : (k + 1) * LANES]
+
+
+def tail_kernel(feats, *refs):
+    tail, last, sem = refs[-3:]
+    rows = feats.shape[1]
+    copy = pltpu.make_async_copy(feats.at[:, rows - SUB : rows, :], last, sem)
+    copy.start()
+    copy.wait()
+    for b in range(3):
+        tail[b] = last[b, SUB - 2 : SUB, :]
 
 
 def stack_kernel(*refs):
@@ -179,9 +201,8 @@
     lax.fori_loop(0, rows // UNROLL, step, start)
 
 
-def finish_kernel(scale, group, i, me, packed, params, coef, incoming, *refs):
-    out, a_s, p_s, y_s, held, sems = refs[-6:]
-    rows = out.shape[0]
+def finish_kernel(scale, i, params, packed, coef, incoming, held, a_s, p_s, y_s):
+    rows = held.shape[1]
     decay = jnp.exp(rates_of(params, i) * (-scale))
     modes_out(a_s, decay)
     modes_out(p_s, coef[i] * decay * incoming[i])
@@ -201,17 +222,38 @@
     lax.fori_loop(0, rows // UNROLL, step, tuple(registers(p_s, HALF)))
     for k in range(CHUNKS):
         held[i, :, k * LANES : (k + 1) * LANES] = y_s[pl.ds(k, rows, stride=SUB), :].astype(
-            out.dtype
+            held.dtype
         )
-    columns_home(group, i, me, out, held, sems).start()
-
-
-def columns_home(group, i, me, out, held, sems):
-    column = pl.ds(pl.multiple_of((me[0] ^ (GROUP * i + group)) * WIDTH, WIDTH), WIDTH)
-    return pltpu.make_async_copy(held.at[i], out.at[:, column], sems.at[i])
-
-
-def pieces(kernel, last, skip, *refs):
+
+
+def finish_body(scale, group, me, packed, params, coef, incoming, *refs):
+    final = group == GROUPS - 1
+    mine, a_s, p_s, y_s, sems = refs[-5:]
+    out = refs[-6] if group else None
+
+    def home(source, g, i, sem):
+        column = pl.ds(pl.multiple_of((me[0] ^ (GROUP * i + g)) * WIDTH, WIDTH), WIDTH)
+        return pltpu.make_async_copy(source.at[i], out.at[:, column], sems.at[sem, i])
+
+    if group:
+        for i in range(GROUP):
+            home(refs[0], group - 1, i, 0).start()
+
+    def one(i, carry):
+        finish_kernel(scale, i, params, packed, coef, incoming, mine, a_s, p_s, y_s)
+        if final:
+            home(mine, group, i, 1).start()
+        return carry
+
+    lax.fori_loop(0, GROUP, one, 0)
+    for i in range(GROUP):
+        if group:
+            home(refs[0], group - 1, i, 0).wait()
+        if final:
+            home(mine, group, i, 1).wait()
+
+
+def pieces(kernel, skip, *refs):
     refs = refs[:1] + refs[1 + skip :]
 
     def one(i, carry):
@@ -219,9 +261,6 @@
         return carry
 
     lax.fori_loop(0, GROUP, one, 0)
-    if last is not None:
-        for i in range(GROUP):
-            last(i, refs[0], refs[-6], refs[-2], refs[-1]).wait()
 
 
 def whole(inputs, outputs, scratch, more=(), smem=1, room=4):
@@ -253,7 +292,7 @@
         cost_estimate=cost(rows, 20 * len(branches)),
         name="stage_part",
         **whole(
-            [pl.BlockSpec(memory_space=pltpu.HBM)] + [ANYWHERE] * len(earlier),
+            [HBM] + [ANYWHERE] * len(earlier),
             [VMEM] * 2,
             (),
             (
@@ -263,17 +302,47 @@
             smem=0,
             room=8,
         ),
-    )(feats, *earlier)
+    )(in_hbm(feats), *earlier)
+
+
+def in_hbm(value):
+    return pltpu.with_memory_space_constraint(value, pltpu.HBM)
 
 
 def pack_part(filters, residues, rates, scale):
     return pl.pallas_call(
         functools.partial(pack_kernel, scale),
         out_shape=pltpu.VMEM((SUB, PARAM_COLS + 2 * WIDTH), F32),
-        grid=(1,),
         name="pack_part",
-        compiler_params=pltpu.CompilerParams(vmem_limit_bytes=4 << 20),
-    )(filters, residues, rates)
+        **whole(
+            [HBM] * 3,
+            VMEM,
+            (),
+            (
+                pltpu.VMEM(filters.shape, filters.dtype),
+                pltpu.VMEM((MODES, WIDTH), F32),
+                pltpu.VMEM((MODES, WIDTH), F32),
+                pltpu.SemaphoreType.DMA((3,)),
+            ),
+            smem=0,
+        ),
+    )(in_hbm(filters), in_hbm(residues), in_hbm(rates))
+
+
+def tail_part(feats, *earlier):
+    width = feats.shape[2]
+    return pl.pallas_call(
+        tail_kernel,
+        out_shape=pltpu.VMEM((3, 2, width), feats.dtype),
+        name="tail_part",
+        **whole(
+            [HBM] + [ANYWHERE] * len(earlier),
+            VMEM,
+            (),
+            (pltpu.VMEM((3, SUB, width), feats.dtype), pltpu.SemaphoreType.DMA),
+            smem=0,
+        ),
+    )(in_hbm(feats), *earlier)
 
 
 def stack_part(parts, *earlier):
@@ -293,7 +362,7 @@
     rows = keyed.shape[1] // SUB
     return pl.pallas_call(
         functools.partial(
-            pieces, functools.partial(ends_kernel, scale, group), None, len(earlier)
+            pieces, functools.partial(ends_kernel, scale, group), len(earlier)
         ),
         out_shape=(
             pltpu.VMEM((GROUP, MODES, WIDTH), F32),
@@ -312,7 +381,7 @@
 def inner_part(group, me, query, tail, params, coef, drive, scale):
     rows = drive.shape[1] // SUB
     return pl.pallas_call(
-        functools.partial(pieces, functools.partial(inner_kernel, scale, group), None, 0),
+        functools.partial(pieces, functools.partial(inner_kernel, scale, group), 0),
         out_shape=pltpu.VMEM((GROUP, rows * SUB, LANES), F32),
         cost_estimate=cost(rows, 36),
         name="inner_part",
@@ -320,30 +389,36 @@
     )(me, query, tail, params, coef, drive)
 
 
-def finish_part(group, me, packed, params, coef, incoming, out, scale):
-    rows = packed.shape[1] // SUB
-    given = [] if out is None else [out]
-    return pl.pallas_call(
-        functools.partial(
-            pieces,
-            functools.partial(finish_kernel, scale, group),
-            functools.partial(columns_home, group),
-            0,
-        ),
-        out_shape=jax.ShapeDtypeStruct((rows, GROUPS * GROUP * WIDTH), jnp.bfloat16),
+def finish_part(group, me, packed, params, coef, incoming, before, scale):
+    rows, width = packed.shape[1] // SUB, GROUPS * GROUP * WIDTH
+    final = group == GROUPS - 1
+    held = (GROUP, rows, WIDTH)
+    out_shape, out_specs, more = [], [], []
+    if group:
+        out_shape.append(jax.ShapeDtypeStruct((rows, width), jnp.bfloat16))
+        out_specs.append(ANYWHERE)
+    if final:
+        more.append(pltpu.VMEM(held, jnp.bfloat16))
+    else:
+        out_shape.append(pltpu.VMEM(held, jnp.bfloat16))
+        out_specs.append(VMEM)
+    given_specs = [VMEM, ANYWHERE][: len(before)]
+    spec = whole(
+        [VMEM] * 4 + given_specs,
+        out_specs,
+        (),
+        more
+        + [pltpu.VMEM((n, LANES), F32) for n in (HALF * SUB, HALF * SUB, rows * SUB)]
+        + [pltpu.SemaphoreType.DMA((2, GROUP))],
+    )
+    return pl.pallas_call(
+        functools.partial(finish_body, scale, group),
+        out_shape=out_shape,
         cost_estimate=cost(rows, 20),
         name="finish_part",
-        input_output_aliases={5: 0} if given else {},
-        **whole(
-            [VMEM] * 4 + [pl.BlockSpec(memory_space=pl.ANY)] * len(given),
-            pl.BlockSpec(memory_space=pl.ANY),
-            (HALF * SUB, HALF * SUB, rows * SUB),
-            (
-                pltpu.VMEM((GROUP, rows, WIDTH), jnp.bfloat16),
-                pltpu.SemaphoreType.DMA((GROUP,)),
-            ),
-        ),
-    )(me, packed, params, coef, incoming, *given)
+        input_output_aliases={6: 0} if len(before) > 1 else {},
+        **spec,
+    )(me, packed, params, coef, incoming, *before)
 
 
 CORE, Y, Z = 1, 2, 4
@@ -445,10 +520,10 @@
     ends, drive = zip(*[ends_part(g, base, keyed, tail, params[g], scale) for g in groups])
     packed = [inner_part(g, base, query, tail, params[g], coef[g], drive[g], scale) for g in groups]
     incoming = by_owner(ends, rates_t, span)
-    out = None
+    done = ()
     for g in groups:
-        out = finish_part(g, base, packed[g], params[g], coef[g], incoming[g], out, scale)
-    return out
+        done = finish_part(g, base, packed[g], params[g], coef[g], incoming[g], done[::-1], scale)
+    return done[0]
 
 
 def per_device(features, short_filter, residues, rates):
@@ -457,23 +532,23 @@
     me = lax.axis_index("ctx").astype(jnp.int32)
     scale = 1.0 / (rows * size)
     feats = features.transpose(1, 0, 2)
-    tail_rows = feats[:, -2:]
-    tail = lax.ppermute(tail_rows, "ctx", [(i, i + 1) for i in range(size - 1)])
-    rates_t = rates.T
+    onward = [(i, i + 1) for i in range(size - 1)]
     span = rows * scale
-    swaps = rates.shape[0] == WIDTH and size == GROUP * GROUPS
-    if not swaps:
+    if rates.shape[0] != WIDTH or size != GROUP * GROUPS:
+        tail = lax.ppermute(feats[:, -2:], "ctx", onward)
         return by_gathers(feats, tail, short_filter, residues, rates, scale, span)
 
     base = me.reshape(1)
-    wide = pack_part(short_filter, residues.T, rates_t, scale)
+    wide = pack_part(short_filter, residues.T, rates.T, scale)
     near = [swap(wide, Z * k) for k in range(1, GROUP)]
-    keyed, staged = stage_part((1, 2), feats, tail_rows, base)
-    params, coef = ([x] for x in stack_part([wide] + near, staged, tail))
+    keyed, staged = stage_part((1, 2), feats, wide, base)
+    tail_rows = tail_part(feats, staged)
+    params, coef = ([x] for x in stack_part([wide] + near, tail_rows))
     params.append(swap(params[0], CORE))
     params.append(swap(params[0], Y))
+    query, staged = stage_part((0,), feats, params[0])
+    tail = lax.ppermute(tail_rows, "ctx", onward)
     coef.append(swap(coef[0], CORE))
-    query, staged = stage_part((0,), feats, params[0])
     ends, drive, packed = [None] * GROUPS, [None] * GROUPS, [None] * GROUPS
 
     def run_ends(g, *earlier):
@@ -482,10 +557,10 @@
     def run_inner(g):
         packed[g] = inner_part(g, base, query, tail, params[g], coef[g], drive[g], scale)
 
-    run_ends(1)
+    run_ends(1, staged)
     from_1 = swap(ends[1], CORE)
     run_ends(0)
-    params[2], ends[0], from_1, _ = after(params[2], ends[0], from_1, staged)
+    params[2], ends[0], from_1 = after(params[2], ends[0], from_1)
     params.append(swap(params[2], CORE))
     run_ends(2)
     low_z, chip_z = join(CORE, span, 0, base, ends[0], from_1, params[0])
@@ -520,15 +595,15 @@
     )
     from_row = swap(to_row, Y)
     core_z = swap(to_core, CORE)
-    out = finish_part(0, base, packed[0], params[0], coef[0], mine_z, None, scale)
-    out = finish_part(1, base, packed[1], params[1], coef[1], core_z, out, scale)
-    from_row, out = after(from_row, out)
+    done = finish_part(0, base, packed[0], params[0], coef[0], mine_z, (), scale)
+    done = finish_part(1, base, packed[1], params[1], coef[1], core_z, done[::-1], scale)
+    from_row, held = after(from_row, done[1])
     mine_y, to_core = small(
         functools.partial(core_kernel, span), 2, "turn_core", base, from_row, low_y, params[2]
     )
     core_y = swap(to_core, CORE)
-    out = finish_part(2, base, packed[2], params[2], coef[2], mine_y, out, scale)
-    return finish_part(3, base, packed[3], params[3], coef[3], core_y, out, scale)
+    done = finish_part(2, base, packed[2], params[2], coef[2], mine_y, (held, done[0]), scale)
+    return finish_part(3, base, packed[3], params[3], coef[3], core_y, done[::-1], scale)[0]
 
 
 def solution(mesh):

time: 66.5 us -> 62.1 us (0.934)
  local copies, waits for them, and re-layouts: 6.12 us -> 0 us
  starting transfers between devices: 21.6 us -> 23.2 us
    unnamed x12 -> x0, local copies, waits for them, and re-layouts: 5.02 us -> none
    ppermute x17, starting transfers between devices: 17 us -> 20.2 us  [swap(): return lax.ppermute(value, 'ctx', [(i, i ^ bit) for i in range(size)])]
    ppermute x1, starting transfers between devices: 4.54 us -> 3.05 us  [per_device(): tail = lax.ppermute(tail_rows, 'ctx', onward)]
    slice x1 -> x0, local copies, waits for them, and re-layouts: 1.1 us -> none  [per_device(): tail_rows = feats[:, -2:]]
    pallas_call x4 -> x5, Pallas kernels: 10 us -> 8.99 us  [the longest x4 7.93 us: finish_part(): pl.pallas_call(functools.partial(finish_body, scale, group), out_shape=ou...]
    pallas_call x1, Pallas kernels: 0.03 us -> 0.84 us  [pack_part(): pl.pallas_call(functools.partial(pack_kernel, scale), out_shape=pltpu.VME...]
  transfers between devices with their start and end apart: 18 -> 18, of which waited for: 6 -> 6; matrix products, arithmetic and copies ran while one was open for 0% -> 0% of each run, Pallas kernels for 44% -> 45%
where the time goes in v3:
time: 62.1 us; the launch traced here: 61.8 us
  Pallas kernels  33.4 us (54%)
  starting transfers between devices  23.2 us (37%)
  waiting for transfers between devices  4.93 us (8%)
    ppermute x17, starting transfers between devices, swap(): return lax.ppermute(value, 'ctx', [(i, i ^ bit) for i in range(size)])  20.2 us
    pallas_call x4, Pallas kernels, inner_part(): pl.pallas_call(functools.partial(pieces, functools.partial(inner_kernel,...  11.2 us
    pallas_call x4, Pallas kernels, finish_part(): pl.pallas_call(functools.partial(finish_body, scale, group), out_shape=ou...  7.93 us
    pallas_call x4, Pallas kernels, ends_part(): pl.pallas_call(functools.partial(pieces, functools.partial(ends_kernel, s...  7.13 us
    pallas_call x2, Pallas kernels, stage_part(): pl.pallas_call(functools.partial(stage_body, branches, stride), out_shape...  4.96 us
    ppermute x17, waiting for transfers between devices, swap(): return lax.ppermute(value, 'ctx', [(i, i ^ bit) for i in range(size)])  4.93 us
    ppermute x1, starting transfers between devices, per_device(): tail = lax.ppermute(tail_rows, 'ctx', onward)  3.05 us
  transfers between devices with their start and end apart: 18, of which 6 were waited for; matrix products, arithmetic and copies ran while one was open for 0% of the time, Pallas kernels for 45%

profile of v3, /device:TPU:1, one launch (start us, length us, event | category | flops | bytes accessed | tf_op | source)
XLA Modules:
  0.0 61.8 jit_solution(9889560855284492181)
XLA Ops:
  0.8 2.2 %collective-permute-start = (f32[8,2688]{1,0:T(8,128)S(1)}, f32[8,2688]{1,0:T(8,128)S(1)}, u32[]{:S(2)}, u32[]{:S(2)}) collective-permute-start(f32[8,2688]{1,0:T(8,128)S(1)} %pack_part.1.refs_0_), channel_id=1, source_target_pairs={{0,4},{1,5},{2,6},{3,7},{4,0},{5,1},{6,2},{7,3},{8,12},{9,13},{10,... | collective-permute-start | bytes 258056 | tf_op jit(solution)/shard_map/ppermute | solution.py:429
  3.0 2.3 %collective-permute-start.1 = (f32[8,2688]{1,0:T(8,128)S(1)}, f32[8,2688]{1,0:T(8,128)S(1)}, u32[]{:S(2)}, u32[]{:S(2)}) collective-permute-start(f32[8,2688]{1,0:T(8,128)S(1)} %pack_part.1.refs_0_), channel_id=1, source_target_pairs={{0,8},{1,9},{2,10},{3,11},{4,12},{5,13},{6,14},{7,15},{8,0},{9,1},... | collective-permute-start | bytes 258056 | tf_op jit(solution)/shard_map/ppermute | solution.py:429
  5.4 3.2 %stage_part.2 = (f32[16,1024,128]{2,1,0:T(8,128)S(1)}, f32[8,128]{1,0:T(8,128)S(1)}) custom-call(bf16[3,128,8192]{2,1,0:T(8,128)(2,1)} %bitcast.4, f32[8,2688]{1,0:T(8,128)S(1)} %pack_part.1.refs_0_, s32[1]{0:T(128)} %bitcast.refs_1_.refs_0_.me), custom_call_target="tpu_custom_call" | custom-call | flops 20971520 | bytes 5242880 | tf_op jit(solution)/shard_map/stage_part/pallas_call | solution.py:286
  10.8 2.8 %collective-permute-start.5 = (f32[4,8,1664]{2,1,0:T(8,128)S(1)}, f32[4,8,1664]{2,1,0:T(8,128)S(1)}, u32[]{:S(2)}, u32[]{:S(2)}) collective-permute-start(f32[4,8,1664]{2,1,0:T(8,128)S(1)} %get-tuple-element.54.refs_3_.refs_0_.params), channel_id=1, source_target_pairs={{0,1},{1,0},{2,3},{3,2},{4,5},{5,4},{6,7},{7,6},{8,9},{9,8},{10,11... | collective-permute-start | bytes 638984 | tf_op jit(solution)/shard_map/ppermute | solution.py:429
  13.6 3.0 %collective-permute-start.4 = (bf16[3,2,8192]{2,1,0:T(2,128)(2,1)S(1)}, bf16[3,2,8192]{2,1,0:T(2,128)(2,1)S(1)}, u32[]{:S(2)}, u32[]{:S(2)}) collective-permute-start(bf16[3,2,8192]{2,1,0:T(2,128)(2,1)S(1)} %tail_part.1.refs_4_), channel_id=1, source_target_pairs={{0,1},{1,2},{2,3},{3,4},{4,5},{5,6},{6,7},{7,8},{8,9},{9,10},{10,1... | collective-permute-start | bytes 294920 | tf_op jit(solution)/shard_map/ppermute | solution.py:550
  16.6 1.2 %collective-permute-start.3 = (f32[4,8,1664]{2,1,0:T(8,128)S(1)}, f32[4,8,1664]{2,1,0:T(8,128)S(1)}, u32[]{:S(2)}, u32[]{:S(2)}) collective-permute-start(f32[4,8,1664]{2,1,0:T(8,128)S(1)} %get-tuple-element.54.refs_3_.refs_0_.params), channel_id=1, source_target_pairs={{0,2},{1,3},{2,0},{3,1},{4,6},{5,7},{6,4},{7,5},{8,10},{9,11},{10,... | collective-permute-start | bytes 638984 | tf_op jit(solution)/shard_map/ppermute | solution.py:429
  17.9 1.8 %stage_part.3 = (f32[16,512,128]{2,1,0:T(8,128)S(1)}, f32[8,128]{1,0:T(8,128)S(1)}) custom-call(bf16[3,128,8192]{2,1,0:T(8,128)(2,1)} %bitcast.6, f32[4,8,1664]{2,1,0:T(8,128)S(1)} %get-tuple-element.54.refs_3_.refs_0_.params), custom_call_target="tpu_custom_call" | custom-call | flops 10485760 | bytes 2621440 | tf_op jit(solution)/shard_map/stage_part/pallas_call | solution.py:286
  19.7 1.8 %ends_part.5 = (f32[4,16,512]{2,1,0:T(8,128)S(1)}, f32[4,1024,128]{2,1,0:T(8,128)S(1)}) custom-call(s32[1]{0:T(128)} %bitcast.refs_1_.refs_0_.me, f32[8,128]{1,0:T(8,128)S(1)} %get-tuple-element.57.refs_1_, f32[16,1024,128]{2,1,0:T(8,128)S(1)} %get-tuple-element.55.refs_1_.refs_2_, bf16[3,2,8192]{2,1,0:T(2,128)(2,1)S(1)} %collective-permute-done.4.refs_2_.refs_3_, ...), custom_call_target="tpu_custom_call" | custom-call | flops 12582912 | bytes 3145728 | tf_op jit(solution)/shard_map/ends_part/pallas_call | solution.py:363
  21.5 1.8 %ends_part.4 = (f32[4,16,512]{2,1,0:T(8,128)S(1)}, f32[4,1024,128]{2,1,0:T(8,128)S(1)}) custom-call(s32[1]{0:T(128)} %bitcast.refs_1_.refs_0_.me, f32[16,1024,128]{2,1,0:T(8,128)S(1)} %get-tuple-element.55.refs_1_.refs_2_, bf16[3,2,8192]{2,1,0:T(2,128)(2,1)S(1)} %collective-permute-done.4.refs_2_.refs_3_, ...), custom_call_target="tpu_custom_call" | custom-call | flops 12582912 | bytes 3145728 | tf_op jit(solution)/shard_map/ends_part/pallas_call | solution.py:363
  24.1 1.8 %ends_part.6 = (f32[4,16,512]{2,1,0:T(8,128)S(1)}, f32[4,1024,128]{2,1,0:T(8,128)S(1)}) custom-call(s32[1]{0:T(128)} %bitcast.refs_1_.refs_0_.me, f32[16,1024,128]{2,1,0:T(8,128)S(1)} %get-tuple-element.55.refs_1_.refs_2_, bf16[3,2,8192]{2,1,0:T(2,128)(2,1)S(1)} %collective-permute-done.4.refs_2_.refs_3_, f32[4,8,1664]{2,1,0:T(8,128)S(1)} %collective-permute-done.3.refs_3_.params), custom_call_target="tpu_custom_call" | custom-call | flops 12582912 | bytes 3145728 | tf_op jit(solution)/shard_map/ends_part/pallas_call | solution.py:363
  25.9 1.8 %ends_part.7 = (f32[4,16,512]{2,1,0:T(8,128)S(1)}, f32[4,1024,128]{2,1,0:T(8,128)S(1)}) custom-call(s32[1]{0:T(128)} %bitcast.refs_1_.refs_0_.me, f32[16,1024,128]{2,1,0:T(8,128)S(1)} %get-tuple-element.55.refs_1_.refs_2_, bf16[3,2,8192]{2,1,0:T(2,128)(2,1)S(1)} %collective-permute-done.4.refs_2_.refs_3_, f32[4,8,1664]{2,1,0:T(8,128)S(1)} %collective-permute-done.7.refs_3_.params), custom_call_target="tpu_custom_call" | custom-call | flops 12582912 | bytes 3145728 | tf_op jit(solution)/shard_map/ends_part/pallas_call | solution.py:363
  27.8 1.2 %collective-permute-done.8.theirs = f32[4,16,512]{2,1,0:T(8,128)S(1)} collective-permute-done((f32[4,16,512]{2,1,0:T(8,128)S(1)}, f32[4,16,512]{2,1,0:T(8,128)S(1)}, u32[]{:S(2)}, u32[]{:S(2)}) %collective-permute-start.8) | collective-permute-done | bytes 131104 | tf_op jit(solution)/shard_map/ppermute | solution.py:429
  29.1 1.4 %collective-permute-start.9 = (f32[4,16,512]{2,1,0:T(8,128)S(1)}, f32[4,16,512]{2,1,0:T(8,128)S(1)}, u32[]{:S(2)}, u32[]{:S(2)}) collective-permute-start(f32[4,16,512]{2,1,0:T(8,128)S(1)} %get-tuple-element.68), channel_id=1, source_target_pairs={{0,2},{1,3},{2,0},{3,1},{4,6},{5,7},{6,4},{7,5},{8,10},{9,11},{10,... | collective-permute-start | bytes 393224 | tf_op jit(solution)/shard_map/ppermute | solution.py:429
  31.1 2.8 %inner_part.4.packed = f32[4,1024,128]{2,1,0:T(8,128)S(1)} custom-call(s32[1]{0:T(128)} %bitcast.refs_1_.refs_0_.me, f32[16,512,128]{2,1,0:T(8,128)S(1)} %get-tuple-element.69.refs_1_, bf16[3,2,8192]{2,1,0:T(2,128)(2,1)S(1)} %collective-permute-done.4.refs_2_.refs_3_, f32[4,8,1664]{2,1,0:T(8,128)S(1)} %get-tuple-element.54.refs_3_.refs_0_.params, ...), custom_call_target="tpu_custom_call" | custom-call | flops 18874368 | bytes 4718592 | tf_op jit(solution)/shard_map/inner_part/pallas_call | solution.py:383
  34.2 2.2 %collective-permute-start.10 = (f32[4,16,512]{2,1,0:T(8,128)S(1)}, f32[4,16,512]{2,1,0:T(8,128)S(1)}, u32[]{:S(2)}, u32[]{:S(2)}) collective-permute-start(f32[4,16,512]{2,1,0:T(8,128)S(1)} %get-tuple-element.74.mine), channel_id=1, source_target_pairs={{0,4},{1,5},{2,6},{3,7},{4,0},{5,1},{6,2},{7,3},{8,12},{9,13},{10,... | collective-permute-start | bytes 393224 | tf_op jit(solution)/shard_map/ppermute | solution.py:429
  36.4 2.8 %inner_part.5.packed = f32[4,1024,128]{2,1,0:T(8,128)S(1)} custom-call(s32[1]{0:T(128)} %bitcast.refs_1_.refs_0_.me, f32[16,512,128]{2,1,0:T(8,128)S(1)} %get-tuple-element.69.refs_1_, bf16[3,2,8192]{2,1,0:T(2,128)(2,1)S(1)} %collective-permute-done.4.refs_2_.refs_3_, f32[4,8,1664]{2,1,0:T(8,128)S(1)} %collective-permute-done.5.refs_4_.refs_3_.params, ...), custom_call_target="tpu_custom_call" | custom-call | flops 18874368 | bytes 4718592 | tf_op jit(solution)/shard_map/inner_part/pallas_call | solution.py:383
  39.2 1.9 %collective-permute-start.14 = (f32[4,16,512]{2,1,0:T(8,128)S(1)}, f32[4,16,512]{2,1,0:T(8,128)S(1)}, u32[]{:S(2)}, u32[]{:S(2)}) collective-permute-start(f32[4,16,512]{2,1,0:T(8,128)S(1)} %collective-permute-done.12.refs_4_.coef), channel_id=1, source_target_pairs={{0,1},{1,0},{2,3},{3,2},{4,5},{5,4},{6,7},{7,6},{8,9},{9,8},{10,11... | collective-permute-start | bytes 393224 | tf_op jit(solution)/shard_map/ppermute | solution.py:429
  41.2 2.8 %collective-permute-start.13 = (f32[4,16,512]{2,1,0:T(8,128)S(1)}, f32[4,16,512]{2,1,0:T(8,128)S(1)}, u32[]{:S(2)}, u32[]{:S(2)}) collective-permute-start(f32[4,16,512]{2,1,0:T(8,128)S(1)} %get-tuple-element.77), channel_id=1, source_target_pairs={{0,8},{1,9},{2,10},{3,11},{4,12},{5,13},{6,14},{7,15},{8,0},{9,1},... | collective-permute-start | bytes 393224 | tf_op jit(solution)/shard_map/ppermute | solution.py:429
  44.0 2.8 %inner_part.6.packed = f32[4,1024,128]{2,1,0:T(8,128)S(1)} custom-call(s32[1]{0:T(128)} %bitcast.refs_1_.refs_0_.me, f32[16,512,128]{2,1,0:T(8,128)S(1)} %get-tuple-element.69.refs_1_, bf16[3,2,8192]{2,1,0:T(2,128)(2,1)S(1)} %collective-permute-done.4.refs_2_.refs_3_, f32[4,8,1664]{2,1,0:T(8,128)S(1)} %collective-permute-done.3.refs_3_.params, ...), custom_call_target="tpu_custom_call" | custom-call | flops 18874368 | bytes 4718592 | tf_op jit(solution)/shard_map/inner_part/pallas_call | solution.py:383
  46.8 2.8 %inner_part.7.packed = f32[4,1024,128]{2,1,0:T(8,128)S(1)} custom-call(s32[1]{0:T(128)} %bitcast.refs_1_.refs_0_.me, f32[16,512,128]{2,1,0:T(8,128)S(1)} %get-tuple-element.69.refs_1_, bf16[3,2,8192]{2,1,0:T(2,128)(2,1)S(1)} %collective-permute-done.4.refs_2_.refs_3_, f32[4,8,1664]{2,1,0:T(8,128)S(1)} %collective-permute-done.7.refs_3_.params, ...), custom_call_target="tpu_custom_call" | custom-call | flops 18874368 | bytes 4718592 | tf_op jit(solution)/shard_map/inner_part/pallas_call | solution.py:383
  52.0 1.8 %finish_part.4.refs_0_ = bf16[4,128,512]{2,1,0:T(8,128)(2,1)S(1)} custom-call(s32[1]{0:T(128)} %bitcast.refs_1_.refs_0_.me, f32[4,1024,128]{2,1,0:T(8,128)S(1)} %inner_part.4.packed, f32[4,8,1664]{2,1,0:T(8,128)S(1)} %get-tuple-element.54.refs_3_.refs_0_.params, f32[4,16,512]{2,1,0:T(8,128)S(1)} %get-tuple-element.70.refs_4_.coef, ...), custom_call_target="tpu_custom_call" | custom-call | flops 10485760 | bytes 2621440 | tf_op jit(solution)/shard_map/finish_part/pallas_call | solution.py:414
  53.8 1.8 %finish_part.5 = (bf16[128,8192]{1,0:T(8,128)(2,1)}, bf16[4,128,512]{2,1,0:T(8,128)(2,1)S(1)}) custom-call(s32[1]{0:T(128)} %bitcast.refs_1_.refs_0_.me, f32[4,1024,128]{2,1,0:T(8,128)S(1)} %inner_part.5.packed, f32[4,8,1664]{2,1,0:T(8,128)S(1)} %collective-permute-done.5.refs_4_.refs_3_.params, f32[4,16,512]{2,1,0:T(8,128)S(1)} %collective-permute-done.11.refs_4_.coef, ...), custom_call_target="tpu_custom_call" | custom-call | flops 10485760 | bytes 2621440 | tf_op jit(solution)/shard_map/finish_part/pallas_call | solution.py:414
  57.5 1.8 %finish_part.6 = (bf16[128,8192]{1,0:T(8,128)(2,1)}, bf16[4,128,512]{2,1,0:T(8,128)(2,1)S(1)}) custom-call(s32[1]{0:T(128)} %bitcast.refs_1_.refs_0_.me, f32[4,1024,128]{2,1,0:T(8,128)S(1)} %inner_part.6.packed, f32[4,8,1664]{2,1,0:T(8,128)S(1)} %collective-permute-done.3.refs_3_.params, ...), custom_call_target="tpu_custom_call", output_to_operand_aliasing={{0}: (6, {})} | custom-call | flops 10485760 | bytes 2621440 | tf_op jit(solution)/shard_map/finish_part/pallas_call | solution.py:414
  59.3 2.5 %finish_part.7 = bf16[128,8192]{1,0:T(8,128)(2,1)} custom-call(s32[1]{0:T(128)} %bitcast.refs_1_.refs_0_.me, f32[4,1024,128]{2,1,0:T(8,128)S(1)} %inner_part.7.packed, f32[4,8,1664]{2,1,0:T(8,128)S(1)} %collective-permute-done.7.refs_3_.params, f32[4,16,512]{2,1,0:T(8,128)S(1)} %collective-permute-done.14.refs_4_.coef, ...), custom_call_target="tpu_custom_call", output_to_operand_aliasing={{}: (6, {})} | custom-call | flops 10485760 | bytes 2621440 | tf_op jit(solution)/shard_map/finish_part/pallas_call | solution.py:414
  (35 shorter events, 9.2 us)
Async XLA Ops:
  0.8 8.8 %collective-permute-start = (f32[8,2688]{1,0:T(8,128)S(1)}, f32[8,2688]{1,0:T(8,128)S(1)}, u32[]{:S(2)}, u32[]{:S(2)}) collective-permute-start(f32[8,2688]{1,0:T(8,128)S(1)} %pack_part.1.refs_0_), channel_id=1, source_target_pairs={{0,4},{1,5},{2,6},{3,7},{4,0},{5,1},{6,2},{7,3},{8,12},{9,13},{10,... | collective-permute-start | bytes 258056 | tf_op jit(solution)/shard_map/ppermute | solution.py:429
  3.0 6.6 %collective-permute-start.1 = (f32[8,2688]{1,0:T(8,128)S(1)}, f32[8,2688]{1,0:T(8,128)S(1)}, u32[]{:S(2)}, u32[]{:S(2)}) collective-permute-start(f32[8,2688]{1,0:T(8,128)S(1)} %pack_part.1.refs_0_), channel_id=1, source_target_pairs={{0,8},{1,9},{2,10},{3,11},{4,12},{5,13},{6,14},{7,15},{8,0},{9,1},... | collective-permute-start | bytes 258056 | tf_op jit(solution)/shard_map/ppermute | solution.py:429
  5.3 5.4 %collective-permute-start.2 = (f32[8,2688]{1,0:T(8,128)S(1)}, f32[8,2688]{1,0:T(8,128)S(1)}, u32[]{:S(2)}, u32[]{:S(2)}) collective-permute-start(f32[8,2688]{1,0:T(8,128)S(1)} %pack_part.1.refs_0_), channel_id=1, source_target_pairs={{0,12},{1,13},{2,14},{3,15},{4,8},{5,9},{6,10},{7,11},{8,4},{9,5},... | collective-permute-start | bytes 258056 | tf_op jit(solution)/shard_map/ppermute | solution.py:429
  10.8 8.8 %collective-permute-start.5 = (f32[4,8,1664]{2,1,0:T(8,128)S(1)}, f32[4,8,1664]{2,1,0:T(8,128)S(1)}, u32[]{:S(2)}, u32[]{:S(2)}) collective-permute-start(f32[4,8,1664]{2,1,0:T(8,128)S(1)} %get-tuple-element.54.refs_3_.refs_0_.params), channel_id=1, source_target_pairs={{0,1},{1,0},{2,3},{3,2},{4,5},{5,4},{6,7},{7,6},{8,9},{9,8},{10,11... | collective-permute-start | bytes 638984 | tf_op jit(solution)/shard_map/ppermute | solution.py:429
  13.6 6.0 %collective-permute-start.4 = (bf16[3,2,8192]{2,1,0:T(2,128)(2,1)S(1)}, bf16[3,2,8192]{2,1,0:T(2,128)(2,1)S(1)}, u32[]{:S(2)}, u32[]{:S(2)}) collective-permute-start(bf16[3,2,8192]{2,1,0:T(2,128)(2,1)S(1)} %tail_part.1.refs_4_), channel_id=1, source_target_pairs={{0,1},{1,2},{2,3},{3,4},{4,5},{5,6},{6,7},{7,8},{8,9},{9,10},{10,1... | collective-permute-start | bytes 294920 | tf_op jit(solution)/shard_map/ppermute | solution.py:550
  16.6 7.0 %collective-permute-start.3 = (f32[4,8,1664]{2,1,0:T(8,128)S(1)}, f32[4,8,1664]{2,1,0:T(8,128)S(1)}, u32[]{:S(2)}, u32[]{:S(2)}) collective-permute-start(f32[4,8,1664]{2,1,0:T(8,128)S(1)} %get-tuple-element.54.refs_3_.refs_0_.params), channel_id=1, source_target_pairs={{0,2},{1,3},{2,0},{3,1},{4,6},{5,7},{6,4},{7,5},{8,10},{9,11},{10,... | collective-permute-start | bytes 638984 | tf_op jit(solution)/shard_map/ppermute | solution.py:429
  21.4 2.2 %collective-permute-start.6 = (f32[4,16,512]{2,1,0:T(8,128)S(1)}, f32[4,16,512]{2,1,0:T(8,128)S(1)}, u32[]{:S(2)}, u32[]{:S(2)}) collective-permute-start(f32[4,16,512]{2,1,0:T(8,128)S(1)} %get-tuple-element.58), channel_id=1, source_target_pairs={{0,1},{1,0},{2,3},{3,2},{4,5},{5,4},{6,7},{7,6},{8,9},{9,8},{10,11... | collective-permute-start | bytes 393224 | tf_op jit(solution)/shard_map/ppermute | solution.py:429
  23.6 2.2 %collective-permute-start.7 = (f32[4,8,1664]{2,1,0:T(8,128)S(1)}, f32[4,8,1664]{2,1,0:T(8,128)S(1)}, u32[]{:S(2)}, u32[]{:S(2)}) collective-permute-start(f32[4,8,1664]{2,1,0:T(8,128)S(1)} %collective-permute-done.3.refs_3_.params), channel_id=1, source_target_pairs={{0,1},{1,0},{2,3},{3,2},{4,5},{5,4},{6,7},{7,6},{8,9},{9,8},{10,11... | collective-permute-start | bytes 638984 | tf_op jit(solution)/shard_map/ppermute | solution.py:429
  27.6 1.4 %collective-permute-start.8 = (f32[4,16,512]{2,1,0:T(8,128)S(1)}, f32[4,16,512]{2,1,0:T(8,128)S(1)}, u32[]{:S(2)}, u32[]{:S(2)}) collective-permute-start(f32[4,16,512]{2,1,0:T(8,128)S(1)} %get-tuple-element.67), channel_id=1, source_target_pairs={{0,1},{1,0},{2,3},{3,2},{4,5},{5,4},{6,7},{7,6},{8,9},{9,8},{10,11... | collective-permute-start | bytes 393224 | tf_op jit(solution)/shard_map/ppermute | solution.py:429
  29.1 5.0 %collective-permute-start.9 = (f32[4,16,512]{2,1,0:T(8,128)S(1)}, f32[4,16,512]{2,1,0:T(8,128)S(1)}, u32[]{:S(2)}, u32[]{:S(2)}) collective-permute-start(f32[4,16,512]{2,1,0:T(8,128)S(1)} %get-tuple-element.68), channel_id=1, source_target_pairs={{0,2},{1,3},{2,0},{3,1},{4,6},{5,7},{6,4},{7,5},{8,10},{9,11},{10,... | collective-permute-start | bytes 393224 | tf_op jit(solution)/shard_map/ppermute | solution.py:429
  30.5 5.9 %collective-permute-start.11 = (f32[4,16,512]{2,1,0:T(8,128)S(1)}, f32[4,16,512]{2,1,0:T(8,128)S(1)}, u32[]{:S(2)}, u32[]{:S(2)}) collective-permute-start(f32[4,16,512]{2,1,0:T(8,128)S(1)} %get-tuple-element.70.refs_4_.coef), channel_id=1, source_target_pairs={{0,1},{1,0},{2,3},{3,2},{4,5},{5,4},{6,7},{7,6},{8,9},{9,8},{10,11... | collective-permute-start | bytes 393224 | tf_op jit(solution)/shard_map/ppermute | solution.py:429
  30.9 8.3 %collective-permute-start.12 = (f32[4,16,512]{2,1,0:T(8,128)S(1)}, f32[4,16,512]{2,1,0:T(8,128)S(1)}, u32[]{:S(2)}, u32[]{:S(2)}) collective-permute-start(f32[4,16,512]{2,1,0:T(8,128)S(1)} %get-tuple-element.70.refs_4_.coef), channel_id=1, source_target_pairs={{0,2},{1,3},{2,0},{3,1},{4,6},{5,7},{6,4},{7,5},{8,10},{9,11},{10,... | collective-permute-start | bytes 393224 | tf_op jit(solution)/shard_map/ppermute | solution.py:429
  34.2 5.1 %collective-permute-start.10 = (f32[4,16,512]{2,1,0:T(8,128)S(1)}, f32[4,16,512]{2,1,0:T(8,128)S(1)}, u32[]{:S(2)}, u32[]{:S(2)}) collective-permute-start(f32[4,16,512]{2,1,0:T(8,128)S(1)} %get-tuple-element.74.mine), channel_id=1, source_target_pairs={{0,4},{1,5},{2,6},{3,7},{4,0},{5,1},{6,2},{7,3},{8,12},{9,13},{10,... | collective-permute-start | bytes 393224 | tf_op jit(solution)/shard_map/ppermute | solution.py:429
  39.2 7.6 %collective-permute-start.14 = (f32[4,16,512]{2,1,0:T(8,128)S(1)}, f32[4,16,512]{2,1,0:T(8,128)S(1)}, u32[]{:S(2)}, u32[]{:S(2)}) collective-permute-start(f32[4,16,512]{2,1,0:T(8,128)S(1)} %collective-permute-done.12.refs_4_.coef), channel_id=1, source_target_pairs={{0,1},{1,0},{2,3},{3,2},{4,5},{5,4},{6,7},{7,6},{8,9},{9,8},{10,11... | collective-permute-start | bytes 393224 | tf_op jit(solution)/shard_map/ppermute | solution.py:429
  41.2 9.5 %collective-permute-start.13 = (f32[4,16,512]{2,1,0:T(8,128)S(1)}, f32[4,16,512]{2,1,0:T(8,128)S(1)}, u32[]{:S(2)}, u32[]{:S(2)}) collective-permute-start(f32[4,16,512]{2,1,0:T(8,128)S(1)} %get-tuple-element.77), channel_id=1, source_target_pairs={{0,8},{1,9},{2,10},{3,11},{4,12},{5,13},{6,14},{7,15},{8,0},{9,1},... | collective-permute-start | bytes 393224 | tf_op jit(solution)/shard_map/ppermute | solution.py:429
  50.8 3.0 %collective-permute-start.16 = (f32[4,16,512]{2,1,0:T(8,128)S(1)}, f32[4,16,512]{2,1,0:T(8,128)S(1)}, u32[]{:S(2)}, u32[]{:S(2)}) collective-permute-start(f32[4,16,512]{2,1,0:T(8,128)S(1)} %get-tuple-element.88), channel_id=1, source_target_pairs={{0,1},{1,0},{2,3},{3,2},{4,5},{5,4},{6,7},{7,6},{8,9},{9,8},{10,11... | collective-permute-start | bytes 393224 | tf_op jit(solution)/shard_map/ppermute | solution.py:429
  51.5 5.1 %collective-permute-start.15 = (f32[4,16,512]{2,1,0:T(8,128)S(1)}, f32[4,16,512]{2,1,0:T(8,128)S(1)}, u32[]{:S(2)}, u32[]{:S(2)}) collective-permute-start(f32[4,16,512]{2,1,0:T(8,128)S(1)} %get-tuple-element.86), channel_id=1, source_target_pairs={{0,2},{1,3},{2,0},{3,1},{4,6},{5,7},{6,4},{7,5},{8,10},{9,11},{10,... | collective-permute-start | bytes 393224 | tf_op jit(solution)/shard_map/ppermute | solution.py:429
  56.6 2.7 %collective-permute-start.17 = (f32[4,16,512]{2,1,0:T(8,128)S(1)}, f32[4,16,512]{2,1,0:T(8,128)S(1)}, u32[]{:S(2)}, u32[]{:S(2)}) collective-permute-start(f32[4,16,512]{2,1,0:T(8,128)S(1)} %get-tuple-element.94), channel_id=1, source_target_pairs={{0,1},{1,0},{2,3},{3,2},{4,5},{5,4},{6,7},{7,6},{8,9},{9,8},{10,11... | collective-permute-start | bytes 393224 | tf_op jit(solution)/shard_map/ppermute | solution.py:429

commit v4 on v3

--- a/solution.py
+++ b/solution.py
@@ -18,7 +18,7 @@
 PARAM_COLS = TAP_COLS + LANES
 GROUP = 4
 GROUPS = 4
-UNROLL = 32
+UNROLL = 64
 HBM = pl.BlockSpec(memory_space=pltpu.HBM)
 F32 = jnp.float32
 VMEM = pl.BlockSpec(memory_space=pltpu.VMEM)
@@ -78,11 +78,19 @@
     done[...] = jnp.zeros_like(done)
 
 
-def pack_kernel(scale, filters_in, residues_in, rates_in, wide, filters, residues, rates, sems):
+def pack_kernel(
+    scale, filters_in, residues_in, rates_in, feats, wide, tail, filters, residues, rates, last, sems
+):
+    count = feats.shape[1]
     copies = [
         pltpu.make_async_copy(source, dest, sems.at[n])
         for n, (source, dest) in enumerate(
-            ((rates_in, rates), (residues_in, residues), (filters_in, filters))
+            (
+                (rates_in, rates),
+                (residues_in, residues),
+                (filters_in, filters),
+                (feats.at[:, count - SUB : count, :], last),
+            )
         )
     ]
     for copy in copies:
@@ -105,25 +113,18 @@
         else:
             for k in range(CHUNKS):
                 wide[k : k + 1, TAP_COLS:PARAM_COLS] = row[:, k * LANES : (k + 1) * LANES]
-
-
-def tail_kernel(feats, *refs):
-    tail, last, sem = refs[-3:]
-    rows = feats.shape[1]
-    copy = pltpu.make_async_copy(feats.at[:, rows - SUB : rows, :], last, sem)
-    copy.start()
-    copy.wait()
+    copies[3].wait()
     for b in range(3):
         tail[b] = last[b, SUB - 2 : SUB, :]
 
 
 def stack_kernel(*refs):
     params, coef = refs[-2:]
-    for i in range(GROUP):
-        params[i] = refs[i][:, 0:PARAM_COLS]
+    for ref, i in zip(refs, NEAR + (0,)):
+        params[i] = ref[:, 0:PARAM_COLS]
         for h in range(2):
             at = PARAM_COLS + h * WIDTH
-            coef[i, h * HALF : (h + 1) * HALF, :] = refs[i][:, at : at + WIDTH]
+            coef[i, h * HALF : (h + 1) * HALF, :] = ref[:, at : at + WIDTH]
 
 
 def ends_kernel(
@@ -309,40 +310,29 @@
     return pltpu.with_memory_space_constraint(value, pltpu.HBM)
 
 
-def pack_part(filters, residues, rates, scale):
+def pack_part(filters, residues, rates, feats, scale):
+    width = feats.shape[2]
     return pl.pallas_call(
         functools.partial(pack_kernel, scale),
-        out_shape=pltpu.VMEM((SUB, PARAM_COLS + 2 * WIDTH), F32),
+        out_shape=(
+            pltpu.VMEM((SUB, PARAM_COLS + 2 * WIDTH), F32),
+            pltpu.VMEM((3, 2, width), feats.dtype),
+        ),
         name="pack_part",
         **whole(
-            [HBM] * 3,
-            VMEM,
+            [HBM] * 4,
+            [VMEM] * 2,
             (),
             (
                 pltpu.VMEM(filters.shape, filters.dtype),
                 pltpu.VMEM((MODES, WIDTH), F32),
                 pltpu.VMEM((MODES, WIDTH), F32),
-                pltpu.SemaphoreType.DMA((3,)),
+                pltpu.VMEM((3, SUB, width), feats.dtype),
+                pltpu.SemaphoreType.DMA((4,)),
             ),
             smem=0,
         ),
-    )(in_hbm(filters), in_hbm(residues), in_hbm(rates))
-
-
-def tail_part(feats, *earlier):
-    width = feats.shape[2]
-    return pl.pallas_call(
-        tail_kernel,
-        out_shape=pltpu.VMEM((3, 2, width), feats.dtype),
-        name="tail_part",
-        **whole(
-            [HBM] + [ANYWHERE] * len(earlier),
-            VMEM,
-            (),
-            (pltpu.VMEM((3, SUB, width), feats.dtype), pltpu.SemaphoreType.DMA),
-            smem=0,
-        ),
-    )(in_hbm(feats), *earlier)
+    )(in_hbm(filters), in_hbm(residues), in_hbm(rates), in_hbm(feats))
 
 
 def stack_part(parts, *earlier):
@@ -422,6 +412,7 @@
 
 
 CORE, Y, Z = 1, 2, 4
+NEAR = (3, 2, 1)
 
 
 def swap(value, bit):
@@ -539,14 +530,14 @@
         return by_gathers(feats, tail, short_filter, residues, rates, scale, span)
 
     base = me.reshape(1)
-    wide = pack_part(short_filter, residues.T, rates.T, scale)
-    near = [swap(wide, Z * k) for k in range(1, GROUP)]
+    wide, tail_rows = pack_part(short_filter, residues.T, rates.T, feats, scale)
+    near = [swap(wide, Z * k) for k in NEAR]
+    tail = lax.ppermute(tail_rows, "ctx", onward)
     keyed, staged = stage_part((1, 2), feats, wide, base)
-    tail_rows = tail_part(feats, staged)
-    params, coef = ([x] for x in stack_part([wide] + near, tail_rows))
+    query, staged = stage_part((0,), feats, staged)
+    params, coef = ([x] for x in stack_part(near + [wide], staged, tail))
     params.append(swap(params[0], CORE))
     params.append(swap(params[0], Y))
-    query, staged = stage_part((0,), feats, params[0])
     tail = lax.ppermute(tail_rows, "ctx", onward)
     coef.append(swap(coef[0], CORE))
     ends, drive, packed = [None] * GROUPS, [None] * GROUPS, [None] * GROUPS
@@ -557,7 +548,7 @@
     def run_inner(g):
         packed[g] = inner_part(g, base, query, tail, params[g], coef[g], drive[g], scale)
 
-    run_ends(1, staged)
+    run_ends(1)
     from_1 = swap(ends[1], CORE)
     run_ends(0)
     params[2], ends[0], from_1 = after(params[2], ends[0], from_1)

time: 62.1 us -> 60.7 us (0.977)
  waiting for transfers between devices: 4.93 us -> 7.35 us
  starting transfers between devices: 23.2 us -> 20.9 us
  Pallas kernels: 33.4 us -> 32.1 us
    ppermute x17, starting transfers between devices: 20.2 us -> 16.4 us  [swap(): return lax.ppermute(value, 'ctx', [(i, i ^ bit) for i in range(size)])]
    ppermute x17, waiting for transfers between devices: 4.93 us -> 7.35 us  [swap(): return lax.ppermute(value, 'ctx', [(i, i ^ bit) for i in range(size)])]
    ppermute x1, starting transfers between devices: 3.05 us -> 4.54 us  [per_device(): tail = lax.ppermute(tail_rows, 'ctx', onward)]
    pallas_call x2 -> x1, Pallas kernels: 1.9 us -> 1.14 us  [pack_part(): pl.pallas_call(functools.partial(pack_kernel, scale), out_shape=(pltpu.VM...]
  transfers between devices with their start and end apart: 18 -> 18, of which waited for: 6 -> 8; matrix products, arithmetic and copies ran while one was open for 0% -> 0% of each run, Pallas kernels for 45% -> 44%
where the time goes in v4:
time: 60.7 us; the launch traced here: 60.6 us
  Pallas kernels  32.1 us (53%)
  starting transfers between devices  20.9 us (34%)
  waiting for transfers between devices  7.35 us (12%)
    ppermute x17, starting transfers between devices, swap(): return lax.ppermute(value, 'ctx', [(i, i ^ bit) for i in range(size)])  16.4 us
    pallas_call x4, Pallas kernels, inner_part(): pl.pallas_call(functools.partial(pieces, functools.partial(inner_kernel,...  10.9 us
    pallas_call x4, Pallas kernels, finish_part(): pl.pallas_call(functools.partial(finish_body, scale, group), out_shape=ou...  7.78 us
    ppermute x17, waiting for transfers between devices, swap(): return lax.ppermute(value, 'ctx', [(i, i ^ bit) for i in range(size)])  7.35 us
    pallas_call x4, Pallas kernels, ends_part(): pl.pallas_call(functools.partial(pieces, functools.partial(ends_kernel, s...  6.96 us
    pallas_call x2, Pallas kernels, stage_part(): pl.pallas_call(functools.partial(stage_body, branches, stride), out_shape...  4.97 us
    ppermute x1, starting transfers between devices, per_device(): tail = lax.ppermute(tail_rows, 'ctx', onward)  4.54 us
  transfers between devices with their start and end apart: 18, of which 8 were waited for; matrix products, arithmetic and copies ran while one was open for 0% of the time, Pallas kernels for 44%

profile of v4, /device:TPU:1, one launch (start us, length us, event | category | flops | bytes accessed | tf_op | source)
XLA Modules:
  0.0 60.6 jit_solution(6701277959751921400)
XLA Ops:
  1.1 4.5 %collective-permute-start.3 = (bf16[3,2,8192]{2,1,0:T(2,128)(2,1)S(1)}, bf16[3,2,8192]{2,1,0:T(2,128)(2,1)S(1)}, u32[]{:S(2)}, u32[]{:S(2)}) collective-permute-start(bf16[3,2,8192]{2,1,0:T(2,128)(2,1)S(1)} %get-tuple-element.58), channel_id=1, source_target_pairs={{0,1},{1,2},{2,3},{3,4},{4,5},{5,6},{6,7},{7,8},{8,9},{9,10},{10,1... | collective-permute-start | bytes 294920 | tf_op jit(solution)/shard_map/ppermute | solution.py:535
  5.7 3.4 %collective-permute-start = (f32[8,2688]{1,0:T(8,128)S(1)}, f32[8,2688]{1,0:T(8,128)S(1)}, u32[]{:S(2)}, u32[]{:S(2)}) collective-permute-start(f32[8,2688]{1,0:T(8,128)S(1)} %get-tuple-element.55.refs_0_.refs_3_), channel_id=1, source_target_pairs={{0,12},{1,13},{2,14},{3,15},{4,8},{5,9},{6,10},{7,11},{8,4},{9,5},... | collective-permute-start | bytes 258056 | tf_op jit(solution)/shard_map/ppermute | solution.py:420
  9.4 3.2 %stage_part.2 = (f32[16,1024,128]{2,1,0:T(8,128)S(1)}, f32[8,128]{1,0:T(8,128)S(1)}) custom-call(bf16[3,128,8192]{2,1,0:T(8,128)(2,1)} %bitcast.5, f32[8,2688]{1,0:T(8,128)S(1)} %get-tuple-element.55.refs_0_.refs_3_, s32[1]{0:T(128)} %bitcast.refs_1_.refs_0_.me), custom_call_target="tpu_custom_call" | custom-call | flops 20971520 | bytes 5242880 | tf_op jit(solution)/shard_map/stage_part/pallas_call | solution.py:287
  12.6 1.8 %stage_part.3 = (f32[16,512,128]{2,1,0:T(8,128)S(1)}, f32[8,128]{1,0:T(8,128)S(1)}) custom-call(bf16[3,128,8192]{2,1,0:T(8,128)(2,1)} %bitcast.6, f32[8,128]{1,0:T(8,128)S(1)} %get-tuple-element.56.refs_0_), custom_call_target="tpu_custom_call" | custom-call | flops 10485760 | bytes 2621440 | tf_op jit(solution)/shard_map/stage_part/pallas_call | solution.py:287
  14.4 1.5 %collective-permute-done.1.refs_1_ = f32[8,2688]{1,0:T(8,128)S(1)} collective-permute-done((f32[8,2688]{1,0:T(8,128)S(1)}, f32[8,2688]{1,0:T(8,128)S(1)}, u32[]{:S(2)}, u32[]{:S(2)}) %collective-permute-start.1) | collective-permute-done | bytes 86048 | tf_op jit(solution)/shard_map/ppermute | solution.py:420
  16.1 1.2 %collective-permute-start.4 = (f32[4,8,1664]{2,1,0:T(8,128)S(1)}, f32[4,8,1664]{2,1,0:T(8,128)S(1)}, u32[]{:S(2)}, u32[]{:S(2)}) collective-permute-start(f32[4,8,1664]{2,1,0:T(8,128)S(1)} %get-tuple-element.59.refs_3_.params), channel_id=1, source_target_pairs={{0,2},{1,3},{2,0},{3,1},{4,6},{5,7},{6,4},{7,5},{8,10},{9,11},{10,... | collective-permute-start | bytes 638984 | tf_op jit(solution)/shard_map/ppermute | solution.py:420
  17.5 1.7 %ends_part.5 = (f32[4,16,512]{2,1,0:T(8,128)S(1)}, f32[4,1024,128]{2,1,0:T(8,128)S(1)}) custom-call(s32[1]{0:T(128)} %bitcast.refs_1_.refs_0_.me, f32[16,1024,128]{2,1,0:T(8,128)S(1)} %get-tuple-element.60.refs_1_, bf16[3,2,8192]{2,1,0:T(2,128)(2,1)S(1)} %collective-permute-done.3.refs_5_.refs_2_, f32[4,8,1664]{2,1,0:T(8,128)S(1)} %collective-permute-done.5.refs_3_.params), custom_call_target="tpu_custom_call" | custom-call | flops 12582912 | bytes 3145728 | tf_op jit(solution)/shard_map/ends_part/pallas_call | solution.py:353
  19.8 1.7 %ends_part.4 = (f32[4,16,512]{2,1,0:T(8,128)S(1)}, f32[4,1024,128]{2,1,0:T(8,128)S(1)}) custom-call(s32[1]{0:T(128)} %bitcast.refs_1_.refs_0_.me, f32[16,1024,128]{2,1,0:T(8,128)S(1)} %get-tuple-element.60.refs_1_, bf16[3,2,8192]{2,1,0:T(2,128)(2,1)S(1)} %collective-permute-done.3.refs_5_.refs_2_, f32[4,8,1664]{2,1,0:T(8,128)S(1)} %get-tuple-element.59.refs_3_.params), custom_call_target="tpu_custom_call" | custom-call | flops 12582912 | bytes 3145728 | tf_op jit(solution)/shard_map/ends_part/pallas_call | solution.py:353
  22.5 1.3 %collective-permute-start.7 = (f32[4,8,1664]{2,1,0:T(8,128)S(1)}, f32[4,8,1664]{2,1,0:T(8,128)S(1)}, u32[]{:S(2)}, u32[]{:S(2)}) collective-permute-start(f32[4,8,1664]{2,1,0:T(8,128)S(1)} %collective-permute-done.4.refs_3_.params), channel_id=1, source_target_pairs={{0,1},{1,0},{2,3},{3,2},{4,5},{5,4},{6,7},{7,6},{8,9},{9,8},{10,11... | collective-permute-start | bytes 638984 | tf_op jit(solution)/shard_map/ppermute | solution.py:420
  23.8 1.7 %ends_part.6 = (f32[4,16,512]{2,1,0:T(8,128)S(1)}, f32[4,1024,128]{2,1,0:T(8,128)S(1)}) custom-call(s32[1]{0:T(128)} %bitcast.refs_1_.refs_0_.me, f32[16,1024,128]{2,1,0:T(8,128)S(1)} %get-tuple-element.60.refs_1_, bf16[3,2,8192]{2,1,0:T(2,128)(2,1)S(1)} %collective-permute-done.3.refs_5_.refs_2_, f32[4,8,1664]{2,1,0:T(8,128)S(1)} %collective-permute-done.4.refs_3_.params), custom_call_target="tpu_custom_call" | custom-call | flops 12582912 | bytes 3145728 | tf_op jit(solution)/shard_map/ends_part/pallas_call | solution.py:353
  25.6 1.7 %ends_part.7 = (f32[4,16,512]{2,1,0:T(8,128)S(1)}, f32[4,1024,128]{2,1,0:T(8,128)S(1)}) custom-call(s32[1]{0:T(128)} %bitcast.refs_1_.refs_0_.me, f32[16,1024,128]{2,1,0:T(8,128)S(1)} %get-tuple-element.60.refs_1_, bf16[3,2,8192]{2,1,0:T(2,128)(2,1)S(1)} %collective-permute-done.3.refs_5_.refs_2_, f32[4,8,1664]{2,1,0:T(8,128)S(1)} %collective-permute-done.7.refs_3_.params), custom_call_target="tpu_custom_call" | custom-call | flops 12582912 | bytes 3145728 | tf_op jit(solution)/shard_map/ends_part/pallas_call | solution.py:353
  27.4 1.3 %collective-permute-done.8.theirs = f32[4,16,512]{2,1,0:T(8,128)S(1)} collective-permute-done((f32[4,16,512]{2,1,0:T(8,128)S(1)}, f32[4,16,512]{2,1,0:T(8,128)S(1)}, u32[]{:S(2)}, u32[]{:S(2)}) %collective-permute-start.8) | collective-permute-done | bytes 131104 | tf_op jit(solution)/shard_map/ppermute | solution.py:420
  28.8 1.3 %collective-permute-start.9 = (f32[4,16,512]{2,1,0:T(8,128)S(1)}, f32[4,16,512]{2,1,0:T(8,128)S(1)}, u32[]{:S(2)}, u32[]{:S(2)}) collective-permute-start(f32[4,16,512]{2,1,0:T(8,128)S(1)} %get-tuple-element.72), channel_id=1, source_target_pairs={{0,2},{1,3},{2,0},{3,1},{4,6},{5,7},{6,4},{7,5},{8,10},{9,11},{10,... | collective-permute-start | bytes 393224 | tf_op jit(solution)/shard_map/ppermute | solution.py:420
  30.7 2.7 %inner_part.4.packed = f32[4,1024,128]{2,1,0:T(8,128)S(1)} custom-call(s32[1]{0:T(128)} %bitcast.refs_1_.refs_0_.me, f32[16,512,128]{2,1,0:T(8,128)S(1)} %get-tuple-element.73.refs_1_, bf16[3,2,8192]{2,1,0:T(2,128)(2,1)S(1)} %collective-permute-done.3.refs_5_.refs_2_, f32[4,8,1664]{2,1,0:T(8,128)S(1)} %get-tuple-element.59.refs_3_.params, ...), custom_call_target="tpu_custom_call" | custom-call | flops 18874368 | bytes 4718592 | tf_op jit(solution)/shard_map/inner_part/pallas_call | solution.py:373
  34.4 2.7 %inner_part.5.packed = f32[4,1024,128]{2,1,0:T(8,128)S(1)} custom-call(s32[1]{0:T(128)} %bitcast.refs_1_.refs_0_.me, f32[16,512,128]{2,1,0:T(8,128)S(1)} %get-tuple-element.73.refs_1_, bf16[3,2,8192]{2,1,0:T(2,128)(2,1)S(1)} %collective-permute-done.3.refs_5_.refs_2_, f32[4,8,1664]{2,1,0:T(8,128)S(1)} %collective-permute-done.5.refs_3_.params, ...), custom_call_target="tpu_custom_call" | custom-call | flops 18874368 | bytes 4718592 | tf_op jit(solution)/shard_map/inner_part/pallas_call | solution.py:373
  37.7 2.7 %collective-permute-start.14 = (f32[4,16,512]{2,1,0:T(8,128)S(1)}, f32[4,16,512]{2,1,0:T(8,128)S(1)}, u32[]{:S(2)}, u32[]{:S(2)}) collective-permute-start(f32[4,16,512]{2,1,0:T(8,128)S(1)} %collective-permute-done.12.refs_4_.coef), channel_id=1, source_target_pairs={{0,1},{1,0},{2,3},{3,2},{4,5},{5,4},{6,7},{7,6},{8,9},{9,8},{10,11... | collective-permute-start | bytes 393224 | tf_op jit(solution)/shard_map/ppermute | solution.py:420
  41.6 2.7 %inner_part.6.packed = f32[4,1024,128]{2,1,0:T(8,128)S(1)} custom-call(s32[1]{0:T(128)} %bitcast.refs_1_.refs_0_.me, f32[16,512,128]{2,1,0:T(8,128)S(1)} %get-tuple-element.73.refs_1_, bf16[3,2,8192]{2,1,0:T(2,128)(2,1)S(1)} %collective-permute-done.3.refs_5_.refs_2_, f32[4,8,1664]{2,1,0:T(8,128)S(1)} %collective-permute-done.4.refs_3_.params, ...), custom_call_target="tpu_custom_call" | custom-call | flops 18874368 | bytes 4718592 | tf_op jit(solution)/shard_map/inner_part/pallas_call | solution.py:373
  44.3 2.7 %inner_part.7.packed = f32[4,1024,128]{2,1,0:T(8,128)S(1)} custom-call(s32[1]{0:T(128)} %bitcast.refs_1_.refs_0_.me, f32[16,512,128]{2,1,0:T(8,128)S(1)} %get-tuple-element.73.refs_1_, bf16[3,2,8192]{2,1,0:T(2,128)(2,1)S(1)} %collective-permute-done.3.refs_5_.refs_2_, f32[4,8,1664]{2,1,0:T(8,128)S(1)} %collective-permute-done.7.refs_3_.params, ...), custom_call_target="tpu_custom_call" | custom-call | flops 18874368 | bytes 4718592 | tf_op jit(solution)/shard_map/inner_part/pallas_call | solution.py:373
  47.1 2.3 %collective-permute-done.13.far = f32[4,16,512]{2,1,0:T(8,128)S(1)} collective-permute-done((f32[4,16,512]{2,1,0:T(8,128)S(1)}, f32[4,16,512]{2,1,0:T(8,128)S(1)}, u32[]{:S(2)}, u32[]{:S(2)}) %collective-permute-start.13) | collective-permute-done | bytes 131104 | tf_op jit(solution)/shard_map/ppermute | solution.py:420
  50.3 1.2 %collective-permute-start.15 = (f32[4,16,512]{2,1,0:T(8,128)S(1)}, f32[4,16,512]{2,1,0:T(8,128)S(1)}, u32[]{:S(2)}, u32[]{:S(2)}) collective-permute-start(f32[4,16,512]{2,1,0:T(8,128)S(1)} %get-tuple-element.90), channel_id=1, source_target_pairs={{0,2},{1,3},{2,0},{3,1},{4,6},{5,7},{6,4},{7,5},{8,10},{9,11},{10,... | collective-permute-start | bytes 393224 | tf_op jit(solution)/shard_map/ppermute | solution.py:420
  51.5 1.8 %finish_part.4.refs_0_ = bf16[4,128,512]{2,1,0:T(8,128)(2,1)S(1)} custom-call(s32[1]{0:T(128)} %bitcast.refs_1_.refs_0_.me, f32[4,1024,128]{2,1,0:T(8,128)S(1)} %inner_part.4.packed, f32[4,8,1664]{2,1,0:T(8,128)S(1)} %get-tuple-element.59.refs_3_.params, f32[4,16,512]{2,1,0:T(8,128)S(1)} %get-tuple-element.74.refs_4_.coef, ...), custom_call_target="tpu_custom_call" | custom-call | flops 10485760 | bytes 2621440 | tf_op jit(solution)/shard_map/finish_part/pallas_call | solution.py:404
  53.3 1.8 %finish_part.5 = (bf16[128,8192]{1,0:T(8,128)(2,1)}, bf16[4,128,512]{2,1,0:T(8,128)(2,1)S(1)}) custom-call(s32[1]{0:T(128)} %bitcast.refs_1_.refs_0_.me, f32[4,1024,128]{2,1,0:T(8,128)S(1)} %inner_part.5.packed, f32[4,8,1664]{2,1,0:T(8,128)S(1)} %collective-permute-done.5.refs_3_.params, f32[4,16,512]{2,1,0:T(8,128)S(1)} %collective-permute-done.11.refs_4_.coef, ...), custom_call_target="tpu_custom_call" | custom-call | flops 10485760 | bytes 2621440 | tf_op jit(solution)/shard_map/finish_part/pallas_call | solution.py:404
  56.3 1.8 %finish_part.6 = (bf16[128,8192]{1,0:T(8,128)(2,1)}, bf16[4,128,512]{2,1,0:T(8,128)(2,1)S(1)}) custom-call(s32[1]{0:T(128)} %bitcast.refs_1_.refs_0_.me, f32[4,1024,128]{2,1,0:T(8,128)S(1)} %inner_part.6.packed, f32[4,8,1664]{2,1,0:T(8,128)S(1)} %collective-permute-done.4.refs_3_.params, ...), custom_call_target="tpu_custom_call", output_to_operand_aliasing={{0}: (6, {})} | custom-call | flops 10485760 | bytes 2621440 | tf_op jit(solution)/shard_map/finish_part/pallas_call | solution.py:404
  58.1 2.4 %finish_part.7 = bf16[128,8192]{1,0:T(8,128)(2,1)} custom-call(s32[1]{0:T(128)} %bitcast.refs_1_.refs_0_.me, f32[4,1024,128]{2,1,0:T(8,128)S(1)} %inner_part.7.packed, f32[4,8,1664]{2,1,0:T(8,128)S(1)} %collective-permute-done.7.refs_3_.params, f32[4,16,512]{2,1,0:T(8,128)S(1)} %collective-permute-done.14.refs_4_.coef, ...), custom_call_target="tpu_custom_call", output_to_operand_aliasing={{}: (6, {})} | custom-call | flops 10485760 | bytes 2621440 | tf_op jit(solution)/shard_map/finish_part/pallas_call | solution.py:404
  (34 shorter events, 8.9 us)
Async XLA Ops:
  1.1 14.8 %collective-permute-start.3 = (bf16[3,2,8192]{2,1,0:T(2,128)(2,1)S(1)}, bf16[3,2,8192]{2,1,0:T(2,128)(2,1)S(1)}, u32[]{:S(2)}, u32[]{:S(2)}) collective-permute-start(bf16[3,2,8192]{2,1,0:T(2,128)(2,1)S(1)} %get-tuple-element.58), channel_id=1, source_target_pairs={{0,1},{1,2},{2,3},{3,4},{4,5},{5,6},{6,7},{7,8},{8,9},{9,10},{10,1... | collective-permute-start | bytes 294920 | tf_op jit(solution)/shard_map/ppermute | solution.py:535
  5.7 8.7 %collective-permute-start = (f32[8,2688]{1,0:T(8,128)S(1)}, f32[8,2688]{1,0:T(8,128)S(1)}, u32[]{:S(2)}, u32[]{:S(2)}) collective-permute-start(f32[8,2688]{1,0:T(8,128)S(1)} %get-tuple-element.55.refs_0_.refs_3_), channel_id=1, source_target_pairs={{0,12},{1,13},{2,14},{3,15},{4,8},{5,9},{6,10},{7,11},{8,4},{9,5},... | collective-permute-start | bytes 258056 | tf_op jit(solution)/shard_map/ppermute | solution.py:420
  9.1 6.8 %collective-permute-start.1 = (f32[8,2688]{1,0:T(8,128)S(1)}, f32[8,2688]{1,0:T(8,128)S(1)}, u32[]{:S(2)}, u32[]{:S(2)}) collective-permute-start(f32[8,2688]{1,0:T(8,128)S(1)} %get-tuple-element.55.refs_0_.refs_3_), channel_id=1, source_target_pairs={{0,8},{1,9},{2,10},{3,11},{4,12},{5,13},{6,14},{7,15},{8,0},{9,1},... | collective-permute-start | bytes 258056 | tf_op jit(solution)/shard_map/ppermute | solution.py:420
  9.1 6.8 %collective-permute-start.2 = (f32[8,2688]{1,0:T(8,128)S(1)}, f32[8,2688]{1,0:T(8,128)S(1)}, u32[]{:S(2)}, u32[]{:S(2)}) collective-permute-start(f32[8,2688]{1,0:T(8,128)S(1)} %get-tuple-element.55.refs_0_.refs_3_), channel_id=1, source_target_pairs={{0,4},{1,5},{2,6},{3,7},{4,0},{5,1},{6,2},{7,3},{8,12},{9,13},{10,... | collective-permute-start | bytes 258056 | tf_op jit(solution)/shard_map/ppermute | solution.py:420
  15.9 1.5 %collective-permute-start.5 = (f32[4,8,1664]{2,1,0:T(8,128)S(1)}, f32[4,8,1664]{2,1,0:T(8,128)S(1)}, u32[]{:S(2)}, u32[]{:S(2)}) collective-permute-start(f32[4,8,1664]{2,1,0:T(8,128)S(1)} %get-tuple-element.59.refs_3_.params), channel_id=1, source_target_pairs={{0,1},{1,0},{2,3},{3,2},{4,5},{5,4},{6,7},{7,6},{8,9},{9,8},{10,11... | collective-permute-start | bytes 638984 | tf_op jit(solution)/shard_map/ppermute | solution.py:420
  16.1 6.4 %collective-permute-start.4 = (f32[4,8,1664]{2,1,0:T(8,128)S(1)}, f32[4,8,1664]{2,1,0:T(8,128)S(1)}, u32[]{:S(2)}, u32[]{:S(2)}) collective-permute-start(f32[4,8,1664]{2,1,0:T(8,128)S(1)} %get-tuple-element.59.refs_3_.params), channel_id=1, source_target_pairs={{0,2},{1,3},{2,0},{3,1},{4,6},{5,7},{6,4},{7,5},{8,10},{9,11},{10,... | collective-permute-start | bytes 638984 | tf_op jit(solution)/shard_map/ppermute | solution.py:420
  19.2 3.3 %collective-permute-start.6 = (f32[4,16,512]{2,1,0:T(8,128)S(1)}, f32[4,16,512]{2,1,0:T(8,128)S(1)}, u32[]{:S(2)}, u32[]{:S(2)}) collective-permute-start(f32[4,16,512]{2,1,0:T(8,128)S(1)} %get-tuple-element.62), channel_id=1, source_target_pairs={{0,1},{1,0},{2,3},{3,2},{4,5},{5,4},{6,7},{7,6},{8,9},{9,8},{10,11... | collective-permute-start | bytes 393224 | tf_op jit(solution)/shard_map/ppermute | solution.py:420
  22.5 3.0 %collective-permute-start.7 = (f32[4,8,1664]{2,1,0:T(8,128)S(1)}, f32[4,8,1664]{2,1,0:T(8,128)S(1)}, u32[]{:S(2)}, u32[]{:S(2)}) collective-permute-start(f32[4,8,1664]{2,1,0:T(8,128)S(1)} %collective-permute-done.4.refs_3_.params), channel_id=1, source_target_pairs={{0,1},{1,0},{2,3},{3,2},{4,5},{5,4},{6,7},{7,6},{8,9},{9,8},{10,11... | collective-permute-start | bytes 638984 | tf_op jit(solution)/shard_map/ppermute | solution.py:420
  27.3 1.4 %collective-permute-start.8 = (f32[4,16,512]{2,1,0:T(8,128)S(1)}, f32[4,16,512]{2,1,0:T(8,128)S(1)}, u32[]{:S(2)}, u32[]{:S(2)}) collective-permute-start(f32[4,16,512]{2,1,0:T(8,128)S(1)} %get-tuple-element.71), channel_id=1, source_target_pairs={{0,1},{1,0},{2,3},{3,2},{4,5},{5,4},{6,7},{7,6},{8,9},{9,8},{10,11... | collective-permute-start | bytes 393224 | tf_op jit(solution)/shard_map/ppermute | solution.py:420
  28.8 5.0 %collective-permute-start.9 = (f32[4,16,512]{2,1,0:T(8,128)S(1)}, f32[4,16,512]{2,1,0:T(8,128)S(1)}, u32[]{:S(2)}, u32[]{:S(2)}) collective-permute-start(f32[4,16,512]{2,1,0:T(8,128)S(1)} %get-tuple-element.72), channel_id=1, source_target_pairs={{0,2},{1,3},{2,0},{3,1},{4,6},{5,7},{6,4},{7,5},{8,10},{9,11},{10,... | collective-permute-start | bytes 393224 | tf_op jit(solution)/shard_map/ppermute | solution.py:420
  30.1 4.3 %collective-permute-start.11 = (f32[4,16,512]{2,1,0:T(8,128)S(1)}, f32[4,16,512]{2,1,0:T(8,128)S(1)}, u32[]{:S(2)}, u32[]{:S(2)}) collective-permute-start(f32[4,16,512]{2,1,0:T(8,128)S(1)} %get-tuple-element.74.refs_4_.coef), channel_id=1, source_target_pairs={{0,1},{1,0},{2,3},{3,2},{4,5},{5,4},{6,7},{7,6},{8,9},{9,8},{10,11... | collective-permute-start | bytes 393224 | tf_op jit(solution)/shard_map/ppermute | solution.py:420
  30.5 6.6 %collective-permute-start.12 = (f32[4,16,512]{2,1,0:T(8,128)S(1)}, f32[4,16,512]{2,1,0:T(8,128)S(1)}, u32[]{:S(2)}, u32[]{:S(2)}) collective-permute-start(f32[4,16,512]{2,1,0:T(8,128)S(1)} %get-tuple-element.74.refs_4_.coef), channel_id=1, source_target_pairs={{0,2},{1,3},{2,0},{3,1},{4,6},{5,7},{6,4},{7,5},{8,10},{9,11},{10,... | collective-permute-start | bytes 393224 | tf_op jit(solution)/shard_map/ppermute | solution.py:420
  33.8 3.9 %collective-permute-start.10 = (f32[4,16,512]{2,1,0:T(8,128)S(1)}, f32[4,16,512]{2,1,0:T(8,128)S(1)}, u32[]{:S(2)}, u32[]{:S(2)}) collective-permute-start(f32[4,16,512]{2,1,0:T(8,128)S(1)} %get-tuple-element.78.mine), channel_id=1, source_target_pairs={{0,4},{1,5},{2,6},{3,7},{4,0},{5,1},{6,2},{7,3},{8,12},{9,13},{10,... | collective-permute-start | bytes 393224 | tf_op jit(solution)/shard_map/ppermute | solution.py:420
  37.7 6.6 %collective-permute-start.14 = (f32[4,16,512]{2,1,0:T(8,128)S(1)}, f32[4,16,512]{2,1,0:T(8,128)S(1)}, u32[]{:S(2)}, u32[]{:S(2)}) collective-permute-start(f32[4,16,512]{2,1,0:T(8,128)S(1)} %collective-permute-done.12.refs_4_.coef), channel_id=1, source_target_pairs={{0,1},{1,0},{2,3},{3,2},{4,5},{5,4},{6,7},{7,6},{8,9},{9,8},{10,11... | collective-permute-start | bytes 393224 | tf_op jit(solution)/shard_map/ppermute | solution.py:420
  40.4 9.0 %collective-permute-start.13 = (f32[4,16,512]{2,1,0:T(8,128)S(1)}, f32[4,16,512]{2,1,0:T(8,128)S(1)}, u32[]{:S(2)}, u32[]{:S(2)}) collective-permute-start(f32[4,16,512]{2,1,0:T(8,128)S(1)} %get-tuple-element.81), channel_id=1, source_target_pairs={{0,8},{1,9},{2,10},{3,11},{4,12},{5,13},{6,14},{7,15},{8,0},{9,1},... | collective-permute-start | bytes 393224 | tf_op jit(solution)/shard_map/ppermute | solution.py:420
  49.5 3.8 %collective-permute-start.16 = (f32[4,16,512]{2,1,0:T(8,128)S(1)}, f32[4,16,512]{2,1,0:T(8,128)S(1)}, u32[]{:S(2)}, u32[]{:S(2)}) collective-permute-start(f32[4,16,512]{2,1,0:T(8,128)S(1)} %get-tuple-element.92), channel_id=1, source_target_pairs={{0,1},{1,0},{2,3},{3,2},{4,5},{5,4},{6,7},{7,6},{8,9},{9,8},{10,11... | collective-permute-start | bytes 393224 | tf_op jit(solution)/shard_map/ppermute | solution.py:420
  50.3 5.1 %collective-permute-start.15 = (f32[4,16,512]{2,1,0:T(8,128)S(1)}, f32[4,16,512]{2,1,0:T(8,128)S(1)}, u32[]{:S(2)}, u32[]{:S(2)}) collective-permute-start(f32[4,16,512]{2,1,0:T(8,128)S(1)} %get-tuple-element.90), channel_id=1, source_target_pairs={{0,2},{1,3},{2,0},{3,1},{4,6},{5,7},{6,4},{7,5},{8,10},{9,11},{10,... | collective-permute-start | bytes 393224 | tf_op jit(solution)/shard_map/ppermute | solution.py:420
  55.4 2.7 %collective-permute-start.17 = (f32[4,16,512]{2,1,0:T(8,128)S(1)}, f32[4,16,512]{2,1,0:T(8,128)S(1)}, u32[]{:S(2)}, u32[]{:S(2)}) collective-permute-start(f32[4,16,512]{2,1,0:T(8,128)S(1)} %get-tuple-element.98), channel_id=1, source_target_pairs={{0,1},{1,0},{2,3},{3,2},{4,5},{5,4},{6,7},{7,6},{8,9},{9,8},{10,11... | collective-permute-start | bytes 393224 | tf_op jit(solution)/shard_map/ppermute | solution.py:420

commit v5 on v4

--- a/solution.py
+++ b/solution.py
@@ -18,7 +18,7 @@
 PARAM_COLS = TAP_COLS + LANES
 GROUP = 4
 GROUPS = 4
-UNROLL = 64
+UNROLL = 128
 HBM = pl.BlockSpec(memory_space=pltpu.HBM)
 F32 = jnp.float32
 VMEM = pl.BlockSpec(memory_space=pltpu.VMEM)
@@ -548,14 +548,14 @@
     def run_inner(g):
         packed[g] = inner_part(g, base, query, tail, params[g], coef[g], drive[g], scale)
 
-    run_ends(1)
+    run_ends(0)
+    run_ends(1, ends[0])
     from_1 = swap(ends[1], CORE)
-    run_ends(0)
-    params[2], ends[0], from_1 = after(params[2], ends[0], from_1)
+    params[2], ends[1] = after(params[2], ends[1])
     params.append(swap(params[2], CORE))
     run_ends(2)
     low_z, chip_z = join(CORE, span, 0, base, ends[0], from_1, params[0])
-    params[3], ends[2], chip_z = after(params[3], ends[2], chip_z)
+    params[3], ends[2] = after(params[3], ends[2])
     run_ends(3)
     from_3 = swap(ends[3], CORE)
     low_y, chip_y = join(CORE, span, 0, base, ends[2], from_3, params[2])

time: 60.7 us -> 60.4 us (level)
  Pallas kernels: 32.1 us -> 31.4 us
  transfers between devices with their start and end apart: 18 -> 18, of which waited for: 8 -> 7; matrix products, arithmetic and copies ran while one was open for 0% -> 0% of each run, Pallas kernels for 44% -> 43%
where the time goes in v5:
time: 60.4 us; the launch traced here: 60.3 us
  Pallas kernels  31.4 us (52%)
  starting transfers between devices  20.8 us (34%)
  waiting for transfers between devices  7.86 us (13%)
    ppermute x17, starting transfers between devices, swap(): return lax.ppermute(value, 'ctx', [(i, i ^ bit) for i in range(size)])  16.2 us
    pallas_call x4, Pallas kernels, inner_part(): pl.pallas_call(functools.partial(pieces, functools.partial(inner_kernel,...  10.8 us
    ppermute x17, waiting for transfers between devices, swap(): return lax.ppermute(value, 'ctx', [(i, i ^ bit) for i in range(size)])  7.86 us
    pallas_call x4, Pallas kernels, finish_part(): pl.pallas_call(functools.partial(finish_body, scale, group), out_shape=ou...  7.49 us
    pallas_call x4, Pallas kernels, ends_part(): pl.pallas_call(functools.partial(pieces, functools.partial(ends_kernel, s...  6.74 us
    pallas_call x2, Pallas kernels, stage_part(): pl.pallas_call(functools.partial(stage_body, branches, stride), out_shape...  4.97 us
    ppermute x1, starting transfers between devices, per_device(): tail = lax.ppermute(tail_rows, 'ctx', onward)  4.54 us
  transfers between devices with their start and end apart: 18, of which 7 were waited for; matrix products, arithmetic and copies ran while one was open for 0% of the time, Pallas kernels for 43%

profile of v5, /device:TPU:1, one launch (start us, length us, event | category | flops | bytes accessed | tf_op | source)
XLA Modules:
  0.0 60.3 jit_solution(642543276549034469)
XLA Ops:
  1.1 4.5 %collective-permute-start = (bf16[3,2,8192]{2,1,0:T(2,128)(2,1)S(1)}, bf16[3,2,8192]{2,1,0:T(2,128)(2,1)S(1)}, u32[]{:S(2)}, u32[]{:S(2)}) collective-permute-start(bf16[3,2,8192]{2,1,0:T(2,128)(2,1)S(1)} %get-tuple-element.54), channel_id=1, source_target_pairs={{0,1},{1,2},{2,3},{3,4},{4,5},{5,6},{6,7},{7,8},{8,9},{9,10},{10,1... | collective-permute-start | bytes 294920 | tf_op jit(solution)/shard_map/ppermute | solution.py:541
  5.7 3.4 %collective-permute-start.1 = (f32[8,2688]{1,0:T(8,128)S(1)}, f32[8,2688]{1,0:T(8,128)S(1)}, u32[]{:S(2)}, u32[]{:S(2)}) collective-permute-start(f32[8,2688]{1,0:T(8,128)S(1)} %get-tuple-element.52.refs_0_.refs_3_), channel_id=1, source_target_pairs={{0,12},{1,13},{2,14},{3,15},{4,8},{5,9},{6,10},{7,11},{8,4},{9,5},... | collective-permute-start | bytes 258056 | tf_op jit(solution)/shard_map/ppermute | solution.py:420
  9.4 3.2 %stage_part.2 = (f32[16,1024,128]{2,1,0:T(8,128)S(1)}, f32[8,128]{1,0:T(8,128)S(1)}) custom-call(bf16[3,128,8192]{2,1,0:T(8,128)(2,1)} %bitcast.5, f32[8,2688]{1,0:T(8,128)S(1)} %get-tuple-element.52.refs_0_.refs_3_, s32[1]{0:T(128)} %bitcast.refs_1_.refs_0_.me), custom_call_target="tpu_custom_call" | custom-call | flops 20971520 | bytes 5242880 | tf_op jit(solution)/shard_map/stage_part/pallas_call | solution.py:287
  12.6 1.8 %stage_part.3 = (f32[16,512,128]{2,1,0:T(8,128)S(1)}, f32[8,128]{1,0:T(8,128)S(1)}) custom-call(bf16[3,128,8192]{2,1,0:T(8,128)(2,1)} %bitcast.6, f32[8,128]{1,0:T(8,128)S(1)} %get-tuple-element.55.refs_0_), custom_call_target="tpu_custom_call" | custom-call | flops 10485760 | bytes 2621440 | tf_op jit(solution)/shard_map/stage_part/pallas_call | solution.py:287
  14.4 1.5 %collective-permute-done.2.refs_1_ = f32[8,2688]{1,0:T(8,128)S(1)} collective-permute-done((f32[8,2688]{1,0:T(8,128)S(1)}, f32[8,2688]{1,0:T(8,128)S(1)}, u32[]{:S(2)}, u32[]{:S(2)}) %collective-permute-start.2) | collective-permute-done | bytes 86048 | tf_op jit(solution)/shard_map/ppermute | solution.py:420
  16.1 1.2 %collective-permute-start.6 = (f32[4,8,1664]{2,1,0:T(8,128)S(1)}, f32[4,8,1664]{2,1,0:T(8,128)S(1)}, u32[]{:S(2)}, u32[]{:S(2)}) collective-permute-start(f32[4,8,1664]{2,1,0:T(8,128)S(1)} %get-tuple-element.57.refs_3_.params), channel_id=1, source_target_pairs={{0,2},{1,3},{2,0},{3,1},{4,6},{5,7},{6,4},{7,5},{8,10},{9,11},{10,... | collective-permute-start | bytes 638984 | tf_op jit(solution)/shard_map/ppermute | solution.py:420
  17.3 1.7 %ends_part.4 = (f32[4,16,512]{2,1,0:T(8,128)S(1)}, f32[4,1024,128]{2,1,0:T(8,128)S(1)}) custom-call(s32[1]{0:T(128)} %bitcast.refs_1_.refs_0_.me, f32[16,1024,128]{2,1,0:T(8,128)S(1)} %get-tuple-element.53.refs_1_.refs_2_, bf16[3,2,8192]{2,1,0:T(2,128)(2,1)S(1)} %collective-permute-done.refs_5_.refs_2_.refs_3_, ...), custom_call_target="tpu_custom_call" | custom-call | flops 12582912 | bytes 3145728 | tf_op jit(solution)/shard_map/ends_part/pallas_call | solution.py:353
  19.0 1.7 %ends_part.5 = (f32[4,16,512]{2,1,0:T(8,128)S(1)}, f32[4,1024,128]{2,1,0:T(8,128)S(1)}) custom-call(s32[1]{0:T(128)} %bitcast.refs_1_.refs_0_.me, f32[4,16,512]{2,1,0:T(8,128)S(1)} %get-tuple-element.58.refs_1_.mine, f32[16,1024,128]{2,1,0:T(8,128)S(1)} %get-tuple-element.53.refs_1_.refs_2_, ...), custom_call_target="tpu_custom_call" | custom-call | flops 12582912 | bytes 3145728 | tf_op jit(solution)/shard_map/ends_part/pallas_call | solution.py:353
  20.7 1.8 %collective-permute-done.6.refs_3_.params = f32[4,8,1664]{2,1,0:T(8,128)S(1)} collective-permute-done((f32[4,8,1664]{2,1,0:T(8,128)S(1)}, f32[4,8,1664]{2,1,0:T(8,128)S(1)}, u32[]{:S(2)}, u32[]{:S(2)}) %collective-permute-start.6) | collective-permute-done | bytes 213024 | tf_op jit(solution)/shard_map/ppermute | solution.py:420
  22.5 1.3 %collective-permute-start.7 = (f32[4,8,1664]{2,1,0:T(8,128)S(1)}, f32[4,8,1664]{2,1,0:T(8,128)S(1)}, u32[]{:S(2)}, u32[]{:S(2)}) collective-permute-start(f32[4,8,1664]{2,1,0:T(8,128)S(1)} %collective-permute-done.6.refs_3_.params), channel_id=1, source_target_pairs={{0,1},{1,0},{2,3},{3,2},{4,5},{5,4},{6,7},{7,6},{8,9},{9,8},{10,11... | collective-permute-start | bytes 638984 | tf_op jit(solution)/shard_map/ppermute | solution.py:420
  23.8 1.7 %ends_part.6 = (f32[4,16,512]{2,1,0:T(8,128)S(1)}, f32[4,1024,128]{2,1,0:T(8,128)S(1)}) custom-call(s32[1]{0:T(128)} %bitcast.refs_1_.refs_0_.me, f32[16,1024,128]{2,1,0:T(8,128)S(1)} %get-tuple-element.53.refs_1_.refs_2_, bf16[3,2,8192]{2,1,0:T(2,128)(2,1)S(1)} %collective-permute-done.refs_5_.refs_2_.refs_3_, ...), custom_call_target="tpu_custom_call" | custom-call | flops 12582912 | bytes 3145728 | tf_op jit(solution)/shard_map/ends_part/pallas_call | solution.py:353
  25.5 1.7 %ends_part.7 = (f32[4,16,512]{2,1,0:T(8,128)S(1)}, f32[4,1024,128]{2,1,0:T(8,128)S(1)}) custom-call(s32[1]{0:T(128)} %bitcast.refs_1_.refs_0_.me, f32[16,1024,128]{2,1,0:T(8,128)S(1)} %get-tuple-element.53.refs_1_.refs_2_, bf16[3,2,8192]{2,1,0:T(2,128)(2,1)S(1)} %collective-permute-done.refs_5_.refs_2_.refs_3_, ...), custom_call_target="tpu_custom_call" | custom-call | flops 12582912 | bytes 3145728 | tf_op jit(solution)/shard_map/ends_part/pallas_call | solution.py:353
  28.6 1.3 %collective-permute-start.9 = (f32[4,16,512]{2,1,0:T(8,128)S(1)}, f32[4,16,512]{2,1,0:T(8,128)S(1)}, u32[]{:S(2)}, u32[]{:S(2)}) collective-permute-start(f32[4,16,512]{2,1,0:T(8,128)S(1)} %get-tuple-element.66), channel_id=1, source_target_pairs={{0,2},{1,3},{2,0},{3,1},{4,6},{5,7},{6,4},{7,5},{8,10},{9,11},{10,... | collective-permute-start | bytes 393224 | tf_op jit(solution)/shard_map/ppermute | solution.py:420
  30.6 2.7 %inner_part.4.packed = f32[4,1024,128]{2,1,0:T(8,128)S(1)} custom-call(s32[1]{0:T(128)} %bitcast.refs_1_.refs_0_.me, f32[16,512,128]{2,1,0:T(8,128)S(1)} %get-tuple-element.67.refs_1_, bf16[3,2,8192]{2,1,0:T(2,128)(2,1)S(1)} %collective-permute-done.refs_5_.refs_2_.refs_3_, f32[4,8,1664]{2,1,0:T(8,128)S(1)} %get-tuple-element.57.refs_3_.params, ...), custom_call_target="tpu_custom_call" | custom-call | flops 18874368 | bytes 4718592 | tf_op jit(solution)/shard_map/inner_part/pallas_call | solution.py:373
  34.2 2.7 %inner_part.5.packed = f32[4,1024,128]{2,1,0:T(8,128)S(1)} custom-call(s32[1]{0:T(128)} %bitcast.refs_1_.refs_0_.me, f32[16,512,128]{2,1,0:T(8,128)S(1)} %get-tuple-element.67.refs_1_, bf16[3,2,8192]{2,1,0:T(2,128)(2,1)S(1)} %collective-permute-done.refs_5_.refs_2_.refs_3_, f32[4,8,1664]{2,1,0:T(8,128)S(1)} %collective-permute-done.4.refs_4_.refs_3_.params, ...), custom_call_target="tpu_custom_call" | custom-call | flops 18874368 | bytes 4718592 | tf_op jit(solution)/shard_map/inner_part/pallas_call | solution.py:373
  37.6 2.7 %collective-permute-start.14 = (f32[4,16,512]{2,1,0:T(8,128)S(1)}, f32[4,16,512]{2,1,0:T(8,128)S(1)}, u32[]{:S(2)}, u32[]{:S(2)}) collective-permute-start(f32[4,16,512]{2,1,0:T(8,128)S(1)} %collective-permute-done.12.refs_4_.coef), channel_id=1, source_target_pairs={{0,1},{1,0},{2,3},{3,2},{4,5},{5,4},{6,7},{7,6},{8,9},{9,8},{10,11... | collective-permute-start | bytes 393224 | tf_op jit(solution)/shard_map/ppermute | solution.py:420
  41.4 2.7 %inner_part.6.packed = f32[4,1024,128]{2,1,0:T(8,128)S(1)} custom-call(s32[1]{0:T(128)} %bitcast.refs_1_.refs_0_.me, f32[16,512,128]{2,1,0:T(8,128)S(1)} %get-tuple-element.67.refs_1_, bf16[3,2,8192]{2,1,0:T(2,128)(2,1)S(1)} %collective-permute-done.refs_5_.refs_2_.refs_3_, f32[4,8,1664]{2,1,0:T(8,128)S(1)} %collective-permute-done.6.refs_3_.params, ...), custom_call_target="tpu_custom_call" | custom-call | flops 18874368 | bytes 4718592 | tf_op jit(solution)/shard_map/inner_part/pallas_call | solution.py:373
  44.1 2.7 %inner_part.7.packed = f32[4,1024,128]{2,1,0:T(8,128)S(1)} custom-call(s32[1]{0:T(128)} %bitcast.refs_1_.refs_0_.me, f32[16,512,128]{2,1,0:T(8,128)S(1)} %get-tuple-element.67.refs_1_, bf16[3,2,8192]{2,1,0:T(2,128)(2,1)S(1)} %collective-permute-done.refs_5_.refs_2_.refs_3_, f32[4,8,1664]{2,1,0:T(8,128)S(1)} %collective-permute-done.7.refs_3_.params, ...), custom_call_target="tpu_custom_call" | custom-call | flops 18874368 | bytes 4718592 | tf_op jit(solution)/shard_map/inner_part/pallas_call | solution.py:373
  46.8 2.4 %collective-permute-done.13.far = f32[4,16,512]{2,1,0:T(8,128)S(1)} collective-permute-done((f32[4,16,512]{2,1,0:T(8,128)S(1)}, f32[4,16,512]{2,1,0:T(8,128)S(1)}, u32[]{:S(2)}, u32[]{:S(2)}) %collective-permute-start.13) | collective-permute-done | bytes 131104 | tf_op jit(solution)/shard_map/ppermute | solution.py:420
  50.1 1.2 %collective-permute-start.15 = (f32[4,16,512]{2,1,0:T(8,128)S(1)}, f32[4,16,512]{2,1,0:T(8,128)S(1)}, u32[]{:S(2)}, u32[]{:S(2)}) collective-permute-start(f32[4,16,512]{2,1,0:T(8,128)S(1)} %get-tuple-element.84), channel_id=1, source_target_pairs={{0,2},{1,3},{2,0},{3,1},{4,6},{5,7},{6,4},{7,5},{8,10},{9,11},{10,... | collective-permute-start | bytes 393224 | tf_op jit(solution)/shard_map/ppermute | solution.py:420
  51.4 1.7 %finish_part.4.refs_0_ = bf16[4,128,512]{2,1,0:T(8,128)(2,1)S(1)} custom-call(s32[1]{0:T(128)} %bitcast.refs_1_.refs_0_.me, f32[4,1024,128]{2,1,0:T(8,128)S(1)} %inner_part.4.packed, f32[4,8,1664]{2,1,0:T(8,128)S(1)} %get-tuple-element.57.refs_3_.params, f32[4,16,512]{2,1,0:T(8,128)S(1)} %get-tuple-element.68.refs_4_.coef, ...), custom_call_target="tpu_custom_call" | custom-call | flops 10485760 | bytes 2621440 | tf_op jit(solution)/shard_map/finish_part/pallas_call | solution.py:404
  53.1 1.7 %finish_part.5 = (bf16[128,8192]{1,0:T(8,128)(2,1)}, bf16[4,128,512]{2,1,0:T(8,128)(2,1)S(1)}) custom-call(s32[1]{0:T(128)} %bitcast.refs_1_.refs_0_.me, f32[4,1024,128]{2,1,0:T(8,128)S(1)} %inner_part.5.packed, f32[4,8,1664]{2,1,0:T(8,128)S(1)} %collective-permute-done.4.refs_4_.refs_3_.params, f32[4,16,512]{2,1,0:T(8,128)S(1)} %collective-permute-done.11.refs_4_.coef, ...), custom_call_target="tpu_custom_call" | custom-call | flops 10485760 | bytes 2621440 | tf_op jit(solution)/shard_map/finish_part/pallas_call | solution.py:404
  56.2 1.7 %finish_part.6 = (bf16[128,8192]{1,0:T(8,128)(2,1)}, bf16[4,128,512]{2,1,0:T(8,128)(2,1)S(1)}) custom-call(s32[1]{0:T(128)} %bitcast.refs_1_.refs_0_.me, f32[4,1024,128]{2,1,0:T(8,128)S(1)} %inner_part.6.packed, f32[4,8,1664]{2,1,0:T(8,128)S(1)} %collective-permute-done.6.refs_3_.params, ...), custom_call_target="tpu_custom_call", output_to_operand_aliasing={{0}: (6, {})} | custom-call | flops 10485760 | bytes 2621440 | tf_op jit(solution)/shard_map/finish_part/pallas_call | solution.py:404
  57.9 2.4 %finish_part.7 = bf16[128,8192]{1,0:T(8,128)(2,1)} custom-call(s32[1]{0:T(128)} %bitcast.refs_1_.refs_0_.me, f32[4,1024,128]{2,1,0:T(8,128)S(1)} %inner_part.7.packed, f32[4,8,1664]{2,1,0:T(8,128)S(1)} %collective-permute-done.7.refs_3_.params, f32[4,16,512]{2,1,0:T(8,128)S(1)} %collective-permute-done.14.refs_4_.coef, ...), custom_call_target="tpu_custom_call", output_to_operand_aliasing={{}: (6, {})} | custom-call | flops 10485760 | bytes 2621440 | tf_op jit(solution)/shard_map/finish_part/pallas_call | solution.py:404
  (34 shorter events, 8.8 us)
Async XLA Ops:
  1.1 14.8 %collective-permute-start = (bf16[3,2,8192]{2,1,0:T(2,128)(2,1)S(1)}, bf16[3,2,8192]{2,1,0:T(2,128)(2,1)S(1)}, u32[]{:S(2)}, u32[]{:S(2)}) collective-permute-start(bf16[3,2,8192]{2,1,0:T(2,128)(2,1)S(1)} %get-tuple-element.54), channel_id=1, source_target_pairs={{0,1},{1,2},{2,3},{3,4},{4,5},{5,6},{6,7},{7,8},{8,9},{9,10},{10,1... | collective-permute-start | bytes 294920 | tf_op jit(solution)/shard_map/ppermute | solution.py:541
  5.7 8.7 %collective-permute-start.1 = (f32[8,2688]{1,0:T(8,128)S(1)}, f32[8,2688]{1,0:T(8,128)S(1)}, u32[]{:S(2)}, u32[]{:S(2)}) collective-permute-start(f32[8,2688]{1,0:T(8,128)S(1)} %get-tuple-element.52.refs_0_.refs_3_), channel_id=1, source_target_pairs={{0,12},{1,13},{2,14},{3,15},{4,8},{5,9},{6,10},{7,11},{8,4},{9,5},... | collective-permute-start | bytes 258056 | tf_op jit(solution)/shard_map/ppermute | solution.py:420
  9.1 6.8 %collective-permute-start.2 = (f32[8,2688]{1,0:T(8,128)S(1)}, f32[8,2688]{1,0:T(8,128)S(1)}, u32[]{:S(2)}, u32[]{:S(2)}) collective-permute-start(f32[8,2688]{1,0:T(8,128)S(1)} %get-tuple-element.52.refs_0_.refs_3_), channel_id=1, source_target_pairs={{0,8},{1,9},{2,10},{3,11},{4,12},{5,13},{6,14},{7,15},{8,0},{9,1},... | collective-permute-start | bytes 258056 | tf_op jit(solution)/shard_map/ppermute | solution.py:420
  9.1 6.8 %collective-permute-start.3 = (f32[8,2688]{1,0:T(8,128)S(1)}, f32[8,2688]{1,0:T(8,128)S(1)}, u32[]{:S(2)}, u32[]{:S(2)}) collective-permute-start(f32[8,2688]{1,0:T(8,128)S(1)} %get-tuple-element.52.refs_0_.refs_3_), channel_id=1, source_target_pairs={{0,4},{1,5},{2,6},{3,7},{4,0},{5,1},{6,2},{7,3},{8,12},{9,13},{10,... | collective-permute-start | bytes 258056 | tf_op jit(solution)/shard_map/ppermute | solution.py:420
  15.9 3.1 %collective-permute-start.4 = (f32[4,8,1664]{2,1,0:T(8,128)S(1)}, f32[4,8,1664]{2,1,0:T(8,128)S(1)}, u32[]{:S(2)}, u32[]{:S(2)}) collective-permute-start(f32[4,8,1664]{2,1,0:T(8,128)S(1)} %get-tuple-element.57.refs_3_.params), channel_id=1, source_target_pairs={{0,1},{1,0},{2,3},{3,2},{4,5},{5,4},{6,7},{7,6},{8,9},{9,8},{10,11... | collective-permute-start | bytes 638984 | tf_op jit(solution)/shard_map/ppermute | solution.py:420
  16.1 6.4 %collective-permute-start.6 = (f32[4,8,1664]{2,1,0:T(8,128)S(1)}, f32[4,8,1664]{2,1,0:T(8,128)S(1)}, u32[]{:S(2)}, u32[]{:S(2)}) collective-permute-start(f32[4,8,1664]{2,1,0:T(8,128)S(1)} %get-tuple-element.57.refs_3_.params), channel_id=1, source_target_pairs={{0,2},{1,3},{2,0},{3,1},{4,6},{5,7},{6,4},{7,5},{8,10},{9,11},{10,... | collective-permute-start | bytes 638984 | tf_op jit(solution)/shard_map/ppermute | solution.py:420
  22.5 2.9 %collective-permute-start.7 = (f32[4,8,1664]{2,1,0:T(8,128)S(1)}, f32[4,8,1664]{2,1,0:T(8,128)S(1)}, u32[]{:S(2)}, u32[]{:S(2)}) collective-permute-start(f32[4,8,1664]{2,1,0:T(8,128)S(1)} %collective-permute-done.6.refs_3_.params), channel_id=1, source_target_pairs={{0,1},{1,0},{2,3},{3,2},{4,5},{5,4},{6,7},{7,6},{8,9},{9,8},{10,11... | collective-permute-start | bytes 638984 | tf_op jit(solution)/shard_map/ppermute | solution.py:420
  27.2 1.4 %collective-permute-start.8 = (f32[4,16,512]{2,1,0:T(8,128)S(1)}, f32[4,16,512]{2,1,0:T(8,128)S(1)}, u32[]{:S(2)}, u32[]{:S(2)}) collective-permute-start(f32[4,16,512]{2,1,0:T(8,128)S(1)} %get-tuple-element.65), channel_id=1, source_target_pairs={{0,1},{1,0},{2,3},{3,2},{4,5},{5,4},{6,7},{7,6},{8,9},{9,8},{10,11... | collective-permute-start | bytes 393224 | tf_op jit(solution)/shard_map/ppermute | solution.py:420
  27.2 6.0 %collective-permute-start.5 = (f32[4,16,512]{2,1,0:T(8,128)S(1)}, f32[4,16,512]{2,1,0:T(8,128)S(1)}, u32[]{:S(2)}, u32[]{:S(2)}) collective-permute-start(f32[4,16,512]{2,1,0:T(8,128)S(1)} %get-tuple-element.59), channel_id=1, source_target_pairs={{0,1},{1,0},{2,3},{3,2},{4,5},{5,4},{6,7},{7,6},{8,9},{9,8},{10,11... | collective-permute-start | bytes 393224 | tf_op jit(solution)/shard_map/ppermute | solution.py:420
  28.6 5.0 %collective-permute-start.9 = (f32[4,16,512]{2,1,0:T(8,128)S(1)}, f32[4,16,512]{2,1,0:T(8,128)S(1)}, u32[]{:S(2)}, u32[]{:S(2)}) collective-permute-start(f32[4,16,512]{2,1,0:T(8,128)S(1)} %get-tuple-element.66), channel_id=1, source_target_pairs={{0,2},{1,3},{2,0},{3,1},{4,6},{5,7},{6,4},{7,5},{8,10},{9,11},{10,... | collective-permute-start | bytes 393224 | tf_op jit(solution)/shard_map/ppermute | solution.py:420
  29.9 4.3 %collective-permute-start.11 = (f32[4,16,512]{2,1,0:T(8,128)S(1)}, f32[4,16,512]{2,1,0:T(8,128)S(1)}, u32[]{:S(2)}, u32[]{:S(2)}) collective-permute-start(f32[4,16,512]{2,1,0:T(8,128)S(1)} %get-tuple-element.68.refs_4_.coef), channel_id=1, source_target_pairs={{0,1},{1,0},{2,3},{3,2},{4,5},{5,4},{6,7},{7,6},{8,9},{9,8},{10,11... | collective-permute-start | bytes 393224 | tf_op jit(solution)/shard_map/ppermute | solution.py:420
  30.4 6.6 %collective-permute-start.12 = (f32[4,16,512]{2,1,0:T(8,128)S(1)}, f32[4,16,512]{2,1,0:T(8,128)S(1)}, u32[]{:S(2)}, u32[]{:S(2)}) collective-permute-start(f32[4,16,512]{2,1,0:T(8,128)S(1)} %get-tuple-element.68.refs_4_.coef), channel_id=1, source_target_pairs={{0,2},{1,3},{2,0},{3,1},{4,6},{5,7},{6,4},{7,5},{8,10},{9,11},{10,... | collective-permute-start | bytes 393224 | tf_op jit(solution)/shard_map/ppermute | solution.py:420
  33.7 3.9 %collective-permute-start.10 = (f32[4,16,512]{2,1,0:T(8,128)S(1)}, f32[4,16,512]{2,1,0:T(8,128)S(1)}, u32[]{:S(2)}, u32[]{:S(2)}) collective-permute-start(f32[4,16,512]{2,1,0:T(8,128)S(1)} %get-tuple-element.72.mine), channel_id=1, source_target_pairs={{0,4},{1,5},{2,6},{3,7},{4,0},{5,1},{6,2},{7,3},{8,12},{9,13},{10,... | collective-permute-start | bytes 393224 | tf_op jit(solution)/shard_map/ppermute | solution.py:420
  37.6 6.6 %collective-permute-start.14 = (f32[4,16,512]{2,1,0:T(8,128)S(1)}, f32[4,16,512]{2,1,0:T(8,128)S(1)}, u32[]{:S(2)}, u32[]{:S(2)}) collective-permute-start(f32[4,16,512]{2,1,0:T(8,128)S(1)} %collective-permute-done.12.refs_4_.coef), channel_id=1, source_target_pairs={{0,1},{1,0},{2,3},{3,2},{4,5},{5,4},{6,7},{7,6},{8,9},{9,8},{10,11... | collective-permute-start | bytes 393224 | tf_op jit(solution)/shard_map/ppermute | solution.py:420
  40.3 9.0 %collective-permute-start.13 = (f32[4,16,512]{2,1,0:T(8,128)S(1)}, f32[4,16,512]{2,1,0:T(8,128)S(1)}, u32[]{:S(2)}, u32[]{:S(2)}) collective-permute-start(f32[4,16,512]{2,1,0:T(8,128)S(1)} %get-tuple-element.75), channel_id=1, source_target_pairs={{0,8},{1,9},{2,10},{3,11},{4,12},{5,13},{6,14},{7,15},{8,0},{9,1},... | collective-permute-start | bytes 393224 | tf_op jit(solution)/shard_map/ppermute | solution.py:420
  49.4 3.7 %collective-permute-start.16 = (f32[4,16,512]{2,1,0:T(8,128)S(1)}, f32[4,16,512]{2,1,0:T(8,128)S(1)}, u32[]{:S(2)}, u32[]{:S(2)}) collective-permute-start(f32[4,16,512]{2,1,0:T(8,128)S(1)} %get-tuple-element.86), channel_id=1, source_target_pairs={{0,1},{1,0},{2,3},{3,2},{4,5},{5,4},{6,7},{7,6},{8,9},{9,8},{10,11... | collective-permute-start | bytes 393224 | tf_op jit(solution)/shard_map/ppermute | solution.py:420
  50.1 5.1 %collective-permute-start.15 = (f32[4,16,512]{2,1,0:T(8,128)S(1)}, f32[4,16,512]{2,1,0:T(8,128)S(1)}, u32[]{:S(2)}, u32[]{:S(2)}) collective-permute-start(f32[4,16,512]{2,1,0:T(8,128)S(1)} %get-tuple-element.84), channel_id=1, source_target_pairs={{0,2},{1,3},{2,0},{3,1},{4,6},{5,7},{6,4},{7,5},{8,10},{9,11},{10,... | collective-permute-start | bytes 393224 | tf_op jit(solution)/shard_map/ppermute | solution.py:420
  55.2 2.6 %collective-permute-start.17 = (f32[4,16,512]{2,1,0:T(8,128)S(1)}, f32[4,16,512]{2,1,0:T(8,128)S(1)}, u32[]{:S(2)}, u32[]{:S(2)}) collective-permute-start(f32[4,16,512]{2,1,0:T(8,128)S(1)} %get-tuple-element.92), channel_id=1, source_target_pairs={{0,1},{1,0},{2,3},{3,2},{4,5},{5,4},{6,7},{7,6},{8,9},{9,8},{10,11... | collective-permute-start | bytes 393224 | tf_op jit(solution)/shard_map/ppermute | solution.py:420

commit v6 on v3

--- a/solution.py
+++ b/solution.py
@@ -18,7 +18,7 @@
 PARAM_COLS = TAP_COLS + LANES
 GROUP = 4
 GROUPS = 4
-UNROLL = 32
+UNROLL = 128
 HBM = pl.BlockSpec(memory_space=pltpu.HBM)
 F32 = jnp.float32
 VMEM = pl.BlockSpec(memory_space=pltpu.VMEM)
@@ -119,11 +119,11 @@
 
 def stack_kernel(*refs):
     params, coef = refs[-2:]
-    for i in range(GROUP):
-        params[i] = refs[i][:, 0:PARAM_COLS]
+    for ref, i in zip(refs, NEAR + (0,)):
+        params[i] = ref[:, 0:PARAM_COLS]
         for h in range(2):
             at = PARAM_COLS + h * WIDTH
-            coef[i, h * HALF : (h + 1) * HALF, :] = refs[i][:, at : at + WIDTH]
+            coef[i, h * HALF : (h + 1) * HALF, :] = ref[:, at : at + WIDTH]
 
 
 def ends_kernel(
@@ -422,6 +422,7 @@
 
 
 CORE, Y, Z = 1, 2, 4
+NEAR = (3, 2, 1)
 
 
 def swap(value, bit):
@@ -540,13 +541,13 @@
 
     base = me.reshape(1)
     wide = pack_part(short_filter, residues.T, rates.T, scale)
-    near = [swap(wide, Z * k) for k in range(1, GROUP)]
+    near = [swap(wide, Z * k) for k in NEAR]
     keyed, staged = stage_part((1, 2), feats, wide, base)
     tail_rows = tail_part(feats, staged)
-    params, coef = ([x] for x in stack_part([wide] + near, tail_rows))
+    query, staged = stage_part((0,), feats, tail_rows)
+    params, coef = ([x] for x in stack_part(near + [wide], tail_rows, staged))
     params.append(swap(params[0], CORE))
     params.append(swap(params[0], Y))
-    query, staged = stage_part((0,), feats, params[0])
     tail = lax.ppermute(tail_rows, "ctx", onward)
     coef.append(swap(coef[0], CORE))
     ends, drive, packed = [None] * GROUPS, [None] * GROUPS, [None] * GROUPS
@@ -557,14 +558,14 @@
     def run_inner(g):
         packed[g] = inner_part(g, base, query, tail, params[g], coef[g], drive[g], scale)
 
-    run_ends(1, staged)
+    run_ends(0)
+    run_ends(1, ends[0])
     from_1 = swap(ends[1], CORE)
-    run_ends(0)
-    params[2], ends[0], from_1 = after(params[2], ends[0], from_1)
+    params[2], ends[1] = after(params[2], ends[1])
     params.append(swap(params[2], CORE))
     run_ends(2)
     low_z, chip_z = join(CORE, span, 0, base, ends[0], from_1, params[0])
-    params[3], ends[2], chip_z = after(params[3], ends[2], chip_z)
+    params[3], ends[2] = after(params[3], ends[2])
     run_ends(3)
     from_3 = swap(ends[3], CORE)
     low_y, chip_y = join(CORE, span, 0, base, ends[2], from_3, params[2])

time: 62.1 us -> 62 us (level)
  waiting for transfers between devices: 4.93 us -> 8.32 us
  starting transfers between devices: 23.2 us -> 21 us
  Pallas kernels: 33.4 us -> 32.2 us
    ppermute x1, waiting for transfers between devices: 0.01 us -> 3.77 us  [per_device(): tail = lax.ppermute(tail_rows, 'ctx', onward)]
    ppermute x17, starting transfers between devices: 20.2 us -> 18.7 us  [swap(): return lax.ppermute(value, 'ctx', [(i, i ^ bit) for i in range(size)])]
    ppermute x1, starting transfers between devices: 3.05 us -> 2.35 us  [per_device(): tail = lax.ppermute(tail_rows, 'ctx', onward)]
  transfers between devices with their start and end apart: 18 -> 18, of which waited for: 6 -> 7; matrix products, arithmetic and copies ran while one was open for 0% -> 0% of each run, Pallas kernels for 45% -> 44%
where the time goes in v6:
time: 62 us; the launch traced here: 61.8 us
  Pallas kernels  32.2 us (52%)
  starting transfers between devices  21 us (34%)
  waiting for transfers between devices  8.32 us (13%)
    ppermute x17, starting transfers between devices, swap(): return lax.ppermute(value, 'ctx', [(i, i ^ bit) for i in range(size)])  18.7 us
    pallas_call x4, Pallas kernels, inner_part(): pl.pallas_call(functools.partial(pieces, functools.partial(inner_kernel,...  10.8 us
    pallas_call x4, Pallas kernels, finish_part(): pl.pallas_call(functools.partial(finish_body, scale, group), out_shape=ou...  7.49 us
    pallas_call x4, Pallas kernels, ends_part(): pl.pallas_call(functools.partial(pieces, functools.partial(ends_kernel, s...  6.74 us
    pallas_call x2, Pallas kernels, stage_part(): pl.pallas_call(functools.partial(stage_body, branches, stride), out_shape...  4.97 us
    ppermute x17, waiting for transfers between devices, swap(): return lax.ppermute(value, 'ctx', [(i, i ^ bit) for i in range(size)])  4.56 us
    ppermute x1, waiting for transfers between devices, per_device(): tail = lax.ppermute(tail_rows, 'ctx', onward)  3.77 us
    ppermute x1, starting transfers between devices, per_device(): tail = lax.ppermute(tail_rows, 'ctx', onward)  2.35 us
  transfers between devices with their start and end apart: 18, of which 7 were waited for; matrix products, arithmetic and copies ran while one was open for 0% of the time, Pallas kernels for 44%

profile of v6, /device:TPU:1, one launch (start us, length us, event | category | flops | bytes accessed | tf_op | source)
XLA Modules:
  0.0 61.8 jit_solution(3616969286404436925)
XLA Ops:
  0.8 4.2 %collective-permute-start.1 = (f32[8,2688]{1,0:T(8,128)S(1)}, f32[8,2688]{1,0:T(8,128)S(1)}, u32[]{:S(2)}, u32[]{:S(2)}) collective-permute-start(f32[8,2688]{1,0:T(8,128)S(1)} %pack_part.1.refs_0_.refs_3_), channel_id=1, source_target_pairs={{0,12},{1,13},{2,14},{3,15},{4,8},{5,9},{6,10},{7,11},{8,4},{9,5},... | collective-permute-start | bytes 258056 | tf_op jit(solution)/shard_map/ppermute | solution.py:430
  5.4 3.2 %stage_part.2 = (f32[16,1024,128]{2,1,0:T(8,128)S(1)}, f32[8,128]{1,0:T(8,128)S(1)}) custom-call(bf16[3,128,8192]{2,1,0:T(8,128)(2,1)} %bitcast.4, f32[8,2688]{1,0:T(8,128)S(1)} %pack_part.1.refs_0_.refs_3_, s32[1]{0:T(128)} %bitcast.refs_1_.refs_0_.me), custom_call_target="tpu_custom_call" | custom-call | flops 20971520 | bytes 5242880 | tf_op jit(solution)/shard_map/stage_part/pallas_call | solution.py:286
  9.7 1.8 %stage_part.3 = (f32[16,512,128]{2,1,0:T(8,128)S(1)}, f32[8,128]{1,0:T(8,128)S(1)}) custom-call(bf16[3,128,8192]{2,1,0:T(8,128)(2,1)} %bitcast.6, bf16[3,2,8192]{2,1,0:T(2,128)(2,1)S(1)} %tail_part.1.refs_0_.refs_4_), custom_call_target="tpu_custom_call" | custom-call | flops 10485760 | bytes 2621440 | tf_op jit(solution)/shard_map/stage_part/pallas_call | solution.py:286
  12.0 1.4 %collective-permute-start.4 = (f32[4,8,1664]{2,1,0:T(8,128)S(1)}, f32[4,8,1664]{2,1,0:T(8,128)S(1)}, u32[]{:S(2)}, u32[]{:S(2)}) collective-permute-start(f32[4,8,1664]{2,1,0:T(8,128)S(1)} %get-tuple-element.53.refs_3_.params), channel_id=1, source_target_pairs={{0,1},{1,0},{2,3},{3,2},{4,5},{5,4},{6,7},{7,6},{8,9},{9,8},{10,11... | collective-permute-start | bytes 638984 | tf_op jit(solution)/shard_map/ppermute | solution.py:430
  13.3 1.3 %collective-permute-start.6 = (f32[4,8,1664]{2,1,0:T(8,128)S(1)}, f32[4,8,1664]{2,1,0:T(8,128)S(1)}, u32[]{:S(2)}, u32[]{:S(2)}) collective-permute-start(f32[4,8,1664]{2,1,0:T(8,128)S(1)} %get-tuple-element.53.refs_3_.params), channel_id=1, source_target_pairs={{0,2},{1,3},{2,0},{3,1},{4,6},{5,7},{6,4},{7,5},{8,10},{9,11},{10,... | collective-permute-start | bytes 638984 | tf_op jit(solution)/shard_map/ppermute | solution.py:430
  14.6 2.4 %collective-permute-start = (bf16[3,2,8192]{2,1,0:T(2,128)(2,1)S(1)}, bf16[3,2,8192]{2,1,0:T(2,128)(2,1)S(1)}, u32[]{:S(2)}, u32[]{:S(2)}) collective-permute-start(bf16[3,2,8192]{2,1,0:T(2,128)(2,1)S(1)} %tail_part.1.refs_0_.refs_4_), channel_id=1, source_target_pairs={{0,1},{1,2},{2,3},{3,4},{4,5},{5,6},{6,7},{7,8},{8,9},{9,10},{10,1... | collective-permute-start | bytes 294920 | tf_op jit(solution)/shard_map/ppermute | solution.py:551
  16.9 3.8 %collective-permute-done.refs_2_.refs_3_ = bf16[3,2,8192]{2,1,0:T(2,128)(2,1)S(1)} collective-permute-done((bf16[3,2,8192]{2,1,0:T(2,128)(2,1)S(1)}, bf16[3,2,8192]{2,1,0:T(2,128)(2,1)S(1)}, u32[]{:S(2)}, u32[]{:S(2)}) %collective-permute-start) | collective-permute-done | bytes 98336 | tf_op jit(solution)/shard_map/ppermute | solution.py:551
  20.7 1.7 %ends_part.4 = (f32[4,16,512]{2,1,0:T(8,128)S(1)}, f32[4,1024,128]{2,1,0:T(8,128)S(1)}) custom-call(s32[1]{0:T(128)} %bitcast.refs_1_.refs_0_.me, f32[16,1024,128]{2,1,0:T(8,128)S(1)} %get-tuple-element.50.refs_1_.refs_2_, bf16[3,2,8192]{2,1,0:T(2,128)(2,1)S(1)} %collective-permute-done.refs_2_.refs_3_, f32[4,8,1664]{2,1,0:T(8,128)S(1)} %get-tuple-element.53.refs_3_.params), custom_call_target="tpu_custom_call" | custom-call | flops 12582912 | bytes 3145728 | tf_op jit(solution)/shard_map/ends_part/pallas_call | solution.py:363
  22.4 1.7 %ends_part.5 = (f32[4,16,512]{2,1,0:T(8,128)S(1)}, f32[4,1024,128]{2,1,0:T(8,128)S(1)}) custom-call(s32[1]{0:T(128)} %bitcast.refs_1_.refs_0_.me, f32[4,16,512]{2,1,0:T(8,128)S(1)} %get-tuple-element.54.refs_1_.mine, f32[16,1024,128]{2,1,0:T(8,128)S(1)} %get-tuple-element.50.refs_1_.refs_2_, bf16[3,2,8192]{2,1,0:T(2,128)(2,1)S(1)} %collective-permute-done.refs_2_.refs_3_, ...), custom_call_target="tpu_custom_call" | custom-call | flops 12582912 | bytes 3145728 | tf_op jit(solution)/shard_map/ends_part/pallas_call | solution.py:363
  24.2 1.7 %ends_part.6 = (f32[4,16,512]{2,1,0:T(8,128)S(1)}, f32[4,1024,128]{2,1,0:T(8,128)S(1)}) custom-call(s32[1]{0:T(128)} %bitcast.refs_1_.refs_0_.me, f32[16,1024,128]{2,1,0:T(8,128)S(1)} %get-tuple-element.50.refs_1_.refs_2_, bf16[3,2,8192]{2,1,0:T(2,128)(2,1)S(1)} %collective-permute-done.refs_2_.refs_3_, f32[4,8,1664]{2,1,0:T(8,128)S(1)} %collective-permute-done.6.refs_3_.params), custom_call_target="tpu_custom_call" | custom-call | flops 12582912 | bytes 3145728 | tf_op jit(solution)/shard_map/ends_part/pallas_call | solution.py:363
  25.9 1.7 %ends_part.7 = (f32[4,16,512]{2,1,0:T(8,128)S(1)}, f32[4,1024,128]{2,1,0:T(8,128)S(1)}) custom-call(s32[1]{0:T(128)} %bitcast.refs_1_.refs_0_.me, f32[16,1024,128]{2,1,0:T(8,128)S(1)} %get-tuple-element.50.refs_1_.refs_2_, bf16[3,2,8192]{2,1,0:T(2,128)(2,1)S(1)} %collective-permute-done.refs_2_.refs_3_, f32[4,8,1664]{2,1,0:T(8,128)S(1)} %collective-permute-done.7.refs_3_.params), custom_call_target="tpu_custom_call" | custom-call | flops 12582912 | bytes 3145728 | tf_op jit(solution)/shard_map/ends_part/pallas_call | solution.py:363
  29.2 2.5 %collective-permute-start.9 = (f32[4,16,512]{2,1,0:T(8,128)S(1)}, f32[4,16,512]{2,1,0:T(8,128)S(1)}, u32[]{:S(2)}, u32[]{:S(2)}) collective-permute-start(f32[4,16,512]{2,1,0:T(8,128)S(1)} %get-tuple-element.62), channel_id=1, source_target_pairs={{0,2},{1,3},{2,0},{3,1},{4,6},{5,7},{6,4},{7,5},{8,10},{9,11},{10,... | collective-permute-start | bytes 393224 | tf_op jit(solution)/shard_map/ppermute | solution.py:430
  32.1 2.7 %inner_part.4.packed = f32[4,1024,128]{2,1,0:T(8,128)S(1)} custom-call(s32[1]{0:T(128)} %bitcast.refs_1_.refs_0_.me, f32[16,512,128]{2,1,0:T(8,128)S(1)} %get-tuple-element.63.refs_1_, bf16[3,2,8192]{2,1,0:T(2,128)(2,1)S(1)} %collective-permute-done.refs_2_.refs_3_, f32[4,8,1664]{2,1,0:T(8,128)S(1)} %get-tuple-element.53.refs_3_.params, ...), custom_call_target="tpu_custom_call" | custom-call | flops 18874368 | bytes 4718592 | tf_op jit(solution)/shard_map/inner_part/pallas_call | solution.py:383
  35.9 2.7 %inner_part.5.packed = f32[4,1024,128]{2,1,0:T(8,128)S(1)} custom-call(s32[1]{0:T(128)} %bitcast.refs_1_.refs_0_.me, f32[16,512,128]{2,1,0:T(8,128)S(1)} %get-tuple-element.63.refs_1_, bf16[3,2,8192]{2,1,0:T(2,128)(2,1)S(1)} %collective-permute-done.refs_2_.refs_3_, f32[4,8,1664]{2,1,0:T(8,128)S(1)} %collective-permute-done.4.refs_4_.refs_3_.params, ...), custom_call_target="tpu_custom_call" | custom-call | flops 18874368 | bytes 4718592 | tf_op jit(solution)/shard_map/inner_part/pallas_call | solution.py:383
  39.3 2.2 %collective-permute-start.14 = (f32[4,16,512]{2,1,0:T(8,128)S(1)}, f32[4,16,512]{2,1,0:T(8,128)S(1)}, u32[]{:S(2)}, u32[]{:S(2)}) collective-permute-start(f32[4,16,512]{2,1,0:T(8,128)S(1)} %collective-permute-done.12.refs_4_.coef), channel_id=1, source_target_pairs={{0,1},{1,0},{2,3},{3,2},{4,5},{5,4},{6,7},{7,6},{8,9},{9,8},{10,11... | collective-permute-start | bytes 393224 | tf_op jit(solution)/shard_map/ppermute | solution.py:430
  41.6 1.8 %collective-permute-start.13 = (f32[4,16,512]{2,1,0:T(8,128)S(1)}, f32[4,16,512]{2,1,0:T(8,128)S(1)}, u32[]{:S(2)}, u32[]{:S(2)}) collective-permute-start(f32[4,16,512]{2,1,0:T(8,128)S(1)} %get-tuple-element.71), channel_id=1, source_target_pairs={{0,8},{1,9},{2,10},{3,11},{4,12},{5,13},{6,14},{7,15},{8,0},{9,1},... | collective-permute-start | bytes 393224 | tf_op jit(solution)/shard_map/ppermute | solution.py:430
  43.4 2.7 %inner_part.6.packed = f32[4,1024,128]{2,1,0:T(8,128)S(1)} custom-call(s32[1]{0:T(128)} %bitcast.refs_1_.refs_0_.me, f32[16,512,128]{2,1,0:T(8,128)S(1)} %get-tuple-element.63.refs_1_, bf16[3,2,8192]{2,1,0:T(2,128)(2,1)S(1)} %collective-permute-done.refs_2_.refs_3_, f32[4,8,1664]{2,1,0:T(8,128)S(1)} %collective-permute-done.6.refs_3_.params, ...), custom_call_target="tpu_custom_call" | custom-call | flops 18874368 | bytes 4718592 | tf_op jit(solution)/shard_map/inner_part/pallas_call | solution.py:383
  46.1 2.7 %inner_part.7.packed = f32[4,1024,128]{2,1,0:T(8,128)S(1)} custom-call(s32[1]{0:T(128)} %bitcast.refs_1_.refs_0_.me, f32[16,512,128]{2,1,0:T(8,128)S(1)} %get-tuple-element.63.refs_1_, bf16[3,2,8192]{2,1,0:T(2,128)(2,1)S(1)} %collective-permute-done.refs_2_.refs_3_, f32[4,8,1664]{2,1,0:T(8,128)S(1)} %collective-permute-done.7.refs_3_.params, ...), custom_call_target="tpu_custom_call" | custom-call | flops 18874368 | bytes 4718592 | tf_op jit(solution)/shard_map/inner_part/pallas_call | solution.py:383
  48.8 1.6 %collective-permute-done.13.far = f32[4,16,512]{2,1,0:T(8,128)S(1)} collective-permute-done((f32[4,16,512]{2,1,0:T(8,128)S(1)}, f32[4,16,512]{2,1,0:T(8,128)S(1)}, u32[]{:S(2)}, u32[]{:S(2)}) %collective-permute-start.13) | collective-permute-done | bytes 131104 | tf_op jit(solution)/shard_map/ppermute | solution.py:430
  51.4 1.7 %collective-permute-start.15 = (f32[4,16,512]{2,1,0:T(8,128)S(1)}, f32[4,16,512]{2,1,0:T(8,128)S(1)}, u32[]{:S(2)}, u32[]{:S(2)}) collective-permute-start(f32[4,16,512]{2,1,0:T(8,128)S(1)} %get-tuple-element.80), channel_id=1, source_target_pairs={{0,2},{1,3},{2,0},{3,1},{4,6},{5,7},{6,4},{7,5},{8,10},{9,11},{10,... | collective-permute-start | bytes 393224 | tf_op jit(solution)/shard_map/ppermute | solution.py:430
  53.1 1.7 %finish_part.4.refs_0_ = bf16[4,128,512]{2,1,0:T(8,128)(2,1)S(1)} custom-call(s32[1]{0:T(128)} %bitcast.refs_1_.refs_0_.me, f32[4,1024,128]{2,1,0:T(8,128)S(1)} %inner_part.4.packed, f32[4,8,1664]{2,1,0:T(8,128)S(1)} %get-tuple-element.53.refs_3_.params, f32[4,16,512]{2,1,0:T(8,128)S(1)} %get-tuple-element.64.refs_4_.coef, ...), custom_call_target="tpu_custom_call" | custom-call | flops 10485760 | bytes 2621440 | tf_op jit(solution)/shard_map/finish_part/pallas_call | solution.py:414
  54.8 1.7 %finish_part.5 = (bf16[128,8192]{1,0:T(8,128)(2,1)}, bf16[4,128,512]{2,1,0:T(8,128)(2,1)S(1)}) custom-call(s32[1]{0:T(128)} %bitcast.refs_1_.refs_0_.me, f32[4,1024,128]{2,1,0:T(8,128)S(1)} %inner_part.5.packed, f32[4,8,1664]{2,1,0:T(8,128)S(1)} %collective-permute-done.4.refs_4_.refs_3_.params, f32[4,16,512]{2,1,0:T(8,128)S(1)} %collective-permute-done.11.refs_4_.coef, ...), custom_call_target="tpu_custom_call" | custom-call | flops 10485760 | bytes 2621440 | tf_op jit(solution)/shard_map/finish_part/pallas_call | solution.py:414
  57.7 1.7 %finish_part.6 = (bf16[128,8192]{1,0:T(8,128)(2,1)}, bf16[4,128,512]{2,1,0:T(8,128)(2,1)S(1)}) custom-call(s32[1]{0:T(128)} %bitcast.refs_1_.refs_0_.me, f32[4,1024,128]{2,1,0:T(8,128)S(1)} %inner_part.6.packed, f32[4,8,1664]{2,1,0:T(8,128)S(1)} %collective-permute-done.6.refs_3_.params, ...), custom_call_target="tpu_custom_call", output_to_operand_aliasing={{0}: (6, {})} | custom-call | flops 10485760 | bytes 2621440 | tf_op jit(solution)/shard_map/finish_part/pallas_call | solution.py:414
  59.4 2.4 %finish_part.7 = bf16[128,8192]{1,0:T(8,128)(2,1)} custom-call(s32[1]{0:T(128)} %bitcast.refs_1_.refs_0_.me, f32[4,1024,128]{2,1,0:T(8,128)S(1)} %inner_part.7.packed, f32[4,8,1664]{2,1,0:T(8,128)S(1)} %collective-permute-done.7.refs_3_.params, f32[4,16,512]{2,1,0:T(8,128)S(1)} %collective-permute-done.14.refs_4_.coef, ...), custom_call_target="tpu_custom_call", output_to_operand_aliasing={{}: (6, {})} | custom-call | flops 10485760 | bytes 2621440 | tf_op jit(solution)/shard_map/finish_part/pallas_call | solution.py:414
  (35 shorter events, 8.7 us)
Async XLA Ops:
  0.8 10.6 %collective-permute-start.1 = (f32[8,2688]{1,0:T(8,128)S(1)}, f32[8,2688]{1,0:T(8,128)S(1)}, u32[]{:S(2)}, u32[]{:S(2)}) collective-permute-start(f32[8,2688]{1,0:T(8,128)S(1)} %pack_part.1.refs_0_.refs_3_), channel_id=1, source_target_pairs={{0,12},{1,13},{2,14},{3,15},{4,8},{5,9},{6,10},{7,11},{8,4},{9,5},... | collective-permute-start | bytes 258056 | tf_op jit(solution)/shard_map/ppermute | solution.py:430
  5.1 6.9 %collective-permute-start.2 = (f32[8,2688]{1,0:T(8,128)S(1)}, f32[8,2688]{1,0:T(8,128)S(1)}, u32[]{:S(2)}, u32[]{:S(2)}) collective-permute-start(f32[8,2688]{1,0:T(8,128)S(1)} %pack_part.1.refs_0_.refs_3_), channel_id=1, source_target_pairs={{0,8},{1,9},{2,10},{3,11},{4,12},{5,13},{6,14},{7,15},{8,0},{9,1},... | collective-permute-start | bytes 258056 | tf_op jit(solution)/shard_map/ppermute | solution.py:430
  5.1 6.9 %collective-permute-start.3 = (f32[8,2688]{1,0:T(8,128)S(1)}, f32[8,2688]{1,0:T(8,128)S(1)}, u32[]{:S(2)}, u32[]{:S(2)}) collective-permute-start(f32[8,2688]{1,0:T(8,128)S(1)} %pack_part.1.refs_0_.refs_3_), channel_id=1, source_target_pairs={{0,4},{1,5},{2,6},{3,7},{4,0},{5,1},{6,2},{7,3},{8,12},{9,13},{10,... | collective-permute-start | bytes 258056 | tf_op jit(solution)/shard_map/ppermute | solution.py:430
  12.0 10.4 %collective-permute-start.4 = (f32[4,8,1664]{2,1,0:T(8,128)S(1)}, f32[4,8,1664]{2,1,0:T(8,128)S(1)}, u32[]{:S(2)}, u32[]{:S(2)}) collective-permute-start(f32[4,8,1664]{2,1,0:T(8,128)S(1)} %get-tuple-element.53.refs_3_.params), channel_id=1, source_target_pairs={{0,1},{1,0},{2,3},{3,2},{4,5},{5,4},{6,7},{7,6},{8,9},{9,8},{10,11... | collective-permute-start | bytes 638984 | tf_op jit(solution)/shard_map/ppermute | solution.py:430
  13.3 10.8 %collective-permute-start.6 = (f32[4,8,1664]{2,1,0:T(8,128)S(1)}, f32[4,8,1664]{2,1,0:T(8,128)S(1)}, u32[]{:S(2)}, u32[]{:S(2)}) collective-permute-start(f32[4,8,1664]{2,1,0:T(8,128)S(1)} %get-tuple-element.53.refs_3_.params), channel_id=1, source_target_pairs={{0,2},{1,3},{2,0},{3,1},{4,6},{5,7},{6,4},{7,5},{8,10},{9,11},{10,... | collective-permute-start | bytes 638984 | tf_op jit(solution)/shard_map/ppermute | solution.py:430
  14.6 6.1 %collective-permute-start = (bf16[3,2,8192]{2,1,0:T(2,128)(2,1)S(1)}, bf16[3,2,8192]{2,1,0:T(2,128)(2,1)S(1)}, u32[]{:S(2)}, u32[]{:S(2)}) collective-permute-start(bf16[3,2,8192]{2,1,0:T(2,128)(2,1)S(1)} %tail_part.1.refs_0_.refs_4_), channel_id=1, source_target_pairs={{0,1},{1,2},{2,3},{3,4},{4,5},{5,6},{6,7},{7,8},{8,9},{9,10},{10,1... | collective-permute-start | bytes 294920 | tf_op jit(solution)/shard_map/ppermute | solution.py:551
  24.1 1.8 %collective-permute-start.7 = (f32[4,8,1664]{2,1,0:T(8,128)S(1)}, f32[4,8,1664]{2,1,0:T(8,128)S(1)}, u32[]{:S(2)}, u32[]{:S(2)}) collective-permute-start(f32[4,8,1664]{2,1,0:T(8,128)S(1)} %collective-permute-done.6.refs_3_.params), channel_id=1, source_target_pairs={{0,1},{1,0},{2,3},{3,2},{4,5},{5,4},{6,7},{7,6},{8,9},{9,8},{10,11... | collective-permute-start | bytes 638984 | tf_op jit(solution)/shard_map/ppermute | solution.py:430
  27.6 1.5 %collective-permute-start.8 = (f32[4,16,512]{2,1,0:T(8,128)S(1)}, f32[4,16,512]{2,1,0:T(8,128)S(1)}, u32[]{:S(2)}, u32[]{:S(2)}) collective-permute-start(f32[4,16,512]{2,1,0:T(8,128)S(1)} %get-tuple-element.61), channel_id=1, source_target_pairs={{0,1},{1,0},{2,3},{3,2},{4,5},{5,4},{6,7},{7,6},{8,9},{9,8},{10,11... | collective-permute-start | bytes 393224 | tf_op jit(solution)/shard_map/ppermute | solution.py:430
  28.1 6.7 %collective-permute-start.5 = (f32[4,16,512]{2,1,0:T(8,128)S(1)}, f32[4,16,512]{2,1,0:T(8,128)S(1)}, u32[]{:S(2)}, u32[]{:S(2)}) collective-permute-start(f32[4,16,512]{2,1,0:T(8,128)S(1)} %get-tuple-element.55), channel_id=1, source_target_pairs={{0,1},{1,0},{2,3},{3,2},{4,5},{5,4},{6,7},{7,6},{8,9},{9,8},{10,11... | collective-permute-start | bytes 393224 | tf_op jit(solution)/shard_map/ppermute | solution.py:430
  29.2 6.2 %collective-permute-start.9 = (f32[4,16,512]{2,1,0:T(8,128)S(1)}, f32[4,16,512]{2,1,0:T(8,128)S(1)}, u32[]{:S(2)}, u32[]{:S(2)}) collective-permute-start(f32[4,16,512]{2,1,0:T(8,128)S(1)} %get-tuple-element.62), channel_id=1, source_target_pairs={{0,2},{1,3},{2,0},{3,1},{4,6},{5,7},{6,4},{7,5},{8,10},{9,11},{10,... | collective-permute-start | bytes 393224 | tf_op jit(solution)/shard_map/ppermute | solution.py:430
  31.7 4.2 %collective-permute-start.11 = (f32[4,16,512]{2,1,0:T(8,128)S(1)}, f32[4,16,512]{2,1,0:T(8,128)S(1)}, u32[]{:S(2)}, u32[]{:S(2)}) collective-permute-start(f32[4,16,512]{2,1,0:T(8,128)S(1)} %get-tuple-element.64.refs_4_.coef), channel_id=1, source_target_pairs={{0,1},{1,0},{2,3},{3,2},{4,5},{5,4},{6,7},{7,6},{8,9},{9,8},{10,11... | collective-permute-start | bytes 393224 | tf_op jit(solution)/shard_map/ppermute | solution.py:430
  32.1 6.5 %collective-permute-start.12 = (f32[4,16,512]{2,1,0:T(8,128)S(1)}, f32[4,16,512]{2,1,0:T(8,128)S(1)}, u32[]{:S(2)}, u32[]{:S(2)}) collective-permute-start(f32[4,16,512]{2,1,0:T(8,128)S(1)} %get-tuple-element.64.refs_4_.coef), channel_id=1, source_target_pairs={{0,2},{1,3},{2,0},{3,1},{4,6},{5,7},{6,4},{7,5},{8,10},{9,11},{10,... | collective-permute-start | bytes 393224 | tf_op jit(solution)/shard_map/ppermute | solution.py:430
  35.4 3.9 %collective-permute-start.10 = (f32[4,16,512]{2,1,0:T(8,128)S(1)}, f32[4,16,512]{2,1,0:T(8,128)S(1)}, u32[]{:S(2)}, u32[]{:S(2)}) collective-permute-start(f32[4,16,512]{2,1,0:T(8,128)S(1)} %get-tuple-element.68.mine), channel_id=1, source_target_pairs={{0,4},{1,5},{2,6},{3,7},{4,0},{5,1},{6,2},{7,3},{8,12},{9,13},{10,... | collective-permute-start | bytes 393224 | tf_op jit(solution)/shard_map/ppermute | solution.py:430
  39.3 6.8 %collective-permute-start.14 = (f32[4,16,512]{2,1,0:T(8,128)S(1)}, f32[4,16,512]{2,1,0:T(8,128)S(1)}, u32[]{:S(2)}, u32[]{:S(2)}) collective-permute-start(f32[4,16,512]{2,1,0:T(8,128)S(1)} %collective-permute-done.12.refs_4_.coef), channel_id=1, source_target_pairs={{0,1},{1,0},{2,3},{3,2},{4,5},{5,4},{6,7},{7,6},{8,9},{9,8},{10,11... | collective-permute-start | bytes 393224 | tf_op jit(solution)/shard_map/ppermute | solution.py:430
  41.6 8.9 %collective-permute-start.13 = (f32[4,16,512]{2,1,0:T(8,128)S(1)}, f32[4,16,512]{2,1,0:T(8,128)S(1)}, u32[]{:S(2)}, u32[]{:S(2)}) collective-permute-start(f32[4,16,512]{2,1,0:T(8,128)S(1)} %get-tuple-element.71), channel_id=1, source_target_pairs={{0,8},{1,9},{2,10},{3,11},{4,12},{5,13},{6,14},{7,15},{8,0},{9,1},... | collective-permute-start | bytes 393224 | tf_op jit(solution)/shard_map/ppermute | solution.py:430
  50.6 4.3 %collective-permute-start.16 = (f32[4,16,512]{2,1,0:T(8,128)S(1)}, f32[4,16,512]{2,1,0:T(8,128)S(1)}, u32[]{:S(2)}, u32[]{:S(2)}) collective-permute-start(f32[4,16,512]{2,1,0:T(8,128)S(1)} %get-tuple-element.82), channel_id=1, source_target_pairs={{0,1},{1,0},{2,3},{3,2},{4,5},{5,4},{6,7},{7,6},{8,9},{9,8},{10,11... | collective-permute-start | bytes 393224 | tf_op jit(solution)/shard_map/ppermute | solution.py:430
  51.4 5.5 %collective-permute-start.15 = (f32[4,16,512]{2,1,0:T(8,128)S(1)}, f32[4,16,512]{2,1,0:T(8,128)S(1)}, u32[]{:S(2)}, u32[]{:S(2)}) collective-permute-start(f32[4,16,512]{2,1,0:T(8,128)S(1)} %get-tuple-element.80), channel_id=1, source_target_pairs={{0,2},{1,3},{2,0},{3,1},{4,6},{5,7},{6,4},{7,5},{8,10},{9,11},{10,... | collective-permute-start | bytes 393224 | tf_op jit(solution)/shard_map/ppermute | solution.py:430
  56.9 2.5 %collective-permute-start.17 = (f32[4,16,512]{2,1,0:T(8,128)S(1)}, f32[4,16,512]{2,1,0:T(8,128)S(1)}, u32[]{:S(2)}, u32[]{:S(2)}) collective-permute-start(f32[4,16,512]{2,1,0:T(8,128)S(1)} %get-tuple-element.88), channel_id=1, source_target_pairs={{0,1},{1,0},{2,3},{3,2},{4,5},{5,4},{6,7},{7,6},{8,9},{9,8},{10,11... | collective-permute-start | bytes 393224 | tf_op jit(solution)/shard_map/ppermute | solution.py:430
